TPU v7x, 32 devices: a whole 2x2x4 slice. The times are simulated.
32 devices in a mesh: orb: 8 (over y, x, core), aux: 4 (over z).
Axes of the slice: x: 2, y: 2, z: 4, core: 2. Of those that a mesh axis runs over, the one named last changes fastest.
Arguments:
- blocks: bfloat16 [32, 256, 6144], P('orb', None, 'aux'), may hold values from -0.65625 to 0.65625
- excitation: float32 [32, 256], replicated, may hold values from 0.5 to 8
- partner: int32 [8, 8], replicated, may hold values from 0 to 3
- neighbours: int32 [8, 8], replicated, may hold values from 0 to 1, as said below
Outputs:
- gradient: bfloat16 [32, 256, 6144], P('orb', None, 'aux')
Inputs may be any that keep to these rules, and one draw needn't show every extreme that they name: neighbours is symmetric: neighbours[d][s] equals neighbours[s][d].
All inputs are finite; a program needn't handle non-finite values.
Results may differ from a plain program's by a relative error of at most 0.0048.
Values may be sent and summed in bfloat16 or wider, within the bound.
No kernel may reach another device: no remote copies, remote signals or barrier semaphores. Data moves between devices by JAX's collectives and lax.ppermute only.
A program may use at most 192 MiB of HBM per device.

v0:
```python
import jax
import jax.numpy as jnp
from jax import lax
from jax.sharding import PartitionSpec as P


def amplitudes(kernel, own_rows, far_rows, weights, excitation):
    denominator = excitation[own_rows][:, :, None] + excitation[far_rows][:, None, :]
    return (-weights[:, None, None] * kernel / denominator).astype(jnp.bfloat16)


def reduce_amplitudes(kernel_part, own_rows, far_rows, weights, excitation):
    kernel = lax.psum(kernel_part, "aux")
    return amplitudes(kernel, own_rows, far_rows, weights, excitation)


def on_device(blocks, excitation, partner, neighbours):
    peers = lax.axis_size("orb")
    anchor = lax.axis_index("orb")
    local_count = blocks.shape[0]
    width = blocks.shape[1]
    aux_width = blocks.shape[2]
    wanted = partner[:, anchor]
    own_rows = anchor * local_count + wanted
    far_rows = jnp.arange(peers, dtype=jnp.int32) * local_count + partner[anchor, :]
    weights = neighbours[anchor, :].astype(jnp.float32)
    outgoing = jnp.take(blocks, wanted, axis=0)
    received = lax.all_to_all(outgoing, "orb", split_axis=0, concat_axis=0, tiled=True)
    kernel_part = jnp.einsum("sap,sbp->sab", outgoing, received, preferred_element_type=jnp.float32)
    amplitude = reduce_amplitudes(kernel_part, own_rows, far_rows, weights, excitation)
    onehot = (wanted[:, None] == jnp.arange(local_count, dtype=jnp.int32)[None, :]).astype(
        jnp.float32
    )
    grouped = 8
    groups = peers // grouped
    amplitude_groups = amplitude.reshape(groups, grouped, width, width)
    received_groups = received.reshape(groups, grouped, width, aux_width)
    onehot_groups = onehot.reshape(groups, grouped, local_count)

    def accumulate(running, pieces):
        product = jnp.einsum(
            "sab,sbp->sap", pieces[0], pieces[1], preferred_element_type=jnp.float32
        )
        added = jnp.einsum("si,sap->iap", pieces[2], product, precision=lax.Precision.HIGHEST)
        return (running + added, None)

    initial = jnp.zeros((local_count, width, aux_width), jnp.float32)
    running, unused = lax.scan(
        accumulate, initial, (amplitude_groups, received_groups, onehot_groups)
    )
    return running.astype(jnp.bfloat16)


def solution(mesh):
    placed = (P("orb", None, "aux"), P(), P(), P())
    return jax.shard_map(
        on_device, mesh=mesh, in_specs=placed, out_specs=P("orb", None, "aux"), check_vma=False
    )
```

profile of v0, /device:TPU:1, one launch (start us, length us, event | category | flops | bytes accessed | tf_op | source)
XLA Modules:
  0.0 208.8 jit_solution(16170676096387874628)
XLA Ops:
  6.5 0.0 copy-start
  6.5 0.0 all-reduce.2.cloned.1.call-start
  6.5 0.9 constant_dynamic-slice_fusion.2
  7.4 0.1 copy.8
  7.5 0.7 fusion.17
  8.2 0.2 copy-done
  8.4 3.6 %gather_fusion = bf16[8,256,1536]{2,1,0:T(8,128)(2,1)} fusion(bf16[4,256,1536]{2,1,0:T(8,128)(2,1)S(1)} %copy-done, s32[1024]{0:T(1024)S(1)} %pad_clamp_fusion.2), kind=kCustom, calls=%fused_computation | custom fusion | bytes 12582944 | tf_op jit(solution)/shard_map/jit(_take)/gather | solution.py:27
  12.0 3.5 %broadcast_select_fusion = bf16[8,256,1536]{2,1,0:T(8,128)(2,1)S(1)} fusion(bf16[8,256,1536]{2,1,0:T(8,128)(2,1)} %gather_fusion, pred[8]{0:T(512)(128)(4,1)S(1)} %and_bitcast_fusion), kind=kLoop, calls=%fused_computation.5 | loop fusion | flops 3145728 | bytes 12582920 | tf_op jit(solution)/shard_map/jit(_take)/select_n | solution.py:27
  15.5 75.2 %all_to_all.5 = bf16[8,256,1536]{2,1,0:T(8,128)(2,1)S(1)} all-to-all(bf16[8,256,1536]{2,1,0:T(8,128)(2,1)S(1)} %broadcast_select_fusion), channel_id=1, replica_groups=mesh['orb'=8,'aux'=4] {'orb'}, dimensions={0} | all-to-all | bytes 12582912 | tf_op jit(solution)/shard_map/all_to_all | solution.py:28
  90.7 0.0 copy-start.1
  90.7 2.6 %copy-done.1 = bf16[8,256,1536]{2,1,0:T(8,128)(2,1)} copy-done((bf16[8,256,1536]{2,1,0:T(8,128)(2,1)}, bf16[8,256,1536]{2,1,0:T(8,128)(2,1)S(1)}, u32[]{:S(2)}) %copy-start.1) | copy-done | bytes 6291480
  93.4 0.0 copy-start.2
  93.4 3.1 %fusion.20 = f32[8,256,256]{2,1,0:T(8,128)} fusion(bf16[8,256,1536]{2,1,0:T(8,128)(2,1)S(1)} %broadcast_select_fusion, bf16[8,256,1536]{2,1,0:T(8,128)(2,1)S(1)} %all_to_all.5), kind=kOutput, calls=%fused_computation.33 | convolution fusion | flops 1610612736 | bytes 14680064 | tf_op jit(solution)/shard_map/sap,sbp->sab/dot_general | solution.py:29
  96.5 0.0 all-reduce.2.cloned.1.call-update
  96.6 0.0 copy-done.2
  96.6 0.6 gather_fusion.1
  97.2 0.6 gather_fusion.2
  97.7 0.7 fusion.14
  98.4 84.8 %all-reduce.2.cloned.1.call-done = f32[8,256,256]{2,1,0:T(8,128)} async-done(((f32[8,256,256]{2,1,0:T(8,128)}), f32[8,256,256]{2,1,0:T(8,128)}) %all-reduce.2.cloned.1.call-update) | async-done | bytes 2097168 | tf_op jit(solution)/shard_map/psum | solution.py:13
  183.2 5.3 %fusion.5 = f32[8,256,1536]{2,1,0:T(8,128)S(1)} fusion(bf16[8,256,1536]{2,1,0:T(8,128)(2,1)} %copy-done.1, f32[8,256,256]{2,1,0:T(8,128)} %all-reduce.2.cloned.1.call-done, f32[8,256]{1,0:T(8,128)S(1)} %gather_fusion.2, f32[8,256]{1,0:T(8,128)S(1)} %gather_fusion.1, f32[8]{0:T(128)S(1)} %fusion.14), kind=kOutput, calls=%fused_computation.8 | convolution fusion | flops 1612709888 | bytes 20987936 | tf_op jit(solution)/shard_map/while/body/eval_jaxpr/sab,sbp->sap/dot_general | solution.py:41
  188.5 11.2 %fusion.2 = bf16[4,256,1536]{2,0,1:T(4,128)(2,1)S(1)} fusion(f32[8,256,1536]{2,1,0:T(8,128)S(1)} %fusion.5, s32[8]{0:T(128)S(1)} %bitcast.25), kind=kOutput, calls=%fused_computation.6 | convolution fusion | flops 152567840 | bytes 15728672 | tf_op jit(solution)/shard_map/while/body/eval_jaxpr/si,sap->iap/dot_general | solution.py:44
  199.7 2.2 %copy.6 = bf16[4,256,1536]{2,1,0:T(8,128)(2,1)} copy(bf16[4,256,1536]{2,0,1:T(4,128)(2,1)S(1)} %fusion.2) | data formatting | bytes 6291456 | tf_op jit(solution)/shard_map/convert_element_type | solution.py:51
  (4 shorter events, 0.0 us)
Async XLA Ops:
  6.5 1.9 copy-start
  6.5 176.7 %all-reduce.2.cloned.1.call-start = ((), (), s32[]{:S(2)}) async-start(), calls=%async_computation.1 | async-start | bytes 4194304 | tf_op jit(solution)/shard_map/psum | solution.py:13
  90.7 2.7 %copy-start.1 = (bf16[8,256,1536]{2,1,0:T(8,128)(2,1)}, bf16[8,256,1536]{2,1,0:T(8,128)(2,1)S(1)}, u32[]{:S(2)}) copy-start(bf16[8,256,1536]{2,1,0:T(8,128)(2,1)S(1)} %all_to_all.5) | copy-start | bytes 18874372
  93.4 3.2 %copy-start.2 = (f32[32,256]{1,0:T(8,128)S(1)}, f32[32,256]{1,0:T(8,128)}, u32[]{:S(2)}) copy-start(f32[32,256]{1,0:T(8,128)} %param.5) | copy-start | bytes 98308
Sparse Core Ops, SparseCore 0:
  96.7 86.5 all-reduce.1
where the time goes:
time: 210 us; the launch traced here: 209 us
  waiting for transfers between devices  84.8 us (40%)
  blocking collectives  75.2 us (36%)
  matrix products  19.6 us (9%)
  between operations  13.4 us (6%)
  local copies, waits for them, and re-layouts  10.8 us (5%)
  other arithmetic  4.87 us (2%)
    psum x1, waiting for transfers between devices, reduce_amplitudes(): kernel = lax.psum(kernel_part, 'aux')  84.8 us
    all_to_all x1, blocking collectives, on_device(): lax.all_to_all(outgoing, 'orb', split_axis=0, concat_axis=0, tiled=True)  75.2 us
    dot_general x1, matrix products, accumulate(): jnp.einsum('si,sap->iap', pieces[2], product, precision=lax.Precision.HIG...  11.2 us
    dot_general x1, matrix products, accumulate(): jnp.einsum('sab,sbp->sap', pieces[0], pieces[1], preferred_element_type=j...  5.28 us
  transfers between devices with their start and end apart: 1, of which 1 were waited for; matrix products, arithmetic and copies ran while one was open for 1% of the time, Pallas kernels for 0%

commit v1 on v0

v1 whole, which is shorter than its diff:
```python
import jax
import jax.numpy as jnp
from jax import lax
from jax.experimental import pallas as pl
from jax.experimental.pallas import tpu as pltpu
from jax.sharding import PartitionSpec as P

VMEM_BYTES = 56 * 1024 * 1024
WINDOW = 2
SMALL = pl.CostEstimate(flops=1, transcendentals=0, bytes_accessed=1)
LARGE = pl.CostEstimate(flops=1, transcendentals=0, bytes_accessed=60_000_000)
PARAMS = pltpu.CompilerParams(vmem_limit_bytes=VMEM_BYTES)


def forward_steps(peers):
    if peers == 8:
        ring = [0, 1, 3, 2]
        around = []
        for d in range(peers):
            place = ring.index(d >> 1)
            turn = 1 if d & 1 == 0 else 3
            around.append(ring[(place + turn) % 4] * 2 + (d & 1))
        crossed = [d ^ (3 if d & 1 == 0 else 5) for d in range(peers)]
        return [[d ^ (6 if d & 4 == 0 else 7) for d in range(peers)], crossed, around]
    steps = []
    for step in range(2, peers, 2):
        top = 1 << (step.bit_length() - 1)
        steps.append([d ^ (step if d & top == 0 else step + 1) for d in range(peers)])
    return steps


def inverse(step):
    back = [0] * len(step)
    for source, target in enumerate(step):
        back[target] = source
    return back


def after(array, *others):
    return lax.optimization_barrier((array, *others))[0]


def own_of(plan, column):
    return plan[2 + 3 * column]


def pick(blocks, partner, neighbours, rows, plan, columns, cost=SMALL):
    local_count, width, depth = blocks.shape
    count = len(columns)

    def lookup(row, index):
        value = row[0]
        for place, entry in enumerate(row[1:], 1):
            value = jnp.where(index == place, entry, value)
        return value

    def body(*refs):
        if plan is None:
            partners, kept, source = refs[:3]
            outs, made, into = refs[3 : 3 + count], refs[3 + count], refs[-1]
            me = lax.axis_index("orb").astype(jnp.int32)
            made[0] = me
            made[1] = lax.axis_index("aux").astype(jnp.int32)
            others = [lookup(row, me) for row in rows]
            for column in columns:
                made[2 + 3 * column] = partners[others[column], me]
        else:
            made, source = refs[:2]
            outs, into = refs[2 : 2 + count], refs[-1]
        reads = []
        for number, column in enumerate(columns):
            reads.append(
                pltpu.make_async_copy(
                    source.at[own_of(made, column)], outs[number], into.at[number]
                )
            )
        for read in reads:
            read.start()
        if plan is None:
            for column, other in enumerate(others):
                made[2 + 3 * column] = partners[other, me]
                made[3 + 3 * column] = other * local_count + partners[me, other]
                made[4 + 3 * column] = kept[me, other]
        for read in reads:
            read.wait()

    anywhere = pl.BlockSpec(memory_space=pl.ANY)
    out_specs = [pl.BlockSpec(memory_space=pltpu.VMEM)] * count
    out_shape = [jax.ShapeDtypeStruct((width, depth), blocks.dtype)] * count
    if plan is None:
        out_specs.append(pl.BlockSpec(memory_space=pltpu.SMEM))
        out_shape.append(jax.ShapeDtypeStruct((2 + 3 * len(rows),), jnp.int32))
    scalars = (partner, neighbours) if plan is None else (plan,)
    return pl.pallas_call(
        body,
        grid_spec=pltpu.PrefetchScalarGridSpec(
            num_scalar_prefetch=len(scalars),
            in_specs=[anywhere],
            out_specs=out_specs,
            scratch_shapes=[pltpu.SemaphoreType.DMA((count,))],
        ),
        out_shape=out_shape,
        compiler_params=PARAMS,
        cost_estimate=cost,
        name="pick",
    )(*scalars, blocks)


def kernel_parts(own, far, shards, sent):
    width, depth = own[0].shape
    rows = width // shards
    pairs = len(own)
    arrived = [block for block in far if block is not None]

    def body(*refs):
        owns, others = refs[:pairs], list(refs[pairs : pairs + len(arrived)])
        outs, full = refs[pairs + len(arrived) : -1], refs[-1]
        turn = lax.axis_index("aux").astype(jnp.int32)
        for pair in range(pairs):
            other = owns[pair] if far[pair] is None else others.pop(0)
            full[...] = lax.dot_general(
                owns[pair][...],
                other[...],
                (((1,), (1,)), ((), ())),
                preferred_element_type=jnp.float32,
            )
            for j in range(shards):
                start = pl.multiple_of(lax.rem(turn + j, shards) * rows, rows)
                outs[j][pair] = full[pl.ds(start, rows), :].astype(outs[j].dtype)

    return pl.pallas_call(
        body,
        out_shape=[
            jax.ShapeDtypeStruct((pairs, rows, width), sent if j else jnp.float32)
            for j in range(shards)
        ],
        scratch_shapes=[pltpu.VMEM((width, width), jnp.float32)],
        compiler_params=PARAMS,
        cost_estimate=SMALL,
        name="kernel_parts",
    )(*own, *arrived)


def denominators(excitation, plan, column_groups, shards, local_count):
    width = excitation.shape[1]
    rows = width // shards
    count = len(column_groups)

    def body(plan, energies, *refs):
        outs, turned = refs[:count], refs[count]
        turned[...] = energies[...].T
        own_part = turned[pl.ds(pl.multiple_of(plan[1] * rows, rows), rows), :]
        lane = lax.broadcasted_iota(jnp.int32, own_part.shape, 1)
        for out, columns in zip(outs, column_groups):
            for pair, column in enumerate(columns):
                own = plan[0] * local_count + own_of(plan, column)
                left = jnp.sum(jnp.where(lane == own, own_part, 0.0), axis=1, keepdims=True)
                right = energies[pl.ds(plan[3 + 3 * column], 1), :]
                kept = plan[4 + 3 * column].astype(jnp.float32)
                out[pair] = jnp.where(kept > 0, left + right, jnp.inf)

    shapes = [(len(columns), rows, width) for columns in column_groups]
    return pl.pallas_call(
        body,
        grid_spec=pltpu.PrefetchScalarGridSpec(
            num_scalar_prefetch=1,
            grid=(1,),
            in_specs=[pl.BlockSpec(excitation.shape, lambda i, plan: (0, 0))],
            out_specs=[pl.BlockSpec(shape, lambda i, plan: (0, 0, 0)) for shape in shapes],
            scratch_shapes=[pltpu.VMEM(excitation.shape[::-1], jnp.float32)],
        ),
        out_shape=[jax.ShapeDtypeStruct(shape, jnp.float32) for shape in shapes],
        cost_estimate=SMALL,
        name="denominators",
    )(plan, excitation)


def amplitudes(parts, denominator):
    kernel = parts[0]
    for part in parts[1:]:
        kernel = kernel + part.astype(jnp.float32)
    return (-kernel / denominator).astype(jnp.bfloat16)


def assemble(shard_refs, pair, turn, scratch, shards):
    rows = shard_refs[0].shape[1]
    for j in range(shards):
        start = pl.multiple_of(lax.rem(turn + shards - j, shards) * rows, rows)
        scratch[pl.ds(start, rows), :] = shard_refs[j][pair]


def whole_spec(array):
    zeros = (0,) * array.ndim
    return pl.BlockSpec(array.shape, lambda i, plan: zeros)


def accumulate(blocks, before, items, groups, plan, shards, kind):
    local_count, width, depth = blocks.shape
    pairs = len(items)
    step = 512 if depth % 512 == 0 and pairs < 16 else 256
    arrived = [item[0] for item in items if item[0] is not None]
    local = len(arrived) < pairs
    flat = [shard for group in groups for shard in group]

    def body(plan, *refs):
        refs = list(refs)
        own_ref = refs.pop(0) if local else None
        sums = None if before is None else refs.pop(0)
        others = [refs.pop(0) for _ in arrived]
        held = [[refs.pop(0) for _ in group] for group in groups]
        out, total, amps, spare = refs

        @pl.when(pl.program_id(0) == 0)
        def _():
            for number, (block, column, group, pair, transposed) in enumerate(items):
                if transposed:
                    assemble(held[group], pair, plan[1], spare, shards)
                    amps[number] = spare[...].T
                else:
                    assemble(held[group], pair, plan[1], amps.at[number], shards)

        total[...] = jnp.zeros_like(total) if sums is None else sums[...]
        for number, (block, column, group, pair, transposed) in enumerate(items):
            factor = own_ref[0] if block is None else others.pop(0)[...]
            total[own_of(plan, column)] += jnp.dot(
                amps[number], factor, preferred_element_type=jnp.float32
            )
        out[...] = total[...].astype(out.dtype)

    own_spec = pl.BlockSpec((1, width, step), lambda i, plan: (own_of(plan, 0), 0, i))
    far_spec = pl.BlockSpec((width, step), lambda i, plan: (0, i))
    all_spec = pl.BlockSpec((local_count, width, step), lambda i, plan: (0, 0, i))
    return pl.pallas_call(
        body,
        grid_spec=pltpu.PrefetchScalarGridSpec(
            num_scalar_prefetch=1,
            grid=(depth // step,),
            in_specs=[own_spec] * local
            + [all_spec] * (before is not None)
            + [far_spec] * len(arrived)
            + [whole_spec(shard) for shard in flat],
            out_specs=all_spec,
            scratch_shapes=[
                pltpu.VMEM((local_count, width, step), jnp.float32),
                pltpu.VMEM((pairs, width, width), jnp.bfloat16),
                pltpu.VMEM((width, width), jnp.bfloat16),
            ],
        ),
        out_shape=jax.ShapeDtypeStruct(blocks.shape, kind),
        compiler_params=PARAMS,
        cost_estimate=SMALL,
        name="accumulate",
    )(
        plan,
        *([blocks] if local else []),
        *([] if before is None else [before]),
        *arrived,
        *flat,
    )


def on_device(blocks, excitation, partner, neighbours):
    peers = lax.axis_size("orb")
    shards = lax.axis_size("aux")
    local_count = blocks.shape[0]
    forward = forward_steps(peers)
    count = len(forward)
    backward = [inverse(step) for step in forward]
    mate = [d ^ 1 for d in range(peers)]
    from_step = [2 + i for i in range(count)]
    to_step = [2 + count + i for i in range(count)]
    rows = [list(range(peers)), mate] + backward + forward
    def around(array, shift):
        return lax.ppermute(array, "aux", [(i, (i + shift) % shards) for i in range(shards)])

    def send(array, step):
        return lax.ppermute(array, "orb", list(enumerate(step)))

    moves, columns = [mate, forward[0]], [1, to_step[0]]
    for i in range(1, count):
        moves += [forward[i], backward[i]]
        columns += [to_step[i], from_step[i]]
    moves.append(backward[0])
    columns.append(from_step[0])
    picked = pick(blocks, partner, neighbours, rows, None, [*columns[:3], 0])
    *picked, local, plan = picked
    picked += pick(blocks, None, None, rows, plan, columns[3:])
    own = dict(zip([*columns, 0], [*picked, local]))

    size = 1 if count <= 3 else 4
    step_groups = [list(range(i, min(i + size, count))) for i in range(1, count, size)]
    column_groups = [[0, 1], [from_step[0]]]
    for steps in step_groups:
        column_groups.append([c for i in steps for c in (from_step[i], to_step[i])])
    energies = denominators(excitation, plan, column_groups, shards, local_count)

    def reduced(far, columns, sent):
        parts = kernel_parts([own[column] for column in columns], far, shards, sent)
        return parts, [parts[0]] + [around(parts[j], j) for j in range(1, shards)]

    def spread(array):
        return [array] + [around(array, j) for j in range(1, shards)]

    received = [send(picked[number], moves[number]) for number in range(3)]

    def move(*gates):
        number = len(received)
        block = after(picked[number], received[number - WINDOW], *gates)
        received.append(send(block, moves[number]))

    parts, held = reduced([None, received[0]], [0, 1], jnp.float32)
    local = amplitudes(held, energies[0])
    move(*held[1:], *energies, *picked)
    far = after(received[1], local, *energies, *picked)
    parts, held = reduced([far], [from_step[0]], jnp.bfloat16)
    mine = amplitudes(held, energies[1])
    theirs = send(mine, backward[0])
    groups = [spread(after(local, *held[1:]))]
    move(theirs)
    waiting = [mine, theirs]
    items = [
        (None, 0, 0, 0, False),
        (received[0], 1, 0, 1, False),
        (received[1], from_step[0], 1, 0, False),
        (None, to_step[0], 1, 1, True),
    ]
    gates = groups[0][1:]
    for number, steps in enumerate(step_groups):
        columns = column_groups[2 + number]
        while len(received) < 2 + 2 * steps[-1]:
            move()
        far = [block for i in steps for block in received[2 * i : 2 * i + 2]]
        far = [after(block, *gates) for block in far]
        parts, held = reduced(far, columns, jnp.bfloat16)
        while len(received) < len(moves) - 1:
            move()
        amplitude = amplitudes(held, energies[2 + number])
        if number == 0:
            move(amplitude)
        for place, column in enumerate(columns):
            items.append((far[place], column, 1 + number, len(waiting) + place, False))
        group = jnp.concatenate([*waiting, amplitude])
        groups.append(spread(group))
        waiting = []
        gates = [group]
    items[3] = (received[-1], *items[3][1:])
    items = items[:3] + items[4:] + [items[3]]
    return accumulate(blocks, None, items, groups, plan, shards, jnp.bfloat16)


def solution(mesh):
    placed = (P("orb", None, "aux"), P(), P(), P())
    return jax.shard_map(
        on_device, mesh=mesh, in_specs=placed, out_specs=P("orb", None, "aux"), check_vma=False
    )
```

time: 210 us -> 111 us (0.53)
  blocking collectives: 75.2 us -> 0 us
  waiting for transfers between devices: 84.8 us -> 27.5 us
  starting transfers between devices: 0.01 us -> 43.8 us
  Pallas kernels: 0 us -> 30.9 us
  matrix products: 19.6 us -> 0 us
  between operations: 13.4 us -> 0.3 us
  local copies, waits for them, and re-layouts: 10.8 us -> 2.55 us
    psum x1 -> x0, waiting for transfers between devices: 84.8 us -> none  [reduce_amplitudes(): kernel = lax.psum(kernel_part, 'aux')]
    all_to_all x1 -> x0, blocking collectives: 75.2 us -> none  [on_device(): lax.all_to_all(outgoing, 'orb', split_axis=0, concat_axis=0, tiled=True)]
    ppermute x0 -> x29, starting transfers between devices: none -> 43.8 us  [the longest x21 28.5 us: around(): lax.ppermute(array, 'aux', [(i, (i + shift) % shards) for i in range(shar...]
    pallas_call x0 -> x8, Pallas kernels: none -> 30.9 us  [the longest x4 12.1 us: kernel_parts(): pl.pallas_call(body, out_shape=[jax.ShapeDtypeStruct((pairs, rows, width)...]
    ppermute x0 -> x29, waiting for transfers between devices: none -> 27.5 us  [the longest x21 24.2 us: around(): lax.ppermute(array, 'aux', [(i, (i + shift) % shards) for i in range(shar...]
    dot_general x3 -> x0, matrix products: 19.6 us -> none  [the longest x1 11.2 us: accumulate(): jnp.einsum('si,sap->iap', pieces[2], product, precision=lax.Precision.HIG...]
    gather x3 -> x0, local copies, waits for them, and re-layouts: 4.73 us -> none  [the longest x1 3.6 us: on_device(): outgoing = jnp.take(blocks, wanted, axis=0)]
    select_n x2 -> x0, other arithmetic: 4.15 us -> none  [the longest x1 3.45 us: on_device(): outgoing = jnp.take(blocks, wanted, axis=0)]
  transfers between devices with their start and end apart: 1 -> 29, of which waited for: 1 -> 14; matrix products, arithmetic and copies ran while one was open for 1% -> 3% of each run, Pallas kernels for 0% -> 17%
where the time goes in v1:
time: 111 us; the launch traced here: 109 us
  starting transfers between devices  43.8 us (39%)
  Pallas kernels  30.9 us (28%)
  waiting for transfers between devices  27.5 us (25%)
  other arithmetic  3.77 us (3%)
  local copies, waits for them, and re-layouts  2.55 us (2%)
    ppermute x21, starting transfers between devices, around(): lax.ppermute(array, 'aux', [(i, (i + shift) % shards) for i in range(shar...  28.5 us
    ppermute x21, waiting for transfers between devices, around(): lax.ppermute(array, 'aux', [(i, (i + shift) % shards) for i in range(shar...  24.2 us
    ppermute x8, starting transfers between devices, send(): return lax.ppermute(array, 'orb', list(enumerate(step)))  15.3 us
    pallas_call x4, Pallas kernels, kernel_parts(): pl.pallas_call(body, out_shape=[jax.ShapeDtypeStruct((pairs, rows, width)...  12.1 us
    pallas_call x2, Pallas kernels, pick(): pl.pallas_call(body, grid_spec=pltpu.PrefetchScalarGridSpec(num_scalar_pr...  8.69 us
    pallas_call x1, Pallas kernels, accumulate(): pl.pallas_call(body, grid_spec=pltpu.PrefetchScalarGridSpec(num_scalar_pr...  7.6 us
    convert_element_type x4, other arithmetic, amplitudes(): return (-kernel / denominator).astype(jnp.bfloat16)  3.75 us
    ppermute x8, waiting for transfers between devices, send(): return lax.ppermute(array, 'orb', list(enumerate(step)))  3.39 us
  transfers between devices with their start and end apart: 29, of which 14 were waited for; matrix products, arithmetic and copies ran while one was open for 3% of the time, Pallas kernels for 17%

profile of v1, /device:TPU:1, one launch (start us, length us, event | category | flops | bytes accessed | tf_op | source)
XLA Modules:
  0.0 108.9 jit_solution(149150855565986062)
XLA Ops:
  0.0 4.5 %pick.2 = (bf16[256,1536]{1,0:T(8,128)(2,1)}, bf16[256,1536]{1,0:T(8,128)(2,1)}, bf16[256,1536]{1,0:T(8,128)(2,1)}, bf16[256,1536]{1,0:T(8,128)(2,1)}, s32[26]{0:T(128)}) custom-call(s32[8,8]{1,0:T(8,128)} %refs_0_.2, s32[8,8]{1,0:T(8,128)} %refs_1_.2, bf16[4,256,1536]{2,1,0:T(8,128)(2,1)} %refs_0_.3), custom_call_target="tpu_custom_call" | custom-call | flops 1 | bytes 1 | tf_op jit(solution)/shard_map/pick/pallas_call | solution.py:94
  4.5 0.2 collective-permute-start
  4.7 3.5 %collective-permute-start.1 = (bf16[256,1536]{1,0:T(8,128)(2,1)}, bf16[256,1536]{1,0:T(8,128)(2,1)S(1)}, u32[]{:S(2)}, u32[]{:S(2)}) collective-permute-start(bf16[256,1536]{1,0:T(8,128)(2,1)} %get-tuple-element.46), channel_id=1, source_target_pairs={{0,24},{4,28},{8,16},{12,20},{16,12},{20,8},{24,4},{28,0},{1,25},{... | collective-permute-start | bytes 2359304 | tf_op jit(solution)/shard_map/ppermute | solution.py:277
  8.1 0.5 collective-permute-start.2
  8.6 0.0 collective-permute-done.refs_2_.refs_1_
  8.6 0.9 copy-done.1
  9.6 3.1 %kernel_parts.4 = (f32[2,64,256]{2,1,0:T(8,128)}, f32[2,64,256]{2,1,0:T(8,128)}, f32[2,64,256]{2,1,0:T(8,128)}, f32[2,64,256]{2,1,0:T(8,128)}) custom-call(bf16[256,1536]{1,0:T(8,128)(2,1)} %get-tuple-element.48.refs_0_, bf16[256,1536]{1,0:T(8,128)(2,1)} %get-tuple-element.45.refs_1_, bf16[256,1536]{1,0:T(8,128)(2,1)} %copy-done.1), custom_call_target="tpu_custom_call" | custom-call | flops 1 | bytes 1 | tf_op jit(solution)/shard_map/kernel_parts/pallas_call | solution.py:131
  12.6 1.3 %collective-permute-start.3 = (f32[2,64,256]{2,1,0:T(8,128)}, f32[2,64,256]{2,1,0:T(8,128)S(1)}, u32[]{:S(2)}, u32[]{:S(2)}) collective-permute-start(f32[2,64,256]{2,1,0:T(8,128)} %get-tuple-element.50), channel_id=1, source_target_pairs={{0,1},{1,2},{2,3},{3,0},{4,5},{5,6},{6,7},{7,4},{8,9},{9,10},{10,1... | collective-permute-start | bytes 393224 | tf_op jit(solution)/shard_map/ppermute | solution.py:274
  13.9 2.3 %collective-permute-start.4 = (f32[2,64,256]{2,1,0:T(8,128)}, f32[2,64,256]{2,1,0:T(8,128)S(1)}, u32[]{:S(2)}, u32[]{:S(2)}) collective-permute-start(f32[2,64,256]{2,1,0:T(8,128)} %get-tuple-element.51), channel_id=1, source_target_pairs={{0,2},{1,3},{2,0},{3,1},{4,6},{5,7},{6,4},{7,5},{8,10},{9,11},{10,... | collective-permute-start | bytes 393224 | tf_op jit(solution)/shard_map/ppermute | solution.py:274
  16.2 1.1 collective-permute-start.5
  17.3 4.2 %pick.3 = (bf16[256,1536]{1,0:T(8,128)(2,1)}, bf16[256,1536]{1,0:T(8,128)(2,1)}, bf16[256,1536]{1,0:T(8,128)(2,1)}, bf16[256,1536]{1,0:T(8,128)(2,1)}) custom-call(s32[26]{0:T(128)} %get-tuple-element.44.plan.refs_0_, bf16[4,256,1536]{2,1,0:T(8,128)(2,1)} %refs_0_.3), custom_call_target="tpu_custom_call" | custom-call | flops 1 | bytes 1 | tf_op jit(solution)/shard_map/pick/pallas_call | solution.py:94
  21.5 2.5 %denominators.1 = (f32[2,64,256]{2,1,0:T(8,128)}, f32[1,64,256]{2,1,0:T(8,128)}, f32[2,64,256]{2,1,0:T(8,128)}, f32[2,64,256]{2,1,0:T(8,128)}) custom-call(s32[26]{0:T(128)} %get-tuple-element.44.plan.refs_0_, f32[32,256]{1,0:T(8,128)} %energies.1), custom_call_target="tpu_custom_call" | custom-call | flops 1 | bytes 1 | tf_op jit(solution)/shard_map/denominators/pallas_call | solution.py:163
  24.1 2.2 %collective-permute-done.1.refs_1_.refs_2_ = bf16[256,1536]{1,0:T(8,128)(2,1)S(1)} collective-permute-done((bf16[256,1536]{1,0:T(8,128)(2,1)}, bf16[256,1536]{1,0:T(8,128)(2,1)S(1)}, u32[]{:S(2)}, u32[]{:S(2)}) %collective-permute-start.1) | collective-permute-done | bytes 786464 | tf_op jit(solution)/shard_map/ppermute | solution.py:277
  26.2 0.0 collective-permute-done.3
  26.2 0.0 collective-permute-done.4
  26.3 1.4 %collective-permute-start.12 = (bf16[256,1536]{1,0:T(8,128)(2,1)}, bf16[256,1536]{1,0:T(8,128)(2,1)S(1)}, u32[]{:S(2)}, u32[]{:S(2)}) collective-permute-start(bf16[256,1536]{1,0:T(8,128)(2,1)} %get-tuple-element.67.refs_0_), channel_id=1, source_target_pairs={{0,20},{4,8},{8,28},{12,0},{16,4},{20,24},{24,12},{28,16},{1,21},{... | collective-permute-start | bytes 2359304 | tf_op jit(solution)/shard_map/ppermute | solution.py:277
  27.7 0.9 divide_convert_fusion.2.refs_8_
  28.6 2.5 %kernel_parts.5 = (f32[1,64,256]{2,1,0:T(8,128)}, bf16[1,64,256]{2,1,0:T(8,128)(2,1)}, bf16[1,64,256]{2,1,0:T(8,128)(2,1)}, bf16[1,64,256]{2,1,0:T(8,128)(2,1)}) custom-call(bf16[256,1536]{1,0:T(8,128)(2,1)} %get-tuple-element.78.refs_0_, bf16[256,1536]{1,0:T(8,128)(2,1)} %copy-done), custom_call_target="tpu_custom_call" | custom-call | flops 1 | bytes 1 | tf_op jit(solution)/shard_map/kernel_parts/pallas_call | solution.py:131
  31.1 2.2 %collective-permute-start.6 = (bf16[1,64,256]{2,1,0:T(8,128)(2,1)}, bf16[1,64,256]{2,1,0:T(8,128)(2,1)S(1)}, u32[]{:S(2)}, u32[]{:S(2)}) collective-permute-start(bf16[1,64,256]{2,1,0:T(8,128)(2,1)} %get-tuple-element.62), channel_id=1, source_target_pairs={{0,1},{1,2},{2,3},{3,0},{4,5},{5,6},{6,7},{7,4},{8,9},{9,10},{10,1... | collective-permute-start | bytes 98312 | tf_op jit(solution)/shard_map/ppermute | solution.py:274
  33.3 1.4 %collective-permute-start.7 = (bf16[1,64,256]{2,1,0:T(8,128)(2,1)}, bf16[1,64,256]{2,1,0:T(8,128)(2,1)S(1)}, u32[]{:S(2)}, u32[]{:S(2)}) collective-permute-start(bf16[1,64,256]{2,1,0:T(8,128)(2,1)} %get-tuple-element.63), channel_id=1, source_target_pairs={{0,2},{1,3},{2,0},{3,1},{4,6},{5,7},{6,4},{7,5},{8,10},{9,11},{10,... | collective-permute-start | bytes 98312 | tf_op jit(solution)/shard_map/ppermute | solution.py:274
  34.8 1.1 collective-permute-start.8
  35.8 0.2 collective-permute-done.6
  36.0 1.7 %collective-permute-done.7 = bf16[1,64,256]{2,1,0:T(8,128)(2,1)S(1)} collective-permute-done((bf16[1,64,256]{2,1,0:T(8,128)(2,1)}, bf16[1,64,256]{2,1,0:T(8,128)(2,1)S(1)}, u32[]{:S(2)}, u32[]{:S(2)}) %collective-permute-start.7) | collective-permute-done | bytes 32800 | tf_op jit(solution)/shard_map/ppermute | solution.py:274
  37.7 0.5 collective-permute-done.8
  38.2 0.9 divide_convert_fusion.3
  39.1 3.1 %collective-permute-start.13 = (bf16[1,64,256]{2,1,0:T(8,128)(2,1)S(1)}, bf16[1,64,256]{2,1,0:T(8,128)(2,1)S(1)}, u32[]{:S(2)}, u32[]{:S(2)}) collective-permute-start(bf16[1,64,256]{2,1,0:T(8,128)(2,1)S(1)} %divide_convert_fusion.3), channel_id=1, source_target_pairs={{0,28},{4,24},{8,20},{12,16},{16,8},{20,12},{24,0},{28,4},{1,29},{... | collective-permute-start | bytes 98312 | tf_op jit(solution)/shard_map/ppermute | solution.py:277
  42.2 0.0 collective-permute-done.2.refs_2_.refs_3_
  42.2 1.2 %collective-permute-done.13 = bf16[1,64,256]{2,1,0:T(8,128)(2,1)S(1)} collective-permute-done((bf16[1,64,256]{2,1,0:T(8,128)(2,1)S(1)}, bf16[1,64,256]{2,1,0:T(8,128)(2,1)S(1)}, u32[]{:S(2)}, u32[]{:S(2)}) %collective-permute-start.13) | collective-permute-done | bytes 32800 | tf_op jit(solution)/shard_map/ppermute | solution.py:277
  43.4 2.3 %collective-permute-start.14 = (bf16[256,1536]{1,0:T(8,128)(2,1)}, bf16[256,1536]{1,0:T(8,128)(2,1)S(1)}, u32[]{:S(2)}, u32[]{:S(2)}) collective-permute-start(bf16[256,1536]{1,0:T(8,128)(2,1)} %get-tuple-element.70.refs_1_), channel_id=1, source_target_pairs={{0,8},{4,20},{8,24},{12,4},{16,0},{20,28},{24,16},{28,12},{1,9},{5... | collective-permute-start | bytes 2359304 | tf_op jit(solution)/shard_map/ppermute | solution.py:277
  45.6 3.0 %collective-permute-start.11 = (bf16[2,64,256]{2,1,0:T(8,128)(2,1)S(1)}, bf16[2,64,256]{2,1,0:T(8,128)(2,1)S(1)}, u32[]{:S(2)}, u32[]{:S(2)}) collective-permute-start(bf16[2,64,256]{2,1,0:T(8,128)(2,1)S(1)} %divide_convert_fusion.2.refs_8_), channel_id=1, source_target_pairs={{0,3},{1,0},{2,1},{3,2},{4,7},{5,4},{6,5},{7,6},{8,11},{9,8},{10,9... | collective-permute-start | bytes 196616 | tf_op jit(solution)/shard_map/ppermute | solution.py:274
  48.7 0.0 collective-permute-start.10
  48.7 0.3 collective-permute-start.9
  49.0 0.5 collective-permute-start.18
  49.5 0.6 collective-permute-done.11.refs_11_
  50.0 4.5 %collective-permute-done.10.refs_10_ = bf16[2,64,256]{2,1,0:T(8,128)(2,1)S(1)} collective-permute-done((bf16[2,64,256]{2,1,0:T(8,128)(2,1)S(1)}, bf16[2,64,256]{2,1,0:T(8,128)(2,1)S(1)}, u32[]{:S(2)}, u32[]{:S(2)}) %collective-permute-start.10) | collective-permute-done | bytes 65568 | tf_op jit(solution)/shard_map/ppermute | solution.py:274
  54.6 3.3 %kernel_parts.6 = (f32[2,64,256]{2,1,0:T(8,128)}, bf16[2,64,256]{2,1,0:T(8,128)(2,1)}, bf16[2,64,256]{2,1,0:T(8,128)(2,1)}, bf16[2,64,256]{2,1,0:T(8,128)(2,1)}) custom-call(bf16[256,1536]{1,0:T(8,128)(2,1)} %get-tuple-element.67.refs_0_, bf16[256,1536]{1,0:T(8,128)(2,1)} %get-tuple-element.47.refs_1_, bf16[256,1536]{1,0:T(8,128)(2,1)} %copy-done.2, ...), custom_call_target="tpu_custom_call" | custom-call | flops 1 | bytes 1 | tf_op jit(solution)/shard_map/kernel_parts/pallas_call | solution.py:131
  57.9 0.1 collective-permute-start.15
  57.9 1.9 %collective-permute-start.16 = (bf16[2,64,256]{2,1,0:T(8,128)(2,1)}, bf16[2,64,256]{2,1,0:T(8,128)(2,1)S(1)}, u32[]{:S(2)}, u32[]{:S(2)}) collective-permute-start(bf16[2,64,256]{2,1,0:T(8,128)(2,1)} %get-tuple-element.73), channel_id=1, source_target_pairs={{0,2},{1,3},{2,0},{3,1},{4,6},{5,7},{6,4},{7,5},{8,10},{9,11},{10,... | collective-permute-start | bytes 196616 | tf_op jit(solution)/shard_map/ppermute | solution.py:274
  59.9 2.3 %collective-permute-start.17 = (bf16[2,64,256]{2,1,0:T(8,128)(2,1)}, bf16[2,64,256]{2,1,0:T(8,128)(2,1)S(1)}, u32[]{:S(2)}, u32[]{:S(2)}) collective-permute-start(bf16[2,64,256]{2,1,0:T(8,128)(2,1)} %get-tuple-element.74), channel_id=1, source_target_pairs={{0,3},{1,0},{2,1},{3,2},{4,7},{5,4},{6,5},{7,6},{8,11},{9,8},{10,9... | collective-permute-start | bytes 196616 | tf_op jit(solution)/shard_map/ppermute | solution.py:274
  62.2 0.8 collective-permute-done.15
  63.0 1.3 %collective-permute-done.17 = bf16[2,64,256]{2,1,0:T(8,128)(2,1)S(1)} collective-permute-done((bf16[2,64,256]{2,1,0:T(8,128)(2,1)}, bf16[2,64,256]{2,1,0:T(8,128)(2,1)S(1)}, u32[]{:S(2)}, u32[]{:S(2)}) %collective-permute-start.17) | collective-permute-done | bytes 65568 | tf_op jit(solution)/shard_map/ppermute | solution.py:274
  64.3 0.9 divide_convert_fusion.1
  65.3 0.0 collective-permute-done.14.refs_2_.refs_5_
  65.3 3.9 %collective-permute-start.19 = (bf16[256,1536]{1,0:T(8,128)(2,1)S(1)}, bf16[256,1536]{1,0:T(8,128)(2,1)S(1)}, u32[]{:S(2)}, u32[]{:S(2)}) collective-permute-start(bf16[256,1536]{1,0:T(8,128)(2,1)S(1)} %copy-done.7), channel_id=1, source_target_pairs={{0,28},{4,24},{8,20},{12,16},{16,8},{20,12},{24,0},{28,4},{1,29},{... | collective-permute-start | bytes 2359304 | tf_op jit(solution)/shard_map/ppermute | solution.py:277
  69.2 0.9 copy-done.5
  70.2 3.2 %kernel_parts.7 = (f32[2,64,256]{2,1,0:T(8,128)}, bf16[2,64,256]{2,1,0:T(8,128)(2,1)}, bf16[2,64,256]{2,1,0:T(8,128)(2,1)}, bf16[2,64,256]{2,1,0:T(8,128)(2,1)}) custom-call(bf16[256,1536]{1,0:T(8,128)(2,1)} %get-tuple-element.76.refs_0_, bf16[256,1536]{1,0:T(8,128)(2,1)} %get-tuple-element.70.refs_1_, bf16[256,1536]{1,0:T(8,128)(2,1)} %copy-done.4, ...), custom_call_target="tpu_custom_call" | custom-call | flops 1 | bytes 1 | tf_op jit(solution)/shard_map/kernel_parts/pallas_call | solution.py:131
  73.4 1.1 %collective-permute-start.23 = (bf16[2,64,256]{2,1,0:T(8,128)(2,1)}, bf16[2,64,256]{2,1,0:T(8,128)(2,1)S(1)}, u32[]{:S(2)}, u32[]{:S(2)}) collective-permute-start(bf16[2,64,256]{2,1,0:T(8,128)(2,1)} %get-tuple-element.80), channel_id=1, source_target_pairs={{0,1},{1,2},{2,3},{3,0},{4,5},{5,6},{6,7},{7,4},{8,9},{9,10},{10,1... | collective-permute-start | bytes 196616 | tf_op jit(solution)/shard_map/ppermute | solution.py:274
  74.6 1.9 %collective-permute-start.24 = (bf16[2,64,256]{2,1,0:T(8,128)(2,1)}, bf16[2,64,256]{2,1,0:T(8,128)(2,1)S(1)}, u32[]{:S(2)}, u32[]{:S(2)}) collective-permute-start(bf16[2,64,256]{2,1,0:T(8,128)(2,1)} %get-tuple-element.81), channel_id=1, source_target_pairs={{0,2},{1,3},{2,0},{3,1},{4,6},{5,7},{6,4},{7,5},{8,10},{9,11},{10,... | collective-permute-start | bytes 196616 | tf_op jit(solution)/shard_map/ppermute | solution.py:274
  76.5 0.2 collective-permute-start.25
  76.7 1.4 %collective-permute-start.22 = (bf16[4,64,256]{2,1,0:T(8,128)(2,1)S(1)}, bf16[4,64,256]{2,1,0:T(8,128)(2,1)S(1)}, u32[]{:S(2)}, u32[]{:S(2)}) collective-permute-start(bf16[4,64,256]{2,1,0:T(8,128)(2,1)S(1)} %pad_maximum_fusion.refs_12_), channel_id=1, source_target_pairs={{0,3},{1,0},{2,1},{3,2},{4,7},{5,4},{6,5},{7,6},{8,11},{9,8},{10,9... | collective-permute-start | bytes 393224 | tf_op jit(solution)/shard_map/ppermute | solution.py:274
  78.1 0.9 collective-permute-done.23
  79.0 0.1 collective-permute-start.21
  79.2 3.2 %collective-permute-done.24 = bf16[2,64,256]{2,1,0:T(8,128)(2,1)S(1)} collective-permute-done((bf16[2,64,256]{2,1,0:T(8,128)(2,1)}, bf16[2,64,256]{2,1,0:T(8,128)(2,1)S(1)}, u32[]{:S(2)}, u32[]{:S(2)}) %collective-permute-start.24) | collective-permute-done | bytes 65568 | tf_op jit(solution)/shard_map/ppermute | solution.py:274
  82.3 0.0 collective-permute-start.20
  82.3 0.0 collective-permute-done.25
  82.3 1.0 divide_convert_fusion.refs_16_
  83.3 3.3 %collective-permute-start.28 = (bf16[2,64,256]{2,1,0:T(8,128)(2,1)S(1)}, bf16[2,64,256]{2,1,0:T(8,128)(2,1)S(1)}, u32[]{:S(2)}, u32[]{:S(2)}) collective-permute-start(bf16[2,64,256]{2,1,0:T(8,128)(2,1)S(1)} %divide_convert_fusion.refs_16_), channel_id=1, source_target_pairs={{0,3},{1,0},{2,1},{3,2},{4,7},{5,4},{6,5},{7,6},{8,11},{9,8},{10,9... | collective-permute-start | bytes 196616 | tf_op jit(solution)/shard_map/ppermute | solution.py:274
  86.6 3.4 %collective-permute-start.27 = (bf16[2,64,256]{2,1,0:T(8,128)(2,1)S(1)}, bf16[2,64,256]{2,1,0:T(8,128)(2,1)S(1)}, u32[]{:S(2)}, u32[]{:S(2)}) collective-permute-start(bf16[2,64,256]{2,1,0:T(8,128)(2,1)S(1)} %divide_convert_fusion.refs_16_), channel_id=1, source_target_pairs={{0,2},{1,3},{2,0},{3,1},{4,6},{5,7},{6,4},{7,5},{8,10},{9,11},{10,... | collective-permute-start | bytes 196616 | tf_op jit(solution)/shard_map/ppermute | solution.py:274
  90.0 5.6 %collective-permute-done.21.refs_14_ = bf16[4,64,256]{2,1,0:T(8,128)(2,1)S(1)} collective-permute-done((bf16[4,64,256]{2,1,0:T(8,128)(2,1)S(1)}, bf16[4,64,256]{2,1,0:T(8,128)(2,1)S(1)}, u32[]{:S(2)}, u32[]{:S(2)}) %collective-permute-start.21) | collective-permute-done | bytes 131104 | tf_op jit(solution)/shard_map/ppermute | solution.py:274
  95.7 0.0 collective-permute-done.19.refs_7_
  95.7 3.4 %collective-permute-done.27.refs_18_ = bf16[2,64,256]{2,1,0:T(8,128)(2,1)S(1)} collective-permute-done((bf16[2,64,256]{2,1,0:T(8,128)(2,1)S(1)}, bf16[2,64,256]{2,1,0:T(8,128)(2,1)S(1)}, u32[]{:S(2)}, u32[]{:S(2)}) %collective-permute-start.27) | collective-permute-done | bytes 65568 | tf_op jit(solution)/shard_map/ppermute | solution.py:274
  99.2 1.4 %collective-permute-done.26.refs_17_ = bf16[2,64,256]{2,1,0:T(8,128)(2,1)S(1)} collective-permute-done((bf16[2,64,256]{2,1,0:T(8,128)(2,1)S(1)}, bf16[2,64,256]{2,1,0:T(8,128)(2,1)S(1)}, u32[]{:S(2)}, u32[]{:S(2)}) %collective-permute-start.26) | collective-permute-done | bytes 65568 | tf_op jit(solution)/shard_map/ppermute | solution.py:274
  100.7 0.6 copy-done.22
  101.3 7.6 %accumulate.1 = bf16[4,256,1536]{2,1,0:T(8,128)(2,1)} custom-call(s32[26]{0:T(128)} %get-tuple-element.44.plan.refs_0_, bf16[4,256,1536]{2,1,0:T(8,128)(2,1)} %refs_0_.3, bf16[256,1536]{1,0:T(8,128)(2,1)} %copy-done.1, bf16[256,1536]{1,0:T(8,128)(2,1)} %copy-done, bf16[256,1536]{1,0:T(8,128)(2,1)} %copy-done.2, bf16[256,1536]{1,0:T(8,128)(2,1)} %copy-done.3, ...), custom_call_target="tpu_custom_call" | custom-call | flops 1 | bytes 1 | tf_op jit(solution)/shard_map/accumulate/pallas_call | solution.py:233
  (53 shorter events, 0.1 us)
Async XLA Ops:
  4.5 4.2 %collective-permute-start = (bf16[256,1536]{1,0:T(8,128)(2,1)}, bf16[256,1536]{1,0:T(8,128)(2,1)S(1)}, u32[]{:S(2)}, u32[]{:S(2)}) collective-permute-start(bf16[256,1536]{1,0:T(8,128)(2,1)} %get-tuple-element.45.refs_1_), channel_id=1, source_target_pairs={{0,4},{4,0},{8,12},{12,8},{16,20},{20,16},{24,28},{28,24},{1,5},{5... | collective-permute-start | bytes 2359304 | tf_op jit(solution)/shard_map/ppermute | solution.py:277
  4.7 21.6 %collective-permute-start.1 = (bf16[256,1536]{1,0:T(8,128)(2,1)}, bf16[256,1536]{1,0:T(8,128)(2,1)S(1)}, u32[]{:S(2)}, u32[]{:S(2)}) collective-permute-start(bf16[256,1536]{1,0:T(8,128)(2,1)} %get-tuple-element.46), channel_id=1, source_target_pairs={{0,24},{4,28},{8,16},{12,20},{16,12},{20,8},{24,4},{28,0},{1,25},{... | collective-permute-start | bytes 2359304 | tf_op jit(solution)/shard_map/ppermute | solution.py:277
  8.1 34.0 %collective-permute-start.2 = (bf16[256,1536]{1,0:T(8,128)(2,1)}, bf16[256,1536]{1,0:T(8,128)(2,1)S(1)}, u32[]{:S(2)}, u32[]{:S(2)}) collective-permute-start(bf16[256,1536]{1,0:T(8,128)(2,1)} %get-tuple-element.47.refs_1_), channel_id=1, source_target_pairs={{0,12},{4,16},{8,4},{12,24},{16,28},{20,0},{24,20},{28,8},{1,13},{... | collective-permute-start | bytes 2359304 | tf_op jit(solution)/shard_map/ppermute | solution.py:277
  8.6 0.9 copy-start.1
  12.6 15.0 %copy-start.16 = (f32[2,64,256]{2,1,0:T(8,128)S(1)}, f32[2,64,256]{2,1,0:T(8,128)}, u32[]{:S(2)}) copy-start(f32[2,64,256]{2,1,0:T(8,128)} %get-tuple-element.49) | copy-start | bytes 393220
  12.6 13.6 %collective-permute-start.3 = (f32[2,64,256]{2,1,0:T(8,128)}, f32[2,64,256]{2,1,0:T(8,128)S(1)}, u32[]{:S(2)}, u32[]{:S(2)}) collective-permute-start(f32[2,64,256]{2,1,0:T(8,128)} %get-tuple-element.50), channel_id=1, source_target_pairs={{0,1},{1,2},{2,3},{3,0},{4,5},{5,6},{6,7},{7,4},{8,9},{9,10},{10,1... | collective-permute-start | bytes 393224 | tf_op jit(solution)/shard_map/ppermute | solution.py:274
  13.9 12.3 %collective-permute-start.4 = (f32[2,64,256]{2,1,0:T(8,128)}, f32[2,64,256]{2,1,0:T(8,128)S(1)}, u32[]{:S(2)}, u32[]{:S(2)}) collective-permute-start(f32[2,64,256]{2,1,0:T(8,128)} %get-tuple-element.51), channel_id=1, source_target_pairs={{0,2},{1,3},{2,0},{3,1},{4,6},{5,7},{6,4},{7,5},{8,10},{9,11},{10,... | collective-permute-start | bytes 393224 | tf_op jit(solution)/shard_map/ppermute | solution.py:274
  16.2 10.0 %collective-permute-start.5 = (f32[2,64,256]{2,1,0:T(8,128)}, f32[2,64,256]{2,1,0:T(8,128)S(1)}, u32[]{:S(2)}, u32[]{:S(2)}) collective-permute-start(f32[2,64,256]{2,1,0:T(8,128)} %get-tuple-element.52), channel_id=1, source_target_pairs={{0,3},{1,0},{2,1},{3,2},{4,7},{5,4},{6,5},{7,6},{8,11},{9,8},{10,9... | collective-permute-start | bytes 393224 | tf_op jit(solution)/shard_map/ppermute | solution.py:274
  21.5 43.8 %copy-start.7 = (bf16[256,1536]{1,0:T(8,128)(2,1)S(1)}, bf16[256,1536]{1,0:T(8,128)(2,1)}, u32[]{:S(2)}) copy-start(bf16[256,1536]{1,0:T(8,128)(2,1)} %get-tuple-element.78.refs_0_) | copy-start | bytes 2359300
  24.1 40.2 %copy-start.15 = (f32[2,64,256]{2,1,0:T(8,128)S(1)}, f32[2,64,256]{2,1,0:T(8,128)}, u32[]{:S(2)}) copy-start(f32[2,64,256]{2,1,0:T(8,128)} %get-tuple-element.56) | copy-start | bytes 393220
  26.2 2.4 %copy-start = (bf16[256,1536]{1,0:T(8,128)(2,1)}, bf16[256,1536]{1,0:T(8,128)(2,1)S(1)}, u32[]{:S(2)}) copy-start(bf16[256,1536]{1,0:T(8,128)(2,1)S(1)} %collective-permute-done.1.refs_1_.refs_2_) | copy-start | bytes 2359300
  26.3 22.7 %collective-permute-start.12 = (bf16[256,1536]{1,0:T(8,128)(2,1)}, bf16[256,1536]{1,0:T(8,128)(2,1)S(1)}, u32[]{:S(2)}, u32[]{:S(2)}) collective-permute-start(bf16[256,1536]{1,0:T(8,128)(2,1)} %get-tuple-element.67.refs_0_), channel_id=1, source_target_pairs={{0,20},{4,8},{8,28},{12,0},{16,4},{20,24},{24,12},{28,16},{1,21},{... | collective-permute-start | bytes 2359304 | tf_op jit(solution)/shard_map/ppermute | solution.py:277
  28.6 44.8 %copy-start.9 = (bf16[2,64,256]{2,1,0:T(8,128)(2,1)}, bf16[2,64,256]{2,1,0:T(8,128)(2,1)S(1)}, u32[]{:S(2)}) copy-start(bf16[2,64,256]{2,1,0:T(8,128)(2,1)S(1)} %divide_convert_fusion.2.refs_8_) | copy-start | bytes 196612
  31.1 4.8 %collective-permute-start.6 = (bf16[1,64,256]{2,1,0:T(8,128)(2,1)}, bf16[1,64,256]{2,1,0:T(8,128)(2,1)S(1)}, u32[]{:S(2)}, u32[]{:S(2)}) collective-permute-start(bf16[1,64,256]{2,1,0:T(8,128)(2,1)} %get-tuple-element.62), channel_id=1, source_target_pairs={{0,1},{1,2},{2,3},{3,0},{4,5},{5,6},{6,7},{7,4},{8,9},{9,10},{10,1... | collective-permute-start | bytes 98312 | tf_op jit(solution)/shard_map/ppermute | solution.py:274
  33.3 4.3 %collective-permute-start.7 = (bf16[1,64,256]{2,1,0:T(8,128)(2,1)}, bf16[1,64,256]{2,1,0:T(8,128)(2,1)S(1)}, u32[]{:S(2)}, u32[]{:S(2)}) collective-permute-start(bf16[1,64,256]{2,1,0:T(8,128)(2,1)} %get-tuple-element.63), channel_id=1, source_target_pairs={{0,2},{1,3},{2,0},{3,1},{4,6},{5,7},{6,4},{7,5},{8,10},{9,11},{10,... | collective-permute-start | bytes 98312 | tf_op jit(solution)/shard_map/ppermute | solution.py:274
  34.8 3.4 %collective-permute-start.8 = (bf16[1,64,256]{2,1,0:T(8,128)(2,1)}, bf16[1,64,256]{2,1,0:T(8,128)(2,1)S(1)}, u32[]{:S(2)}, u32[]{:S(2)}) collective-permute-start(bf16[1,64,256]{2,1,0:T(8,128)(2,1)} %get-tuple-element.64), channel_id=1, source_target_pairs={{0,3},{1,0},{2,1},{3,2},{4,7},{5,4},{6,5},{7,6},{8,11},{9,8},{10,9... | collective-permute-start | bytes 98312 | tf_op jit(solution)/shard_map/ppermute | solution.py:274
  39.1 43.3 %copy-start.14 = (f32[2,64,256]{2,1,0:T(8,128)S(1)}, f32[2,64,256]{2,1,0:T(8,128)}, u32[]{:S(2)}) copy-start(f32[2,64,256]{2,1,0:T(8,128)} %get-tuple-element.57) | copy-start | bytes 393220
  39.1 4.3 %collective-permute-start.13 = (bf16[1,64,256]{2,1,0:T(8,128)(2,1)S(1)}, bf16[1,64,256]{2,1,0:T(8,128)(2,1)S(1)}, u32[]{:S(2)}, u32[]{:S(2)}) collective-permute-start(bf16[1,64,256]{2,1,0:T(8,128)(2,1)S(1)} %divide_convert_fusion.3), channel_id=1, source_target_pairs={{0,28},{4,24},{8,20},{12,16},{16,8},{20,12},{24,0},{28,4},{1,29},{... | collective-permute-start | bytes 98312 | tf_op jit(solution)/shard_map/ppermute | solution.py:277
  42.2 12.4 %copy-start.2 = (bf16[256,1536]{1,0:T(8,128)(2,1)}, bf16[256,1536]{1,0:T(8,128)(2,1)S(1)}, u32[]{:S(2)}) copy-start(bf16[256,1536]{1,0:T(8,128)(2,1)S(1)} %collective-permute-done.2.refs_2_.refs_3_) | copy-start | bytes 2359300
  43.4 21.9 %collective-permute-start.14 = (bf16[256,1536]{1,0:T(8,128)(2,1)}, bf16[256,1536]{1,0:T(8,128)(2,1)S(1)}, u32[]{:S(2)}, u32[]{:S(2)}) collective-permute-start(bf16[256,1536]{1,0:T(8,128)(2,1)} %get-tuple-element.70.refs_1_), channel_id=1, source_target_pairs={{0,8},{4,20},{8,24},{12,4},{16,0},{20,28},{24,16},{28,12},{1,9},{5... | collective-permute-start | bytes 2359304 | tf_op jit(solution)/shard_map/ppermute | solution.py:277
  45.6 4.4 %collective-permute-start.11 = (bf16[2,64,256]{2,1,0:T(8,128)(2,1)S(1)}, bf16[2,64,256]{2,1,0:T(8,128)(2,1)S(1)}, u32[]{:S(2)}, u32[]{:S(2)}) collective-permute-start(bf16[2,64,256]{2,1,0:T(8,128)(2,1)S(1)} %divide_convert_fusion.2.refs_8_), channel_id=1, source_target_pairs={{0,3},{1,0},{2,1},{3,2},{4,7},{5,4},{6,5},{7,6},{8,11},{9,8},{10,9... | collective-permute-start | bytes 196616 | tf_op jit(solution)/shard_map/ppermute | solution.py:274
  48.7 5.9 %collective-permute-start.10 = (bf16[2,64,256]{2,1,0:T(8,128)(2,1)S(1)}, bf16[2,64,256]{2,1,0:T(8,128)(2,1)S(1)}, u32[]{:S(2)}, u32[]{:S(2)}) collective-permute-start(bf16[2,64,256]{2,1,0:T(8,128)(2,1)S(1)} %divide_convert_fusion.2.refs_8_), channel_id=1, source_target_pairs={{0,2},{1,3},{2,0},{3,1},{4,6},{5,7},{6,4},{7,5},{8,10},{9,11},{10,... | collective-permute-start | bytes 196616 | tf_op jit(solution)/shard_map/ppermute | solution.py:274
  48.7 5.9 %collective-permute-start.9 = (bf16[2,64,256]{2,1,0:T(8,128)(2,1)S(1)}, bf16[2,64,256]{2,1,0:T(8,128)(2,1)S(1)}, u32[]{:S(2)}, u32[]{:S(2)}) collective-permute-start(bf16[2,64,256]{2,1,0:T(8,128)(2,1)S(1)} %divide_convert_fusion.2.refs_8_), channel_id=1, source_target_pairs={{0,1},{1,2},{2,3},{3,0},{4,5},{5,6},{6,7},{7,4},{8,9},{9,10},{10,1... | collective-permute-start | bytes 196616 | tf_op jit(solution)/shard_map/ppermute | solution.py:274
  49.0 5.6 %copy-start.3 = (bf16[256,1536]{1,0:T(8,128)(2,1)}, bf16[256,1536]{1,0:T(8,128)(2,1)S(1)}, u32[]{:S(2)}) copy-start(bf16[256,1536]{1,0:T(8,128)(2,1)S(1)} %collective-permute-done.12.refs_3_.refs_4_) | copy-start | bytes 2359300
  49.0 20.2 %collective-permute-start.18 = (bf16[256,1536]{1,0:T(8,128)(2,1)}, bf16[256,1536]{1,0:T(8,128)(2,1)S(1)}, u32[]{:S(2)}, u32[]{:S(2)}) collective-permute-start(bf16[256,1536]{1,0:T(8,128)(2,1)} %get-tuple-element.76.refs_0_), channel_id=1, source_target_pairs={{0,16},{4,12},{8,0},{12,28},{16,24},{20,4},{24,8},{28,20},{1,17},{... | collective-permute-start | bytes 2359304 | tf_op jit(solution)/shard_map/ppermute | solution.py:277
  50.0 23.4 %copy-start.17 = (bf16[2,64,256]{2,1,0:T(8,128)(2,1)}, bf16[2,64,256]{2,1,0:T(8,128)(2,1)S(1)}, u32[]{:S(2)}) copy-start(bf16[2,64,256]{2,1,0:T(8,128)(2,1)S(1)} %collective-permute-done.11.refs_11_) | copy-start | bytes 196612
  54.6 18.8 %copy-start.18 = (bf16[2,64,256]{2,1,0:T(8,128)(2,1)}, bf16[2,64,256]{2,1,0:T(8,128)(2,1)S(1)}, u32[]{:S(2)}) copy-start(bf16[2,64,256]{2,1,0:T(8,128)(2,1)S(1)} %collective-permute-done.10.refs_10_) | copy-start | bytes 196612
  54.6 18.8 %copy-start.19 = (bf16[2,64,256]{2,1,0:T(8,128)(2,1)}, bf16[2,64,256]{2,1,0:T(8,128)(2,1)S(1)}, u32[]{:S(2)}) copy-start(bf16[2,64,256]{2,1,0:T(8,128)(2,1)S(1)} %collective-permute-done.9.refs_9_) | copy-start | bytes 196612
  57.9 5.2 %collective-permute-start.15 = (bf16[2,64,256]{2,1,0:T(8,128)(2,1)}, bf16[2,64,256]{2,1,0:T(8,128)(2,1)S(1)}, u32[]{:S(2)}, u32[]{:S(2)}) collective-permute-start(bf16[2,64,256]{2,1,0:T(8,128)(2,1)} %get-tuple-element.72), channel_id=1, source_target_pairs={{0,1},{1,2},{2,3},{3,0},{4,5},{5,6},{6,7},{7,4},{8,9},{9,10},{10,1... | collective-permute-start | bytes 196616 | tf_op jit(solution)/shard_map/ppermute | solution.py:274
  57.9 5.1 %collective-permute-start.16 = (bf16[2,64,256]{2,1,0:T(8,128)(2,1)}, bf16[2,64,256]{2,1,0:T(8,128)(2,1)S(1)}, u32[]{:S(2)}, u32[]{:S(2)}) collective-permute-start(bf16[2,64,256]{2,1,0:T(8,128)(2,1)} %get-tuple-element.73), channel_id=1, source_target_pairs={{0,2},{1,3},{2,0},{3,1},{4,6},{5,7},{6,4},{7,5},{8,10},{9,11},{10,... | collective-permute-start | bytes 196616 | tf_op jit(solution)/shard_map/ppermute | solution.py:274
  59.9 4.5 %collective-permute-start.17 = (bf16[2,64,256]{2,1,0:T(8,128)(2,1)}, bf16[2,64,256]{2,1,0:T(8,128)(2,1)S(1)}, u32[]{:S(2)}, u32[]{:S(2)}) collective-permute-start(bf16[2,64,256]{2,1,0:T(8,128)(2,1)} %get-tuple-element.74), channel_id=1, source_target_pairs={{0,3},{1,0},{2,1},{3,2},{4,7},{5,4},{6,5},{7,6},{8,11},{9,8},{10,9... | collective-permute-start | bytes 196616 | tf_op jit(solution)/shard_map/ppermute | solution.py:274
  65.3 3.9 %copy-start.4 = (bf16[256,1536]{1,0:T(8,128)(2,1)}, bf16[256,1536]{1,0:T(8,128)(2,1)S(1)}, u32[]{:S(2)}) copy-start(bf16[256,1536]{1,0:T(8,128)(2,1)S(1)} %collective-permute-done.14.refs_2_.refs_5_) | copy-start | bytes 2359300
  65.3 30.4 %collective-permute-start.19 = (bf16[256,1536]{1,0:T(8,128)(2,1)S(1)}, bf16[256,1536]{1,0:T(8,128)(2,1)S(1)}, u32[]{:S(2)}, u32[]{:S(2)}) collective-permute-start(bf16[256,1536]{1,0:T(8,128)(2,1)S(1)} %copy-done.7), channel_id=1, source_target_pairs={{0,28},{4,24},{8,20},{12,16},{16,8},{20,12},{24,0},{28,4},{1,29},{... | collective-permute-start | bytes 2359304 | tf_op jit(solution)/shard_map/ppermute | solution.py:277
  69.2 31.4 %copy-start.8 = (bf16[4,64,256]{2,1,0:T(8,128)(2,1)}, bf16[4,64,256]{2,1,0:T(8,128)(2,1)S(1)}, u32[]{:S(2)}) copy-start(bf16[4,64,256]{2,1,0:T(8,128)(2,1)S(1)} %pad_maximum_fusion.refs_12_) | copy-start | bytes 393220
  69.2 0.9 copy-start.5
  73.4 5.6 %collective-permute-start.23 = (bf16[2,64,256]{2,1,0:T(8,128)(2,1)}, bf16[2,64,256]{2,1,0:T(8,128)(2,1)S(1)}, u32[]{:S(2)}, u32[]{:S(2)}) collective-permute-start(bf16[2,64,256]{2,1,0:T(8,128)(2,1)} %get-tuple-element.80), channel_id=1, source_target_pairs={{0,1},{1,2},{2,3},{3,0},{4,5},{5,6},{6,7},{7,4},{8,9},{9,10},{10,1... | collective-permute-start | bytes 196616 | tf_op jit(solution)/shard_map/ppermute | solution.py:274
  74.6 7.8 %collective-permute-start.24 = (bf16[2,64,256]{2,1,0:T(8,128)(2,1)}, bf16[2,64,256]{2,1,0:T(8,128)(2,1)S(1)}, u32[]{:S(2)}, u32[]{:S(2)}) collective-permute-start(bf16[2,64,256]{2,1,0:T(8,128)(2,1)} %get-tuple-element.81), channel_id=1, source_target_pairs={{0,2},{1,3},{2,0},{3,1},{4,6},{5,7},{6,4},{7,5},{8,10},{9,11},{10,... | collective-permute-start | bytes 196616 | tf_op jit(solution)/shard_map/ppermute | solution.py:274
  76.5 5.8 %collective-permute-start.25 = (bf16[2,64,256]{2,1,0:T(8,128)(2,1)}, bf16[2,64,256]{2,1,0:T(8,128)(2,1)S(1)}, u32[]{:S(2)}, u32[]{:S(2)}) collective-permute-start(bf16[2,64,256]{2,1,0:T(8,128)(2,1)} %get-tuple-element.82), channel_id=1, source_target_pairs={{0,3},{1,0},{2,1},{3,2},{4,7},{5,4},{6,5},{7,6},{8,11},{9,8},{10,9... | collective-permute-start | bytes 196616 | tf_op jit(solution)/shard_map/ppermute | solution.py:274
  76.7 9.9 %collective-permute-start.22 = (bf16[4,64,256]{2,1,0:T(8,128)(2,1)S(1)}, bf16[4,64,256]{2,1,0:T(8,128)(2,1)S(1)}, u32[]{:S(2)}, u32[]{:S(2)}) collective-permute-start(bf16[4,64,256]{2,1,0:T(8,128)(2,1)S(1)} %pad_maximum_fusion.refs_12_), channel_id=1, source_target_pairs={{0,3},{1,0},{2,1},{3,2},{4,7},{5,4},{6,5},{7,6},{8,11},{9,8},{10,9... | collective-permute-start | bytes 393224 | tf_op jit(solution)/shard_map/ppermute | solution.py:274
  79.0 16.6 %collective-permute-start.21 = (bf16[4,64,256]{2,1,0:T(8,128)(2,1)S(1)}, bf16[4,64,256]{2,1,0:T(8,128)(2,1)S(1)}, u32[]{:S(2)}, u32[]{:S(2)}) collective-permute-start(bf16[4,64,256]{2,1,0:T(8,128)(2,1)S(1)} %pad_maximum_fusion.refs_12_), channel_id=1, source_target_pairs={{0,2},{1,3},{2,0},{3,1},{4,6},{5,7},{6,4},{7,5},{8,10},{9,11},{10,... | collective-permute-start | bytes 393224 | tf_op jit(solution)/shard_map/ppermute | solution.py:274
  82.3 13.3 %collective-permute-start.20 = (bf16[4,64,256]{2,1,0:T(8,128)(2,1)S(1)}, bf16[4,64,256]{2,1,0:T(8,128)(2,1)S(1)}, u32[]{:S(2)}, u32[]{:S(2)}) collective-permute-start(bf16[4,64,256]{2,1,0:T(8,128)(2,1)S(1)} %pad_maximum_fusion.refs_12_), channel_id=1, source_target_pairs={{0,1},{1,2},{2,3},{3,0},{4,5},{5,6},{6,7},{7,4},{8,9},{9,10},{10,1... | collective-permute-start | bytes 393224 | tf_op jit(solution)/shard_map/ppermute | solution.py:274
  83.3 17.3 %copy-start.10 = (bf16[2,64,256]{2,1,0:T(8,128)(2,1)}, bf16[2,64,256]{2,1,0:T(8,128)(2,1)S(1)}, u32[]{:S(2)}) copy-start(bf16[2,64,256]{2,1,0:T(8,128)(2,1)S(1)} %divide_convert_fusion.refs_16_) | copy-start | bytes 196612
  83.3 12.4 %collective-permute-start.28 = (bf16[2,64,256]{2,1,0:T(8,128)(2,1)S(1)}, bf16[2,64,256]{2,1,0:T(8,128)(2,1)S(1)}, u32[]{:S(2)}, u32[]{:S(2)}) collective-permute-start(bf16[2,64,256]{2,1,0:T(8,128)(2,1)S(1)} %divide_convert_fusion.refs_16_), channel_id=1, source_target_pairs={{0,3},{1,0},{2,1},{3,2},{4,7},{5,4},{6,5},{7,6},{8,11},{9,8},{10,9... | collective-permute-start | bytes 196616 | tf_op jit(solution)/shard_map/ppermute | solution.py:274
  86.6 14.0 %copy-start.11 = (bf16[4,64,256]{2,1,0:T(8,128)(2,1)}, bf16[4,64,256]{2,1,0:T(8,128)(2,1)S(1)}, u32[]{:S(2)}) copy-start(bf16[4,64,256]{2,1,0:T(8,128)(2,1)S(1)} %collective-permute-done.22.refs_15_) | copy-start | bytes 393220
  86.6 12.6 %collective-permute-start.27 = (bf16[2,64,256]{2,1,0:T(8,128)(2,1)S(1)}, bf16[2,64,256]{2,1,0:T(8,128)(2,1)S(1)}, u32[]{:S(2)}, u32[]{:S(2)}) collective-permute-start(bf16[2,64,256]{2,1,0:T(8,128)(2,1)S(1)} %divide_convert_fusion.refs_16_), channel_id=1, source_target_pairs={{0,2},{1,3},{2,0},{3,1},{4,6},{5,7},{6,4},{7,5},{8,10},{9,11},{10,... | collective-permute-start | bytes 196616 | tf_op jit(solution)/shard_map/ppermute | solution.py:274
  95.7 4.9 %copy-start.12 = (bf16[4,64,256]{2,1,0:T(8,128)(2,1)}, bf16[4,64,256]{2,1,0:T(8,128)(2,1)S(1)}, u32[]{:S(2)}) copy-start(bf16[4,64,256]{2,1,0:T(8,128)(2,1)S(1)} %collective-permute-done.21.refs_14_) | copy-start | bytes 393220
  95.7 4.9 %collective-permute-start.26 = (bf16[2,64,256]{2,1,0:T(8,128)(2,1)S(1)}, bf16[2,64,256]{2,1,0:T(8,128)(2,1)S(1)}, u32[]{:S(2)}, u32[]{:S(2)}) collective-permute-start(bf16[2,64,256]{2,1,0:T(8,128)(2,1)S(1)} %divide_convert_fusion.refs_16_), channel_id=1, source_target_pairs={{0,1},{1,2},{2,3},{3,0},{4,5},{5,6},{6,7},{7,4},{8,9},{9,10},{10,1... | collective-permute-start | bytes 196616 | tf_op jit(solution)/shard_map/ppermute | solution.py:274
  95.7 4.9 %copy-start.13 = (bf16[4,64,256]{2,1,0:T(8,128)(2,1)}, bf16[4,64,256]{2,1,0:T(8,128)(2,1)S(1)}, u32[]{:S(2)}) copy-start(bf16[4,64,256]{2,1,0:T(8,128)(2,1)S(1)} %collective-permute-done.20.refs_13_) | copy-start | bytes 393220
  95.7 4.9 %copy-start.6 = (bf16[256,1536]{1,0:T(8,128)(2,1)}, bf16[256,1536]{1,0:T(8,128)(2,1)S(1)}, u32[]{:S(2)}) copy-start(bf16[256,1536]{1,0:T(8,128)(2,1)S(1)} %collective-permute-done.19.refs_7_) | copy-start | bytes 2359300
  95.7 4.9 %copy-start.20 = (bf16[2,64,256]{2,1,0:T(8,128)(2,1)}, bf16[2,64,256]{2,1,0:T(8,128)(2,1)S(1)}, u32[]{:S(2)}) copy-start(bf16[2,64,256]{2,1,0:T(8,128)(2,1)S(1)} %collective-permute-done.28.refs_19_) | copy-start | bytes 196612
  99.2 1.5 %copy-start.21 = (bf16[2,64,256]{2,1,0:T(8,128)(2,1)}, bf16[2,64,256]{2,1,0:T(8,128)(2,1)S(1)}, u32[]{:S(2)}) copy-start(bf16[2,64,256]{2,1,0:T(8,128)(2,1)S(1)} %collective-permute-done.27.refs_18_) | copy-start | bytes 196612
  100.6 0.6 copy-start.22

commit v2 on v1

--- a/solution.py
+++ b/solution.py
@@ -86,7 +86,9 @@
 
     anywhere = pl.BlockSpec(memory_space=pl.ANY)
     out_specs = [pl.BlockSpec(memory_space=pltpu.VMEM)] * count
-    out_shape = [jax.ShapeDtypeStruct((width, depth), blocks.dtype)] * count
+    near = count * width * depth * blocks.dtype.itemsize <= 4 * 1024 * 1024
+    place = pltpu.VMEM if near else jax.ShapeDtypeStruct
+    out_shape = [place((width, depth), blocks.dtype)] * count
     if plan is None:
         out_specs.append(pl.BlockSpec(memory_space=pltpu.SMEM))
         out_shape.append(jax.ShapeDtypeStruct((2 + 3 * len(rows),), jnp.int32))
@@ -107,38 +109,20 @@
 
 
 def kernel_parts(own, far, shards, sent):
-    width, depth = own[0].shape
+    width = own[0].shape[0]
     rows = width // shards
-    pairs = len(own)
-    arrived = [block for block in far if block is not None]
-
-    def body(*refs):
-        owns, others = refs[:pairs], list(refs[pairs : pairs + len(arrived)])
-        outs, full = refs[pairs + len(arrived) : -1], refs[-1]
-        turn = lax.axis_index("aux").astype(jnp.int32)
-        for pair in range(pairs):
-            other = owns[pair] if far[pair] is None else others.pop(0)
-            full[...] = lax.dot_general(
-                owns[pair][...],
-                other[...],
-                (((1,), (1,)), ((), ())),
-                preferred_element_type=jnp.float32,
-            )
-            for j in range(shards):
-                start = pl.multiple_of(lax.rem(turn + j, shards) * rows, rows)
-                outs[j][pair] = full[pl.ds(start, rows), :].astype(outs[j].dtype)
-
-    return pl.pallas_call(
-        body,
-        out_shape=[
-            jax.ShapeDtypeStruct((pairs, rows, width), sent if j else jnp.float32)
-            for j in range(shards)
-        ],
-        scratch_shapes=[pltpu.VMEM((width, width), jnp.float32)],
-        compiler_params=PARAMS,
-        cost_estimate=SMALL,
-        name="kernel_parts",
-    )(*own, *arrived)
+    turn = lax.axis_index("aux").astype(jnp.int32)
+    kernels = []
+    for mine, other in zip(own, far):
+        other = mine if other is None else other
+        kernels.append(jnp.einsum("ap,bp->ab", mine, other, preferred_element_type=jnp.float32))
+    stacked = jnp.stack(kernels)
+    parts = []
+    for j in range(shards):
+        start = lax.rem(turn + j, shards) * rows
+        part = lax.dynamic_slice_in_dim(stacked, start, rows, 1)
+        parts.append(part.astype(sent) if j else part)
+    return parts
 
 
 def denominators(excitation, plan, column_groups, shards, local_count):
@@ -197,7 +181,7 @@
 def accumulate(blocks, before, items, groups, plan, shards, kind):
     local_count, width, depth = blocks.shape
     pairs = len(items)
-    step = 512 if depth % 512 == 0 and pairs < 16 else 256
+    step = 768 if depth % 768 == 0 and pairs < 16 else 256
     arrived = [item[0] for item in items if item[0] is not None]
     local = len(arrived) < pairs
     flat = [shard for group in groups for shard in group]
@@ -335,14 +319,14 @@
         while len(received) < len(moves) - 1:
             move()
         amplitude = amplitudes(held, energies[2 + number])
-        if number == 0:
-            move(amplitude)
         for place, column in enumerate(columns):
             items.append((far[place], column, 1 + number, len(waiting) + place, False))
         group = jnp.concatenate([*waiting, amplitude])
         groups.append(spread(group))
+        if number == 0:
+            move(amplitude)
         waiting = []
-        gates = [group]
+        gates = [group, *groups[-1][1:3]]
     items[3] = (received[-1], *items[3][1:])
     items = items[:3] + items[4:] + [items[3]]
     return accumulate(blocks, None, items, groups, plan, shards, jnp.bfloat16)

time: 111 us -> 107 us (0.964); the launches traced: 109 us -> 106 us
  starting transfers between devices: 43.8 us -> 62.8 us
  Pallas kernels: 30.9 us -> 15.6 us
  waiting for transfers between devices: 27.5 us -> 18.7 us
  matrix products: 0 us -> 5.1 us
  other arithmetic: 3.77 us -> 2.15 us
    ppermute x21, starting transfers between devices: 28.5 us -> 42 us  [around(): lax.ppermute(array, 'aux', [(i, (i + shift) % shards) for i in range(shar...]
    pallas_call x4 -> x0, Pallas kernels: 12.1 us -> none  [kernel_parts(): pl.pallas_call(body, out_shape=[jax.ShapeDtypeStruct((pairs, rows, width)...]
    ppermute x21, waiting for transfers between devices: 24.2 us -> 12.5 us  [around(): lax.ppermute(array, 'aux', [(i, (i + shift) % shards) for i in range(shar...]
    ppermute x8, starting transfers between devices: 15.3 us -> 20.8 us  [send(): return lax.ppermute(array, 'orb', list(enumerate(step)))]
    dot_general x0 -> x7, matrix products: none -> 5.1 us  [kernel_parts(): jnp.einsum('ap,bp->ab', mine, other, preferred_element_type=jnp.float32)]
    ppermute x8, waiting for transfers between devices: 3.39 us -> 6.28 us  [send(): return lax.ppermute(array, 'orb', list(enumerate(step)))]
    pallas_call x2, Pallas kernels: 8.69 us -> 6.13 us  [pick(): pl.pallas_call(body, grid_spec=pltpu.PrefetchScalarGridSpec(num_scalar_pr...]
    convert_element_type x4, other arithmetic: 3.75 us -> 1.27 us  [amplitudes(): return (-kernel / denominator).astype(jnp.bfloat16)]
  transfers between devices with their start and end apart: 29 -> 29, of which waited for: 14 -> 12; matrix products, arithmetic and copies ran while one was open for 3% -> 7% of each run, Pallas kernels for 17% -> 5%
where the time goes in v2:
time: 107 us; the launch traced here: 106 us
  starting transfers between devices  62.8 us (59%)
  waiting for transfers between devices  18.7 us (17%)
  Pallas kernels  15.6 us (15%)
  matrix products  5.1 us (5%)
  other arithmetic  2.15 us (2%)
  local copies, waits for them, and re-layouts  1.61 us (2%)
    ppermute x21, starting transfers between devices, around(): lax.ppermute(array, 'aux', [(i, (i + shift) % shards) for i in range(shar...  42 us
    ppermute x8, starting transfers between devices, send(): return lax.ppermute(array, 'orb', list(enumerate(step)))  20.8 us
    ppermute x21, waiting for transfers between devices, around(): lax.ppermute(array, 'aux', [(i, (i + shift) % shards) for i in range(shar...  12.5 us
    pallas_call x1, Pallas kernels, accumulate(): pl.pallas_call(body, grid_spec=pltpu.PrefetchScalarGridSpec(num_scalar_pr...  7.11 us
    ppermute x8, waiting for transfers between devices, send(): return lax.ppermute(array, 'orb', list(enumerate(step)))  6.28 us
    pallas_call x2, Pallas kernels, pick(): pl.pallas_call(body, grid_spec=pltpu.PrefetchScalarGridSpec(num_scalar_pr...  6.13 us
    dot_general x7, matrix products, kernel_parts(): jnp.einsum('ap,bp->ab', mine, other, preferred_element_type=jnp.float32)  5.1 us
    pallas_call x1, Pallas kernels, denominators(): pl.pallas_call(body, grid_spec=pltpu.PrefetchScalarGridSpec(num_scalar_pr...  2.39 us
  transfers between devices with their start and end apart: 29, of which 12 were waited for; matrix products, arithmetic and copies ran while one was open for 7% of the time, Pallas kernels for 5%

profile of v2, /device:TPU:1, one launch (start us, length us, event | category | flops | bytes accessed | tf_op | source)
XLA Modules:
  0.0 106.5 jit_solution(13050240382113161544)
XLA Ops:
  0.0 3.6 %pick.2 = (bf16[256,1536]{1,0:T(8,128)(2,1)S(1)}, bf16[256,1536]{1,0:T(8,128)(2,1)}, bf16[256,1536]{1,0:T(8,128)(2,1)S(1)}, bf16[256,1536]{1,0:T(8,128)(2,1)S(1)}, s32[26]{0:T(128)}) custom-call(s32[8,8]{1,0:T(8,128)} %refs_0_.2, s32[8,8]{1,0:T(8,128)} %refs_1_.2, bf16[4,256,1536]{2,1,0:T(8,128)(2,1)} %refs_0_.3), custom_call_target="tpu_custom_call" | custom-call | flops 1 | bytes 1 | tf_op jit(solution)/shard_map/pick/pallas_call | solution.py:96
  3.6 0.1 collective-permute-start
  3.7 3.6 %collective-permute-start.1 = (bf16[256,1536]{1,0:T(8,128)(2,1)}, bf16[256,1536]{1,0:T(8,128)(2,1)}, u32[]{:S(2)}, u32[]{:S(2)}) collective-permute-start(bf16[256,1536]{1,0:T(8,128)(2,1)} %get-tuple-element.30), channel_id=1, source_target_pairs={{0,24},{4,28},{8,16},{12,20},{16,12},{20,8},{24,4},{28,0},{1,25},{... | collective-permute-start | bytes 2359304 | tf_op jit(solution)/shard_map/ppermute | solution.py:261
  7.3 0.4 convolution_bitcast_fusion.5
  7.7 0.0 collective-permute-done.refs_1_
  7.8 0.4 convolution_bitcast_fusion.4
  8.2 0.8 fusion.31
  9.0 1.3 %collective-permute-start.3 = (f32[2,64,256]{2,1,0:T(8,128)}, f32[2,64,256]{2,1,0:T(8,128)}, u32[]{:S(2)}, u32[]{:S(2)}) collective-permute-start(f32[2,64,256]{2,1,0:T(8,128)} %get-tuple-element.57), channel_id=1, source_target_pairs={{0,1},{1,2},{2,3},{3,0},{4,5},{5,6},{6,7},{7,4},{8,9},{9,10},{10,1... | collective-permute-start | bytes 393224 | tf_op jit(solution)/shard_map/ppermute | solution.py:258
  10.3 2.3 %collective-permute-start.4 = (f32[2,64,256]{2,1,0:T(8,128)}, f32[2,64,256]{2,1,0:T(8,128)}, u32[]{:S(2)}, u32[]{:S(2)}) collective-permute-start(f32[2,64,256]{2,1,0:T(8,128)} %get-tuple-element.58), channel_id=1, source_target_pairs={{0,2},{1,3},{2,0},{3,1},{4,6},{5,7},{6,4},{7,5},{8,10},{9,11},{10,... | collective-permute-start | bytes 393224 | tf_op jit(solution)/shard_map/ppermute | solution.py:258
  12.6 1.1 %collective-permute-start.5 = (f32[2,64,256]{2,1,0:T(8,128)S(1)}, f32[2,64,256]{2,1,0:T(8,128)}, u32[]{:S(2)}, u32[]{:S(2)}) collective-permute-start(f32[2,64,256]{2,1,0:T(8,128)S(1)} %get-tuple-element.59), channel_id=1, source_target_pairs={{0,3},{1,0},{2,1},{3,2},{4,7},{5,4},{6,5},{7,6},{8,11},{9,8},{10,9... | collective-permute-start | bytes 393224 | tf_op jit(solution)/shard_map/ppermute | solution.py:258
  13.7 1.7 %collective-permute-start.2 = (bf16[256,1536]{1,0:T(8,128)(2,1)S(1)}, bf16[256,1536]{1,0:T(8,128)(2,1)}, u32[]{:S(2)}, u32[]{:S(2)}) collective-permute-start(bf16[256,1536]{1,0:T(8,128)(2,1)S(1)} %get-tuple-element.31), channel_id=1, source_target_pairs={{0,12},{4,16},{8,4},{12,24},{16,28},{20,0},{24,20},{28,8},{1,13},{... | collective-permute-start | bytes 2359304 | tf_op jit(solution)/shard_map/ppermute | solution.py:261
  15.3 2.5 %pick.3 = (bf16[256,1536]{1,0:T(8,128)(2,1)S(1)}, bf16[256,1536]{1,0:T(8,128)(2,1)S(1)}, bf16[256,1536]{1,0:T(8,128)(2,1)S(1)}, bf16[256,1536]{1,0:T(8,128)(2,1)S(1)}) custom-call(s32[26]{0:T(128)} %get-tuple-element.28.plan.refs_0_, bf16[4,256,1536]{2,1,0:T(8,128)(2,1)} %refs_0_.3), custom_call_target="tpu_custom_call" | custom-call | flops 1 | bytes 1 | tf_op jit(solution)/shard_map/pick/pallas_call | solution.py:96
  17.9 0.9 copy-done
  18.8 2.4 %denominators.1 = (f32[2,64,256]{2,1,0:T(8,128)}, f32[1,64,256]{2,1,0:T(8,128)}, f32[2,64,256]{2,1,0:T(8,128)}, f32[2,64,256]{2,1,0:T(8,128)}) custom-call(s32[26]{0:T(128)} %get-tuple-element.28.plan.refs_0_, f32[32,256]{1,0:T(8,128)} %energies.1), custom_call_target="tpu_custom_call" | custom-call | flops 1 | bytes 1 | tf_op jit(solution)/shard_map/denominators/pallas_call | solution.py:147
  21.2 4.4 %collective-permute-done.1.refs_2_ = bf16[256,1536]{1,0:T(8,128)(2,1)} collective-permute-done((bf16[256,1536]{1,0:T(8,128)(2,1)}, bf16[256,1536]{1,0:T(8,128)(2,1)}, u32[]{:S(2)}, u32[]{:S(2)}) %collective-permute-start.1) | collective-permute-done | bytes 786464 | tf_op jit(solution)/shard_map/ppermute | solution.py:261
  25.6 0.0 collective-permute-done.3
  25.6 0.0 collective-permute-done.5
  25.6 1.2 %fusion.33.refs_8_ = bf16[2,64,256]{2,1,0:T(8,128)(2,1)S(1)} fusion(f32[2,64,256]{2,1,0:T(8,128)} %get-tuple-element.33, f32[2,64,256]{2,1,0:T(8,128)} %collective-permute-done.5, f32[2,64,256]{2,1,0:T(8,128)} %collective-permute-done.4, f32[2,64,256]{2,1,0:T(8,128)} %collective-permute-done.3, s32[]{:T(128)S(6)} %select_n.8, f32[1,256,256]{2,1,0:T(8,128)} %copy-done.6, ...), kind=kLoop, calls=%fused_computation.64 | loop fusion | flops 229376 | bytes 1114116 | tf_op jit(solution)/shard_map/convert_element_type | solution.py:166
  26.7 1.4 %collective-permute-start.12 = (bf16[256,1536]{1,0:T(8,128)(2,1)}, bf16[256,1536]{1,0:T(8,128)(2,1)S(1)}, u32[]{:S(2)}, u32[]{:S(2)}) collective-permute-start(bf16[256,1536]{1,0:T(8,128)(2,1)} %copy-done), channel_id=1, source_target_pairs={{0,20},{4,8},{8,28},{12,0},{16,4},{20,24},{24,12},{28,16},{1,21},{... | collective-permute-start | bytes 2359304 | tf_op jit(solution)/shard_map/ppermute | solution.py:261
  28.2 1.5 %fusion.44 = f32[256,256]{1,0:T(8,128)S(1)} fusion(bf16[256,1536]{1,0:T(8,128)(2,1)S(1)} %get-tuple-element.50, bf16[256,1536]{1,0:T(8,128)(2,1)} %collective-permute-done.1.refs_2_), kind=kOutput, calls=%fused_computation.79 | convolution fusion | flops 201326592 | bytes 1835008 | tf_op jit(solution)/shard_map/ap,bp->ab/dot_general | solution.py:118
  29.7 3.4 %collective-permute-start.8 = (bf16[1,64,256]{2,1,0:T(8,128)(2,1)S(1)}, bf16[1,64,256]{2,1,0:T(8,128)(2,1)S(1)}, u32[]{:S(2)}, u32[]{:S(2)}) collective-permute-start(bf16[1,64,256]{2,1,0:T(8,128)(2,1)S(1)} %get-tuple-element.60), channel_id=1, source_target_pairs={{0,3},{1,0},{2,1},{3,2},{4,7},{5,4},{6,5},{7,6},{8,11},{9,8},{10,9... | collective-permute-start | bytes 98312 | tf_op jit(solution)/shard_map/ppermute | solution.py:258
  33.1 0.0 collective-permute-start.7
  33.1 0.5 collective-permute-start.6
  33.5 0.6 collective-permute-done.8
  34.1 2.6 %collective-permute-done.7 = bf16[1,64,256]{2,1,0:T(8,128)(2,1)S(1)} collective-permute-done((bf16[1,64,256]{2,1,0:T(8,128)(2,1)S(1)}, bf16[1,64,256]{2,1,0:T(8,128)(2,1)S(1)}, u32[]{:S(2)}, u32[]{:S(2)}) %collective-permute-start.7) | collective-permute-done | bytes 32800 | tf_op jit(solution)/shard_map/ppermute | solution.py:258
  36.8 0.9 collective-permute-done.6
  37.7 0.8 collective-permute-start.11
  38.5 0.5 collective-permute-start.10
  38.9 1.5 %collective-permute-start.9 = (bf16[2,64,256]{2,1,0:T(8,128)(2,1)S(1)}, bf16[2,64,256]{2,1,0:T(8,128)(2,1)S(1)}, u32[]{:S(2)}, u32[]{:S(2)}) collective-permute-start(bf16[2,64,256]{2,1,0:T(8,128)(2,1)S(1)} %fusion.33.refs_8_), channel_id=1, source_target_pairs={{0,1},{1,2},{2,3},{3,0},{4,5},{5,6},{6,7},{7,4},{8,9},{9,10},{10,1... | collective-permute-start | bytes 196616 | tf_op jit(solution)/shard_map/ppermute | solution.py:258
  40.4 3.5 %collective-permute-start.13 = (bf16[1,64,256]{2,1,0:T(8,128)(2,1)S(1)}, bf16[1,64,256]{2,1,0:T(8,128)(2,1)S(1)}, u32[]{:S(2)}, u32[]{:S(2)}) collective-permute-start(bf16[1,64,256]{2,1,0:T(8,128)(2,1)S(1)} %fusion.40), channel_id=1, source_target_pairs={{0,28},{4,24},{8,20},{12,16},{16,8},{20,12},{24,0},{28,4},{1,29},{... | collective-permute-start | bytes 98312 | tf_op jit(solution)/shard_map/ppermute | solution.py:261
  44.0 1.0 collective-permute-done.13
  45.0 1.9 %collective-permute-start.14 = (bf16[256,1536]{1,0:T(8,128)(2,1)S(1)}, bf16[256,1536]{1,0:T(8,128)(2,1)S(1)}, u32[]{:S(2)}, u32[]{:S(2)}) collective-permute-start(bf16[256,1536]{1,0:T(8,128)(2,1)S(1)} %get-tuple-element.46), channel_id=1, source_target_pairs={{0,8},{4,20},{8,24},{12,4},{16,0},{20,28},{24,16},{28,12},{1,9},{5... | collective-permute-start | bytes 2359304 | tf_op jit(solution)/shard_map/ppermute | solution.py:261
  46.9 0.0 collective-permute-done.11.refs_11_
  46.9 0.0 collective-permute-done.10.refs_10_
  47.0 1.6 %convolution_bitcast_fusion.3 = f32[1,256,256]{2,1,0:T(8,128)S(1)} fusion(bf16[256,1536]{1,0:T(8,128)(2,1)S(1)} %copy-done.1, bf16[256,1536]{1,0:T(8,128)(2,1)} %collective-permute-done.2.refs_3_), kind=kOutput, calls=%fused_computation.3 | convolution fusion | flops 201326592 | bytes 1835008 | tf_op jit(solution)/shard_map/ap,bp->ab/dot_general | solution.py:118
  48.5 0.0 collective-permute-done.12.refs_4_
  48.6 0.1 collective-permute-start.20
  48.6 0.4 convolution_bitcast_fusion.2
  49.1 1.3 %collective-permute-start.15 = (bf16[2,64,256]{2,1,0:T(8,128)(2,1)S(1)}, bf16[2,64,256]{2,1,0:T(8,128)(2,1)S(1)}, u32[]{:S(2)}, u32[]{:S(2)}) collective-permute-start(bf16[2,64,256]{2,1,0:T(8,128)(2,1)S(1)} %get-tuple-element.54), channel_id=1, source_target_pairs={{0,1},{1,2},{2,3},{3,0},{4,5},{5,6},{6,7},{7,4},{8,9},{9,10},{10,1... | collective-permute-start | bytes 196616 | tf_op jit(solution)/shard_map/ppermute | solution.py:258
  50.4 1.1 collective-permute-start.16
  51.5 1.5 %collective-permute-start.17 = (bf16[2,64,256]{2,1,0:T(8,128)(2,1)S(1)}, bf16[2,64,256]{2,1,0:T(8,128)(2,1)S(1)}, u32[]{:S(2)}, u32[]{:S(2)}) collective-permute-start(bf16[2,64,256]{2,1,0:T(8,128)(2,1)S(1)} %get-tuple-element.56), channel_id=1, source_target_pairs={{0,3},{1,0},{2,1},{3,2},{4,7},{5,4},{6,5},{7,6},{8,11},{9,8},{10,9... | collective-permute-start | bytes 196616 | tf_op jit(solution)/shard_map/ppermute | solution.py:258
  53.0 1.1 %collective-permute-done.15 = bf16[2,64,256]{2,1,0:T(8,128)(2,1)S(1)} collective-permute-done((bf16[2,64,256]{2,1,0:T(8,128)(2,1)S(1)}, bf16[2,64,256]{2,1,0:T(8,128)(2,1)S(1)}, u32[]{:S(2)}, u32[]{:S(2)}) %collective-permute-start.15) | collective-permute-done | bytes 65568 | tf_op jit(solution)/shard_map/ppermute | solution.py:258
  54.1 1.3 %collective-permute-done.16 = bf16[2,64,256]{2,1,0:T(8,128)(2,1)S(1)} collective-permute-done((bf16[2,64,256]{2,1,0:T(8,128)(2,1)S(1)}, bf16[2,64,256]{2,1,0:T(8,128)(2,1)S(1)}, u32[]{:S(2)}, u32[]{:S(2)}) %collective-permute-start.16) | collective-permute-done | bytes 65568 | tf_op jit(solution)/shard_map/ppermute | solution.py:258
  55.6 0.8 collective-permute-start.19
  56.3 2.6 %collective-permute-start.18 = (bf16[4,64,256]{2,1,0:T(8,128)(2,1)S(1)}, bf16[4,64,256]{2,1,0:T(8,128)(2,1)S(1)}, u32[]{:S(2)}, u32[]{:S(2)}) collective-permute-start(bf16[4,64,256]{2,1,0:T(8,128)(2,1)S(1)} %pad_maximum_fusion.refs_12_), channel_id=1, source_target_pairs={{0,1},{1,2},{2,3},{3,0},{4,5},{5,6},{6,7},{7,4},{8,9},{9,10},{10,1... | collective-permute-start | bytes 393224 | tf_op jit(solution)/shard_map/ppermute | solution.py:258
  58.9 0.8 collective-permute-done.14.refs_5_
  59.8 8.5 %collective-permute-start.21 = (bf16[256,1536]{1,0:T(8,128)(2,1)S(1)}, bf16[256,1536]{1,0:T(8,128)(2,1)S(1)}, u32[]{:S(2)}, u32[]{:S(2)}) collective-permute-start(bf16[256,1536]{1,0:T(8,128)(2,1)S(1)} %get-tuple-element.50), channel_id=1, source_target_pairs={{0,28},{4,24},{8,20},{12,16},{16,8},{20,12},{24,0},{28,4},{1,29},{... | collective-permute-start | bytes 2359304 | tf_op jit(solution)/shard_map/ppermute | solution.py:261
  68.3 0.0 collective-permute-done.18.refs_13_
  68.3 0.4 convolution_bitcast_fusion.1
  68.7 0.0 collective-permute-done.20.refs_6_
  68.8 0.4 convolution_bitcast_fusion
  69.2 1.3 %collective-permute-start.23 = (bf16[2,64,256]{2,1,0:T(8,128)(2,1)S(1)}, bf16[2,64,256]{2,1,0:T(8,128)(2,1)S(1)}, u32[]{:S(2)}, u32[]{:S(2)}) collective-permute-start(bf16[2,64,256]{2,1,0:T(8,128)(2,1)S(1)} %get-tuple-element.51), channel_id=1, source_target_pairs={{0,1},{1,2},{2,3},{3,0},{4,5},{5,6},{6,7},{7,4},{8,9},{9,10},{10,1... | collective-permute-start | bytes 196616 | tf_op jit(solution)/shard_map/ppermute | solution.py:258
  70.5 15.9 %collective-permute-start.24 = (bf16[2,64,256]{2,1,0:T(8,128)(2,1)S(1)}, bf16[2,64,256]{2,1,0:T(8,128)(2,1)S(1)}, u32[]{:S(2)}, u32[]{:S(2)}) collective-permute-start(bf16[2,64,256]{2,1,0:T(8,128)(2,1)S(1)} %get-tuple-element.52), channel_id=1, source_target_pairs={{0,2},{1,3},{2,0},{3,1},{4,6},{5,7},{6,4},{7,5},{8,10},{9,11},{10,... | collective-permute-start | bytes 196616 | tf_op jit(solution)/shard_map/ppermute | solution.py:258
  86.4 2.3 %collective-permute-start.25 = (bf16[2,64,256]{2,1,0:T(8,128)(2,1)S(1)}, bf16[2,64,256]{2,1,0:T(8,128)(2,1)S(1)}, u32[]{:S(2)}, u32[]{:S(2)}) collective-permute-start(bf16[2,64,256]{2,1,0:T(8,128)(2,1)S(1)} %get-tuple-element.53), channel_id=1, source_target_pairs={{0,3},{1,0},{2,1},{3,2},{4,7},{5,4},{6,5},{7,6},{8,11},{9,8},{10,9... | collective-permute-start | bytes 196616 | tf_op jit(solution)/shard_map/ppermute | solution.py:258
  88.7 0.0 collective-permute-start.22
  88.7 0.0 collective-permute-done.24
  88.7 1.3 %collective-permute-done.25 = bf16[2,64,256]{2,1,0:T(8,128)(2,1)S(1)} collective-permute-done((bf16[2,64,256]{2,1,0:T(8,128)(2,1)S(1)}, bf16[2,64,256]{2,1,0:T(8,128)(2,1)S(1)}, u32[]{:S(2)}, u32[]{:S(2)}) %collective-permute-start.25) | collective-permute-done | bytes 65568 | tf_op jit(solution)/shard_map/ppermute | solution.py:258
  90.1 3.6 %collective-permute-start.28 = (bf16[2,64,256]{2,1,0:T(8,128)(2,1)S(1)}, bf16[2,64,256]{2,1,0:T(8,128)(2,1)S(1)}, u32[]{:S(2)}, u32[]{:S(2)}) collective-permute-start(bf16[2,64,256]{2,1,0:T(8,128)(2,1)S(1)} %fusion.35.refs_16_), channel_id=1, source_target_pairs={{0,3},{1,0},{2,1},{3,2},{4,7},{5,4},{6,5},{7,6},{8,11},{9,8},{10,9... | collective-permute-start | bytes 196616 | tf_op jit(solution)/shard_map/ppermute | solution.py:258
  93.7 0.4 collective-permute-start.26
  94.1 0.9 collective-permute-done.28.refs_19_
  95.0 2.7 %collective-permute-done.27.refs_18_ = bf16[2,64,256]{2,1,0:T(8,128)(2,1)S(1)} collective-permute-done((bf16[2,64,256]{2,1,0:T(8,128)(2,1)S(1)}, bf16[2,64,256]{2,1,0:T(8,128)(2,1)S(1)}, u32[]{:S(2)}, u32[]{:S(2)}) %collective-permute-start.27) | collective-permute-done | bytes 65568 | tf_op jit(solution)/shard_map/ppermute | solution.py:258
  97.7 0.9 collective-permute-done.26.refs_17_
  98.7 0.6 copy-done.21
  99.3 7.1 %accumulate.1 = bf16[4,256,1536]{2,1,0:T(8,128)(2,1)} custom-call(s32[26]{0:T(128)} %get-tuple-element.28.plan.refs_0_, bf16[4,256,1536]{2,1,0:T(8,128)(2,1)} %refs_0_.3, bf16[256,1536]{1,0:T(8,128)(2,1)} %copy-done.2, bf16[256,1536]{1,0:T(8,128)(2,1)} %collective-permute-done.1.refs_2_, bf16[256,1536]{1,0:T(8,128)(2,1)} %collective-permute-done.2.refs_3_, ...), custom_call_target="tpu_custom_call" | custom-call | flops 1 | bytes 1 | tf_op jit(solution)/shard_map/accumulate/pallas_call | solution.py:217
  (60 shorter events, 0.3 us)
Async XLA Ops:
  3.6 4.2 %collective-permute-start = (bf16[256,1536]{1,0:T(8,128)(2,1)S(1)}, bf16[256,1536]{1,0:T(8,128)(2,1)S(1)}, u32[]{:S(2)}, u32[]{:S(2)}) collective-permute-start(bf16[256,1536]{1,0:T(8,128)(2,1)S(1)} %get-tuple-element.29), channel_id=1, source_target_pairs={{0,4},{4,0},{8,12},{12,8},{16,20},{20,16},{24,28},{28,24},{1,5},{5... | collective-permute-start | bytes 2359304 | tf_op jit(solution)/shard_map/ppermute | solution.py:261
  3.7 21.8 %collective-permute-start.1 = (bf16[256,1536]{1,0:T(8,128)(2,1)}, bf16[256,1536]{1,0:T(8,128)(2,1)}, u32[]{:S(2)}, u32[]{:S(2)}) collective-permute-start(bf16[256,1536]{1,0:T(8,128)(2,1)} %get-tuple-element.30), channel_id=1, source_target_pairs={{0,24},{4,28},{8,16},{12,20},{16,12},{20,8},{24,4},{28,0},{1,25},{... | collective-permute-start | bytes 2359304 | tf_op jit(solution)/shard_map/ppermute | solution.py:261
  7.8 7.6 %copy-start.2 = (bf16[256,1536]{1,0:T(8,128)(2,1)}, bf16[256,1536]{1,0:T(8,128)(2,1)S(1)}, u32[]{:S(2)}) copy-start(bf16[256,1536]{1,0:T(8,128)(2,1)S(1)} %collective-permute-done.refs_1_) | copy-start | bytes 2359300
  8.2 7.1 %copy-start.6 = (f32[1,256,256]{2,1,0:T(8,128)}, f32[1,256,256]{2,1,0:T(8,128)S(1)}, u32[]{:S(2)}) copy-start(f32[1,256,256]{2,1,0:T(8,128)S(1)} %convolution_bitcast_fusion.4) | copy-start | bytes 786436
  9.0 16.6 %collective-permute-start.3 = (f32[2,64,256]{2,1,0:T(8,128)}, f32[2,64,256]{2,1,0:T(8,128)}, u32[]{:S(2)}, u32[]{:S(2)}) collective-permute-start(f32[2,64,256]{2,1,0:T(8,128)} %get-tuple-element.57), channel_id=1, source_target_pairs={{0,1},{1,2},{2,3},{3,0},{4,5},{5,6},{6,7},{7,4},{8,9},{9,10},{10,1... | collective-permute-start | bytes 393224 | tf_op jit(solution)/shard_map/ppermute | solution.py:258
  10.3 15.3 %collective-permute-start.4 = (f32[2,64,256]{2,1,0:T(8,128)}, f32[2,64,256]{2,1,0:T(8,128)}, u32[]{:S(2)}, u32[]{:S(2)}) collective-permute-start(f32[2,64,256]{2,1,0:T(8,128)} %get-tuple-element.58), channel_id=1, source_target_pairs={{0,2},{1,3},{2,0},{3,1},{4,6},{5,7},{6,4},{7,5},{8,10},{9,11},{10,... | collective-permute-start | bytes 393224 | tf_op jit(solution)/shard_map/ppermute | solution.py:258
  12.6 13.0 %collective-permute-start.5 = (f32[2,64,256]{2,1,0:T(8,128)S(1)}, f32[2,64,256]{2,1,0:T(8,128)}, u32[]{:S(2)}, u32[]{:S(2)}) collective-permute-start(f32[2,64,256]{2,1,0:T(8,128)S(1)} %get-tuple-element.59), channel_id=1, source_target_pairs={{0,3},{1,0},{2,1},{3,2},{4,7},{5,4},{6,5},{7,6},{8,11},{9,8},{10,9... | collective-permute-start | bytes 393224 | tf_op jit(solution)/shard_map/ppermute | solution.py:258
  13.7 26.8 %collective-permute-start.2 = (bf16[256,1536]{1,0:T(8,128)(2,1)S(1)}, bf16[256,1536]{1,0:T(8,128)(2,1)}, u32[]{:S(2)}, u32[]{:S(2)}) collective-permute-start(bf16[256,1536]{1,0:T(8,128)(2,1)S(1)} %get-tuple-element.31), channel_id=1, source_target_pairs={{0,12},{4,16},{8,4},{12,24},{16,28},{20,0},{24,20},{28,8},{1,13},{... | collective-permute-start | bytes 2359304 | tf_op jit(solution)/shard_map/ppermute | solution.py:261
  17.9 0.9 copy-start
  21.2 19.2 %copy-start.22 = (f32[1,64,256]{2,1,0:T(8,128)S(1)}, f32[1,64,256]{2,1,0:T(8,128)}, u32[]{:S(2)}) copy-start(f32[1,64,256]{2,1,0:T(8,128)} %get-tuple-element.35) | copy-start | bytes 196612
  21.2 25.8 %copy-start.1 = (bf16[256,1536]{1,0:T(8,128)(2,1)S(1)}, bf16[256,1536]{1,0:T(8,128)(2,1)}, u32[]{:S(2)}) copy-start(bf16[256,1536]{1,0:T(8,128)(2,1)} %copy-done) | copy-start | bytes 2359300
  26.7 22.4 %copy-start.9 = (bf16[2,64,256]{2,1,0:T(8,128)(2,1)}, bf16[2,64,256]{2,1,0:T(8,128)(2,1)S(1)}, u32[]{:S(2)}) copy-start(bf16[2,64,256]{2,1,0:T(8,128)(2,1)S(1)} %fusion.33.refs_8_) | copy-start | bytes 196612
  26.7 28.7 %copy-start.15 = (f32[2,64,256]{2,1,0:T(8,128)S(1)}, f32[2,64,256]{2,1,0:T(8,128)}, u32[]{:S(2)}) copy-start(f32[2,64,256]{2,1,0:T(8,128)} %get-tuple-element.36) | copy-start | bytes 393220
  26.7 21.8 %collective-permute-start.12 = (bf16[256,1536]{1,0:T(8,128)(2,1)}, bf16[256,1536]{1,0:T(8,128)(2,1)S(1)}, u32[]{:S(2)}, u32[]{:S(2)}) collective-permute-start(bf16[256,1536]{1,0:T(8,128)(2,1)} %copy-done), channel_id=1, source_target_pairs={{0,20},{4,8},{8,28},{12,0},{16,4},{20,24},{24,12},{28,16},{1,21},{... | collective-permute-start | bytes 2359304 | tf_op jit(solution)/shard_map/ppermute | solution.py:261
  29.7 4.4 %collective-permute-start.8 = (bf16[1,64,256]{2,1,0:T(8,128)(2,1)S(1)}, bf16[1,64,256]{2,1,0:T(8,128)(2,1)S(1)}, u32[]{:S(2)}, u32[]{:S(2)}) collective-permute-start(bf16[1,64,256]{2,1,0:T(8,128)(2,1)S(1)} %get-tuple-element.60), channel_id=1, source_target_pairs={{0,3},{1,0},{2,1},{3,2},{4,7},{5,4},{6,5},{7,6},{8,11},{9,8},{10,9... | collective-permute-start | bytes 98312 | tf_op jit(solution)/shard_map/ppermute | solution.py:258
  33.1 3.7 %collective-permute-start.7 = (bf16[1,64,256]{2,1,0:T(8,128)(2,1)S(1)}, bf16[1,64,256]{2,1,0:T(8,128)(2,1)S(1)}, u32[]{:S(2)}, u32[]{:S(2)}) collective-permute-start(bf16[1,64,256]{2,1,0:T(8,128)(2,1)S(1)} %get-tuple-element.61), channel_id=1, source_target_pairs={{0,2},{1,3},{2,0},{3,1},{4,6},{5,7},{6,4},{7,5},{8,10},{9,11},{10,... | collective-permute-start | bytes 98312 | tf_op jit(solution)/shard_map/ppermute | solution.py:258
  33.1 4.6 %collective-permute-start.6 = (bf16[1,64,256]{2,1,0:T(8,128)(2,1)S(1)}, bf16[1,64,256]{2,1,0:T(8,128)(2,1)S(1)}, u32[]{:S(2)}, u32[]{:S(2)}) collective-permute-start(bf16[1,64,256]{2,1,0:T(8,128)(2,1)S(1)} %get-tuple-element.62), channel_id=1, source_target_pairs={{0,1},{1,2},{2,3},{3,0},{4,5},{5,6},{6,7},{7,4},{8,9},{9,10},{10,1... | collective-permute-start | bytes 98312 | tf_op jit(solution)/shard_map/ppermute | solution.py:258
  37.7 9.2 %collective-permute-start.11 = (bf16[2,64,256]{2,1,0:T(8,128)(2,1)S(1)}, bf16[2,64,256]{2,1,0:T(8,128)(2,1)S(1)}, u32[]{:S(2)}, u32[]{:S(2)}) collective-permute-start(bf16[2,64,256]{2,1,0:T(8,128)(2,1)S(1)} %fusion.33.refs_8_), channel_id=1, source_target_pairs={{0,3},{1,0},{2,1},{3,2},{4,7},{5,4},{6,5},{7,6},{8,11},{9,8},{10,9... | collective-permute-start | bytes 196616 | tf_op jit(solution)/shard_map/ppermute | solution.py:258
  38.5 8.5 %collective-permute-start.10 = (bf16[2,64,256]{2,1,0:T(8,128)(2,1)S(1)}, bf16[2,64,256]{2,1,0:T(8,128)(2,1)S(1)}, u32[]{:S(2)}, u32[]{:S(2)}) collective-permute-start(bf16[2,64,256]{2,1,0:T(8,128)(2,1)S(1)} %fusion.33.refs_8_), channel_id=1, source_target_pairs={{0,2},{1,3},{2,0},{3,1},{4,6},{5,7},{6,4},{7,5},{8,10},{9,11},{10,... | collective-permute-start | bytes 196616 | tf_op jit(solution)/shard_map/ppermute | solution.py:258
  38.9 8.0 %collective-permute-start.9 = (bf16[2,64,256]{2,1,0:T(8,128)(2,1)S(1)}, bf16[2,64,256]{2,1,0:T(8,128)(2,1)S(1)}, u32[]{:S(2)}, u32[]{:S(2)}) collective-permute-start(bf16[2,64,256]{2,1,0:T(8,128)(2,1)S(1)} %fusion.33.refs_8_), channel_id=1, source_target_pairs={{0,1},{1,2},{2,3},{3,0},{4,5},{5,6},{6,7},{7,4},{8,9},{9,10},{10,1... | collective-permute-start | bytes 196616 | tf_op jit(solution)/shard_map/ppermute | solution.py:258
  40.4 4.6 %collective-permute-start.13 = (bf16[1,64,256]{2,1,0:T(8,128)(2,1)S(1)}, bf16[1,64,256]{2,1,0:T(8,128)(2,1)S(1)}, u32[]{:S(2)}, u32[]{:S(2)}) collective-permute-start(bf16[1,64,256]{2,1,0:T(8,128)(2,1)S(1)} %fusion.40), channel_id=1, source_target_pairs={{0,28},{4,24},{8,20},{12,16},{16,8},{20,12},{24,0},{28,4},{1,29},{... | collective-permute-start | bytes 98312 | tf_op jit(solution)/shard_map/ppermute | solution.py:261
  45.0 14.8 %collective-permute-start.14 = (bf16[256,1536]{1,0:T(8,128)(2,1)S(1)}, bf16[256,1536]{1,0:T(8,128)(2,1)S(1)}, u32[]{:S(2)}, u32[]{:S(2)}) collective-permute-start(bf16[256,1536]{1,0:T(8,128)(2,1)S(1)} %get-tuple-element.46), channel_id=1, source_target_pairs={{0,8},{4,20},{8,24},{12,4},{16,0},{20,28},{24,16},{28,12},{1,9},{5... | collective-permute-start | bytes 2359304 | tf_op jit(solution)/shard_map/ppermute | solution.py:261
  46.9 21.8 %copy-start.16 = (bf16[2,64,256]{2,1,0:T(8,128)(2,1)}, bf16[2,64,256]{2,1,0:T(8,128)(2,1)S(1)}, u32[]{:S(2)}) copy-start(bf16[2,64,256]{2,1,0:T(8,128)(2,1)S(1)} %collective-permute-done.11.refs_11_) | copy-start | bytes 196612
  46.9 21.8 %copy-start.17 = (bf16[2,64,256]{2,1,0:T(8,128)(2,1)}, bf16[2,64,256]{2,1,0:T(8,128)(2,1)S(1)}, u32[]{:S(2)}) copy-start(bf16[2,64,256]{2,1,0:T(8,128)(2,1)S(1)} %collective-permute-done.10.refs_10_) | copy-start | bytes 196612
  46.9 21.8 %copy-start.18 = (bf16[2,64,256]{2,1,0:T(8,128)(2,1)}, bf16[2,64,256]{2,1,0:T(8,128)(2,1)S(1)}, u32[]{:S(2)}) copy-start(bf16[2,64,256]{2,1,0:T(8,128)(2,1)S(1)} %collective-permute-done.9.refs_9_) | copy-start | bytes 196612
  48.5 20.6 %copy-start.3 = (bf16[256,1536]{1,0:T(8,128)(2,1)}, bf16[256,1536]{1,0:T(8,128)(2,1)S(1)}, u32[]{:S(2)}) copy-start(bf16[256,1536]{1,0:T(8,128)(2,1)S(1)} %collective-permute-done.12.refs_4_) | copy-start | bytes 2359300
  48.6 20.2 %collective-permute-start.20 = (bf16[256,1536]{1,0:T(8,128)(2,1)S(1)}, bf16[256,1536]{1,0:T(8,128)(2,1)S(1)}, u32[]{:S(2)}, u32[]{:S(2)}) collective-permute-start(bf16[256,1536]{1,0:T(8,128)(2,1)S(1)} %get-tuple-element.48), channel_id=1, source_target_pairs={{0,16},{4,12},{8,0},{12,28},{16,24},{20,4},{24,8},{28,20},{1,17},{... | collective-permute-start | bytes 2359304 | tf_op jit(solution)/shard_map/ppermute | solution.py:261
  49.0 41.0 %copy-start.14 = (f32[2,64,256]{2,1,0:T(8,128)S(1)}, f32[2,64,256]{2,1,0:T(8,128)}, u32[]{:S(2)}) copy-start(f32[2,64,256]{2,1,0:T(8,128)} %get-tuple-element.37) | copy-start | bytes 393220
  49.1 5.0 %collective-permute-start.15 = (bf16[2,64,256]{2,1,0:T(8,128)(2,1)S(1)}, bf16[2,64,256]{2,1,0:T(8,128)(2,1)S(1)}, u32[]{:S(2)}, u32[]{:S(2)}) collective-permute-start(bf16[2,64,256]{2,1,0:T(8,128)(2,1)S(1)} %get-tuple-element.54), channel_id=1, source_target_pairs={{0,1},{1,2},{2,3},{3,0},{4,5},{5,6},{6,7},{7,4},{8,9},{9,10},{10,1... | collective-permute-start | bytes 196616 | tf_op jit(solution)/shard_map/ppermute | solution.py:258
  50.4 5.1 %collective-permute-start.16 = (bf16[2,64,256]{2,1,0:T(8,128)(2,1)S(1)}, bf16[2,64,256]{2,1,0:T(8,128)(2,1)S(1)}, u32[]{:S(2)}, u32[]{:S(2)}) collective-permute-start(bf16[2,64,256]{2,1,0:T(8,128)(2,1)S(1)} %get-tuple-element.55), channel_id=1, source_target_pairs={{0,2},{1,3},{2,0},{3,1},{4,6},{5,7},{6,4},{7,5},{8,10},{9,11},{10,... | collective-permute-start | bytes 196616 | tf_op jit(solution)/shard_map/ppermute | solution.py:258
  51.5 4.0 %collective-permute-start.17 = (bf16[2,64,256]{2,1,0:T(8,128)(2,1)S(1)}, bf16[2,64,256]{2,1,0:T(8,128)(2,1)S(1)}, u32[]{:S(2)}, u32[]{:S(2)}) collective-permute-start(bf16[2,64,256]{2,1,0:T(8,128)(2,1)S(1)} %get-tuple-element.56), channel_id=1, source_target_pairs={{0,3},{1,0},{2,1},{3,2},{4,7},{5,4},{6,5},{7,6},{8,11},{9,8},{10,9... | collective-permute-start | bytes 196616 | tf_op jit(solution)/shard_map/ppermute | solution.py:258
  55.5 43.1 %copy-start.8 = (bf16[4,64,256]{2,1,0:T(8,128)(2,1)}, bf16[4,64,256]{2,1,0:T(8,128)(2,1)S(1)}, u32[]{:S(2)}) copy-start(bf16[4,64,256]{2,1,0:T(8,128)(2,1)S(1)} %pad_maximum_fusion.refs_12_) | copy-start | bytes 393220
  55.6 12.7 %collective-permute-start.19 = (bf16[4,64,256]{2,1,0:T(8,128)(2,1)S(1)}, bf16[4,64,256]{2,1,0:T(8,128)(2,1)S(1)}, u32[]{:S(2)}, u32[]{:S(2)}) collective-permute-start(bf16[4,64,256]{2,1,0:T(8,128)(2,1)S(1)} %pad_maximum_fusion.refs_12_), channel_id=1, source_target_pairs={{0,2},{1,3},{2,0},{3,1},{4,6},{5,7},{6,4},{7,5},{8,10},{9,11},{10,... | collective-permute-start | bytes 393224 | tf_op jit(solution)/shard_map/ppermute | solution.py:258
  56.3 12.0 %collective-permute-start.18 = (bf16[4,64,256]{2,1,0:T(8,128)(2,1)S(1)}, bf16[4,64,256]{2,1,0:T(8,128)(2,1)S(1)}, u32[]{:S(2)}, u32[]{:S(2)}) collective-permute-start(bf16[4,64,256]{2,1,0:T(8,128)(2,1)S(1)} %pad_maximum_fusion.refs_12_), channel_id=1, source_target_pairs={{0,1},{1,2},{2,3},{3,0},{4,5},{5,6},{6,7},{7,4},{8,9},{9,10},{10,1... | collective-permute-start | bytes 393224 | tf_op jit(solution)/shard_map/ppermute | solution.py:258
  59.8 38.8 %copy-start.4 = (bf16[256,1536]{1,0:T(8,128)(2,1)}, bf16[256,1536]{1,0:T(8,128)(2,1)S(1)}, u32[]{:S(2)}) copy-start(bf16[256,1536]{1,0:T(8,128)(2,1)S(1)} %collective-permute-done.14.refs_5_) | copy-start | bytes 2359300
  59.8 34.3 %collective-permute-start.21 = (bf16[256,1536]{1,0:T(8,128)(2,1)S(1)}, bf16[256,1536]{1,0:T(8,128)(2,1)S(1)}, u32[]{:S(2)}, u32[]{:S(2)}) collective-permute-start(bf16[256,1536]{1,0:T(8,128)(2,1)S(1)} %get-tuple-element.50), channel_id=1, source_target_pairs={{0,28},{4,24},{8,20},{12,16},{16,8},{20,12},{24,0},{28,4},{1,29},{... | collective-permute-start | bytes 2359304 | tf_op jit(solution)/shard_map/ppermute | solution.py:261
  68.3 30.3 %copy-start.11 = (bf16[4,64,256]{2,1,0:T(8,128)(2,1)}, bf16[4,64,256]{2,1,0:T(8,128)(2,1)S(1)}, u32[]{:S(2)}) copy-start(bf16[4,64,256]{2,1,0:T(8,128)(2,1)S(1)} %collective-permute-done.19.refs_14_) | copy-start | bytes 393220
  68.3 30.3 %copy-start.12 = (bf16[4,64,256]{2,1,0:T(8,128)(2,1)}, bf16[4,64,256]{2,1,0:T(8,128)(2,1)S(1)}, u32[]{:S(2)}) copy-start(bf16[4,64,256]{2,1,0:T(8,128)(2,1)S(1)} %collective-permute-done.18.refs_13_) | copy-start | bytes 393220
  68.8 29.9 %copy-start.5 = (bf16[256,1536]{1,0:T(8,128)(2,1)}, bf16[256,1536]{1,0:T(8,128)(2,1)S(1)}, u32[]{:S(2)}) copy-start(bf16[256,1536]{1,0:T(8,128)(2,1)S(1)} %collective-permute-done.20.refs_6_) | copy-start | bytes 2359300
  69.2 19.5 %collective-permute-start.23 = (bf16[2,64,256]{2,1,0:T(8,128)(2,1)S(1)}, bf16[2,64,256]{2,1,0:T(8,128)(2,1)S(1)}, u32[]{:S(2)}, u32[]{:S(2)}) collective-permute-start(bf16[2,64,256]{2,1,0:T(8,128)(2,1)S(1)} %get-tuple-element.51), channel_id=1, source_target_pairs={{0,1},{1,2},{2,3},{3,0},{4,5},{5,6},{6,7},{7,4},{8,9},{9,10},{10,1... | collective-permute-start | bytes 196616 | tf_op jit(solution)/shard_map/ppermute | solution.py:258
  70.5 18.2 %collective-permute-start.24 = (bf16[2,64,256]{2,1,0:T(8,128)(2,1)S(1)}, bf16[2,64,256]{2,1,0:T(8,128)(2,1)S(1)}, u32[]{:S(2)}, u32[]{:S(2)}) collective-permute-start(bf16[2,64,256]{2,1,0:T(8,128)(2,1)S(1)} %get-tuple-element.52), channel_id=1, source_target_pairs={{0,2},{1,3},{2,0},{3,1},{4,6},{5,7},{6,4},{7,5},{8,10},{9,11},{10,... | collective-permute-start | bytes 196616 | tf_op jit(solution)/shard_map/ppermute | solution.py:258
  86.4 3.6 %collective-permute-start.25 = (bf16[2,64,256]{2,1,0:T(8,128)(2,1)S(1)}, bf16[2,64,256]{2,1,0:T(8,128)(2,1)S(1)}, u32[]{:S(2)}, u32[]{:S(2)}) collective-permute-start(bf16[2,64,256]{2,1,0:T(8,128)(2,1)S(1)} %get-tuple-element.53), channel_id=1, source_target_pairs={{0,3},{1,0},{2,1},{3,2},{4,7},{5,4},{6,5},{7,6},{8,11},{9,8},{10,9... | collective-permute-start | bytes 196616 | tf_op jit(solution)/shard_map/ppermute | solution.py:258
  88.7 5.4 %collective-permute-start.22 = (bf16[4,64,256]{2,1,0:T(8,128)(2,1)S(1)}, bf16[4,64,256]{2,1,0:T(8,128)(2,1)S(1)}, u32[]{:S(2)}, u32[]{:S(2)}) collective-permute-start(bf16[4,64,256]{2,1,0:T(8,128)(2,1)S(1)} %pad_maximum_fusion.refs_12_), channel_id=1, source_target_pairs={{0,3},{1,0},{2,1},{3,2},{4,7},{5,4},{6,5},{7,6},{8,11},{9,8},{10,9... | collective-permute-start | bytes 393224 | tf_op jit(solution)/shard_map/ppermute | solution.py:258
  90.1 8.6 %copy-start.10 = (bf16[2,64,256]{2,1,0:T(8,128)(2,1)}, bf16[2,64,256]{2,1,0:T(8,128)(2,1)S(1)}, u32[]{:S(2)}) copy-start(bf16[2,64,256]{2,1,0:T(8,128)(2,1)S(1)} %fusion.35.refs_16_) | copy-start | bytes 196612
  90.1 5.0 %collective-permute-start.28 = (bf16[2,64,256]{2,1,0:T(8,128)(2,1)S(1)}, bf16[2,64,256]{2,1,0:T(8,128)(2,1)S(1)}, u32[]{:S(2)}, u32[]{:S(2)}) collective-permute-start(bf16[2,64,256]{2,1,0:T(8,128)(2,1)S(1)} %fusion.35.refs_16_), channel_id=1, source_target_pairs={{0,3},{1,0},{2,1},{3,2},{4,7},{5,4},{6,5},{7,6},{8,11},{9,8},{10,9... | collective-permute-start | bytes 196616 | tf_op jit(solution)/shard_map/ppermute | solution.py:258
  93.7 4.0 %collective-permute-start.27 = (bf16[2,64,256]{2,1,0:T(8,128)(2,1)S(1)}, bf16[2,64,256]{2,1,0:T(8,128)(2,1)S(1)}, u32[]{:S(2)}, u32[]{:S(2)}) collective-permute-start(bf16[2,64,256]{2,1,0:T(8,128)(2,1)S(1)} %fusion.35.refs_16_), channel_id=1, source_target_pairs={{0,2},{1,3},{2,0},{3,1},{4,6},{5,7},{6,4},{7,5},{8,10},{9,11},{10,... | collective-permute-start | bytes 196616 | tf_op jit(solution)/shard_map/ppermute | solution.py:258
  93.7 4.9 %collective-permute-start.26 = (bf16[2,64,256]{2,1,0:T(8,128)(2,1)S(1)}, bf16[2,64,256]{2,1,0:T(8,128)(2,1)S(1)}, u32[]{:S(2)}, u32[]{:S(2)}) collective-permute-start(bf16[2,64,256]{2,1,0:T(8,128)(2,1)S(1)} %fusion.35.refs_16_), channel_id=1, source_target_pairs={{0,1},{1,2},{2,3},{3,0},{4,5},{5,6},{6,7},{7,4},{8,9},{9,10},{10,1... | collective-permute-start | bytes 196616 | tf_op jit(solution)/shard_map/ppermute | solution.py:258
  94.1 4.6 %copy-start.13 = (bf16[4,64,256]{2,1,0:T(8,128)(2,1)}, bf16[4,64,256]{2,1,0:T(8,128)(2,1)S(1)}, u32[]{:S(2)}) copy-start(bf16[4,64,256]{2,1,0:T(8,128)(2,1)S(1)} %collective-permute-done.22.refs_15_) | copy-start | bytes 393220
  94.1 4.6 %copy-start.7 = (bf16[256,1536]{1,0:T(8,128)(2,1)}, bf16[256,1536]{1,0:T(8,128)(2,1)S(1)}, u32[]{:S(2)}) copy-start(bf16[256,1536]{1,0:T(8,128)(2,1)S(1)} %collective-permute-done.21.refs_7_) | copy-start | bytes 2359300
  95.0 3.6 %copy-start.19 = (bf16[2,64,256]{2,1,0:T(8,128)(2,1)}, bf16[2,64,256]{2,1,0:T(8,128)(2,1)S(1)}, u32[]{:S(2)}) copy-start(bf16[2,64,256]{2,1,0:T(8,128)(2,1)S(1)} %collective-permute-done.28.refs_19_) | copy-start | bytes 196612
  97.7 1.0 copy-start.20
  98.7 0.6 copy-start.21

commit v3 on v2

--- a/solution.py
+++ b/solution.py
@@ -324,7 +324,7 @@
         group = jnp.concatenate([*waiting, amplitude])
         groups.append(spread(group))
         if number == 0:
-            move(amplitude)
+            move(amplitude, received[-1])
         waiting = []
         gates = [group, *groups[-1][1:3]]
     items[3] = (received[-1], *items[3][1:])

time: 107 us -> 99.9 us (0.934); the launches traced: 106 us -> 98 us
  starting transfers between devices: 62.8 us -> 44.1 us
  waiting for transfers between devices: 18.7 us -> 28.2 us
    ppermute x21, starting transfers between devices: 42 us -> 27.7 us  [around(): lax.ppermute(array, 'aux', [(i, (i + shift) % shards) for i in range(shar...]
    ppermute x21, waiting for transfers between devices: 12.5 us -> 18.4 us  [around(): lax.ppermute(array, 'aux', [(i, (i + shift) % shards) for i in range(shar...]
    ppermute x8, starting transfers between devices: 20.8 us -> 16.4 us  [send(): return lax.ppermute(array, 'orb', list(enumerate(step)))]
    ppermute x8, waiting for transfers between devices: 6.28 us -> 9.86 us  [send(): return lax.ppermute(array, 'orb', list(enumerate(step)))]
  transfers between devices with their start and end apart: 29 -> 29, of which waited for: 12 -> 16; matrix products, arithmetic and copies ran while one was open for 7% -> 7% of each run, Pallas kernels for 5% -> 5%
where the time goes in v3:
time: 99.9 us; the launch traced here: 98 us
  starting transfers between devices  44.1 us (44%)
  waiting for transfers between devices  28.2 us (28%)
  Pallas kernels  15.6 us (16%)
  matrix products  5.09 us (5%)
  local copies, waits for them, and re-layouts  2.41 us (2%)
  other arithmetic  2.15 us (2%)
    ppermute x21, starting transfers between devices, around(): lax.ppermute(array, 'aux', [(i, (i + shift) % shards) for i in range(shar...  27.7 us
    ppermute x21, waiting for transfers between devices, around(): lax.ppermute(array, 'aux', [(i, (i + shift) % shards) for i in range(shar...  18.4 us
    ppermute x8, starting transfers between devices, send(): return lax.ppermute(array, 'orb', list(enumerate(step)))  16.4 us
    ppermute x8, waiting for transfers between devices, send(): return lax.ppermute(array, 'orb', list(enumerate(step)))  9.86 us
    pallas_call x1, Pallas kernels, accumulate(): pl.pallas_call(body, grid_spec=pltpu.PrefetchScalarGridSpec(num_scalar_pr...  7.12 us
    pallas_call x2, Pallas kernels, pick(): pl.pallas_call(body, grid_spec=pltpu.PrefetchScalarGridSpec(num_scalar_pr...  6.13 us
    dot_general x7, matrix products, kernel_parts(): jnp.einsum('ap,bp->ab', mine, other, preferred_element_type=jnp.float32)  5.09 us
    pallas_call x1, Pallas kernels, denominators(): pl.pallas_call(body, grid_spec=pltpu.PrefetchScalarGridSpec(num_scalar_pr...  2.39 us
  transfers between devices with their start and end apart: 29, of which 16 were waited for; matrix products, arithmetic and copies ran while one was open for 7% of the time, Pallas kernels for 5%

profile of v3, /device:TPU:1, one launch (start us, length us, event | category | flops | bytes accessed | tf_op | source)
XLA Modules:
  0.0 98.0 jit_solution(13898607740407285629)
XLA Ops:
  0.0 3.6 %pick.2 = (bf16[256,1536]{1,0:T(8,128)(2,1)S(1)}, bf16[256,1536]{1,0:T(8,128)(2,1)}, bf16[256,1536]{1,0:T(8,128)(2,1)S(1)}, bf16[256,1536]{1,0:T(8,128)(2,1)S(1)}, s32[26]{0:T(128)}) custom-call(s32[8,8]{1,0:T(8,128)} %refs_0_.2, s32[8,8]{1,0:T(8,128)} %refs_1_.2, bf16[4,256,1536]{2,1,0:T(8,128)(2,1)} %refs_0_.3), custom_call_target="tpu_custom_call" | custom-call | flops 1 | bytes 1 | tf_op jit(solution)/shard_map/pick/pallas_call | solution.py:96
  3.6 0.2 collective-permute-start
  3.8 3.7 %collective-permute-start.1 = (bf16[256,1536]{1,0:T(8,128)(2,1)}, bf16[256,1536]{1,0:T(8,128)(2,1)}, u32[]{:S(2)}, u32[]{:S(2)}) collective-permute-start(bf16[256,1536]{1,0:T(8,128)(2,1)} %get-tuple-element.30), channel_id=1, source_target_pairs={{0,24},{4,28},{8,16},{12,20},{16,12},{20,8},{24,4},{28,0},{1,25},{... | collective-permute-start | bytes 2359304 | tf_op jit(solution)/shard_map/ppermute | solution.py:261
  7.5 0.4 convolution_bitcast_fusion.5
  7.9 0.0 collective-permute-done.refs_1_
  7.9 0.4 convolution_bitcast_fusion.4
  8.3 0.8 fusion.31
  9.1 1.3 %collective-permute-start.3 = (f32[2,64,256]{2,1,0:T(8,128)}, f32[2,64,256]{2,1,0:T(8,128)}, u32[]{:S(2)}, u32[]{:S(2)}) collective-permute-start(f32[2,64,256]{2,1,0:T(8,128)} %get-tuple-element.57), channel_id=1, source_target_pairs={{0,1},{1,2},{2,3},{3,0},{4,5},{5,6},{6,7},{7,4},{8,9},{9,10},{10,1... | collective-permute-start | bytes 393224 | tf_op jit(solution)/shard_map/ppermute | solution.py:258
  10.4 2.3 %collective-permute-start.4 = (f32[2,64,256]{2,1,0:T(8,128)}, f32[2,64,256]{2,1,0:T(8,128)}, u32[]{:S(2)}, u32[]{:S(2)}) collective-permute-start(f32[2,64,256]{2,1,0:T(8,128)} %get-tuple-element.58), channel_id=1, source_target_pairs={{0,2},{1,3},{2,0},{3,1},{4,6},{5,7},{6,4},{7,5},{8,10},{9,11},{10,... | collective-permute-start | bytes 393224 | tf_op jit(solution)/shard_map/ppermute | solution.py:258
  12.7 1.1 %collective-permute-start.5 = (f32[2,64,256]{2,1,0:T(8,128)S(1)}, f32[2,64,256]{2,1,0:T(8,128)}, u32[]{:S(2)}, u32[]{:S(2)}) collective-permute-start(f32[2,64,256]{2,1,0:T(8,128)S(1)} %get-tuple-element.59), channel_id=1, source_target_pairs={{0,3},{1,0},{2,1},{3,2},{4,7},{5,4},{6,5},{7,6},{8,11},{9,8},{10,9... | collective-permute-start | bytes 393224 | tf_op jit(solution)/shard_map/ppermute | solution.py:258
  13.8 1.5 %collective-permute-start.2 = (bf16[256,1536]{1,0:T(8,128)(2,1)S(1)}, bf16[256,1536]{1,0:T(8,128)(2,1)}, u32[]{:S(2)}, u32[]{:S(2)}) collective-permute-start(bf16[256,1536]{1,0:T(8,128)(2,1)S(1)} %get-tuple-element.31), channel_id=1, source_target_pairs={{0,12},{4,16},{8,4},{12,24},{16,28},{20,0},{24,20},{28,8},{1,13},{... | collective-permute-start | bytes 2359304 | tf_op jit(solution)/shard_map/ppermute | solution.py:261
  15.3 2.5 %pick.3 = (bf16[256,1536]{1,0:T(8,128)(2,1)S(1)}, bf16[256,1536]{1,0:T(8,128)(2,1)S(1)}, bf16[256,1536]{1,0:T(8,128)(2,1)S(1)}, bf16[256,1536]{1,0:T(8,128)(2,1)S(1)}) custom-call(s32[26]{0:T(128)} %get-tuple-element.28.plan.refs_0_, bf16[4,256,1536]{2,1,0:T(8,128)(2,1)} %refs_0_.3), custom_call_target="tpu_custom_call" | custom-call | flops 1 | bytes 1 | tf_op jit(solution)/shard_map/pick/pallas_call | solution.py:96
  17.9 0.9 copy-done
  18.8 2.4 %denominators.1 = (f32[2,64,256]{2,1,0:T(8,128)}, f32[1,64,256]{2,1,0:T(8,128)}, f32[2,64,256]{2,1,0:T(8,128)}, f32[2,64,256]{2,1,0:T(8,128)}) custom-call(s32[26]{0:T(128)} %get-tuple-element.28.plan.refs_0_, f32[32,256]{1,0:T(8,128)} %energies.1), custom_call_target="tpu_custom_call" | custom-call | flops 1 | bytes 1 | tf_op jit(solution)/shard_map/denominators/pallas_call | solution.py:147
  21.2 4.5 %collective-permute-done.1.refs_2_ = bf16[256,1536]{1,0:T(8,128)(2,1)} collective-permute-done((bf16[256,1536]{1,0:T(8,128)(2,1)}, bf16[256,1536]{1,0:T(8,128)(2,1)}, u32[]{:S(2)}, u32[]{:S(2)}) %collective-permute-start.1) | collective-permute-done | bytes 786464 | tf_op jit(solution)/shard_map/ppermute | solution.py:261
  25.7 0.0 collective-permute-done.3
  25.7 0.0 collective-permute-done.4
  25.7 0.0 collective-permute-done.5
  25.7 1.2 %fusion.33.refs_8_ = bf16[2,64,256]{2,1,0:T(8,128)(2,1)S(1)} fusion(f32[2,64,256]{2,1,0:T(8,128)} %get-tuple-element.33, f32[2,64,256]{2,1,0:T(8,128)} %collective-permute-done.5, f32[2,64,256]{2,1,0:T(8,128)} %collective-permute-done.4, f32[2,64,256]{2,1,0:T(8,128)} %collective-permute-done.3, s32[]{:T(128)S(6)} %select_n.8, f32[1,256,256]{2,1,0:T(8,128)} %copy-done.6, ...), kind=kLoop, calls=%fused_computation.64 | loop fusion | flops 229376 | bytes 1114116 | tf_op jit(solution)/shard_map/convert_element_type | solution.py:166
  26.9 1.3 %collective-permute-start.12 = (bf16[256,1536]{1,0:T(8,128)(2,1)}, bf16[256,1536]{1,0:T(8,128)(2,1)S(1)}, u32[]{:S(2)}, u32[]{:S(2)}) collective-permute-start(bf16[256,1536]{1,0:T(8,128)(2,1)} %copy-done), channel_id=1, source_target_pairs={{0,20},{4,8},{8,28},{12,0},{16,4},{20,24},{24,12},{28,16},{1,21},{... | collective-permute-start | bytes 2359304 | tf_op jit(solution)/shard_map/ppermute | solution.py:261
  28.2 1.5 %fusion.44 = f32[256,256]{1,0:T(8,128)S(1)} fusion(bf16[256,1536]{1,0:T(8,128)(2,1)S(1)} %get-tuple-element.50, bf16[256,1536]{1,0:T(8,128)(2,1)} %collective-permute-done.1.refs_2_), kind=kOutput, calls=%fused_computation.79 | convolution fusion | flops 201326592 | bytes 1835008 | tf_op jit(solution)/shard_map/ap,bp->ab/dot_general | solution.py:118
  29.8 3.4 %collective-permute-start.8 = (bf16[1,64,256]{2,1,0:T(8,128)(2,1)S(1)}, bf16[1,64,256]{2,1,0:T(8,128)(2,1)S(1)}, u32[]{:S(2)}, u32[]{:S(2)}) collective-permute-start(bf16[1,64,256]{2,1,0:T(8,128)(2,1)S(1)} %get-tuple-element.60), channel_id=1, source_target_pairs={{0,3},{1,0},{2,1},{3,2},{4,7},{5,4},{6,5},{7,6},{8,11},{9,8},{10,9... | collective-permute-start | bytes 98312 | tf_op jit(solution)/shard_map/ppermute | solution.py:258
  33.2 0.0 collective-permute-start.7
  33.2 0.4 collective-permute-start.6
  33.6 0.6 collective-permute-done.8
  34.2 2.6 %collective-permute-done.7 = bf16[1,64,256]{2,1,0:T(8,128)(2,1)S(1)} collective-permute-done((bf16[1,64,256]{2,1,0:T(8,128)(2,1)S(1)}, bf16[1,64,256]{2,1,0:T(8,128)(2,1)S(1)}, u32[]{:S(2)}, u32[]{:S(2)}) %collective-permute-start.7) | collective-permute-done | bytes 32800 | tf_op jit(solution)/shard_map/ppermute | solution.py:258
  36.8 0.9 collective-permute-done.6
  37.8 0.9 collective-permute-start.11
  38.6 0.4 collective-permute-start.10
  39.0 1.5 %collective-permute-start.9 = (bf16[2,64,256]{2,1,0:T(8,128)(2,1)S(1)}, bf16[2,64,256]{2,1,0:T(8,128)(2,1)S(1)}, u32[]{:S(2)}, u32[]{:S(2)}) collective-permute-start(bf16[2,64,256]{2,1,0:T(8,128)(2,1)S(1)} %fusion.33.refs_8_), channel_id=1, source_target_pairs={{0,1},{1,2},{2,3},{3,0},{4,5},{5,6},{6,7},{7,4},{8,9},{9,10},{10,1... | collective-permute-start | bytes 196616 | tf_op jit(solution)/shard_map/ppermute | solution.py:258
  40.5 3.6 %collective-permute-start.13 = (bf16[1,64,256]{2,1,0:T(8,128)(2,1)S(1)}, bf16[1,64,256]{2,1,0:T(8,128)(2,1)S(1)}, u32[]{:S(2)}, u32[]{:S(2)}) collective-permute-start(bf16[1,64,256]{2,1,0:T(8,128)(2,1)S(1)} %fusion.40), channel_id=1, source_target_pairs={{0,28},{4,24},{8,20},{12,16},{16,8},{20,12},{24,0},{28,4},{1,29},{... | collective-permute-start | bytes 98312 | tf_op jit(solution)/shard_map/ppermute | solution.py:261
  44.1 1.0 %collective-permute-done.13 = bf16[1,64,256]{2,1,0:T(8,128)(2,1)S(1)} collective-permute-done((bf16[1,64,256]{2,1,0:T(8,128)(2,1)S(1)}, bf16[1,64,256]{2,1,0:T(8,128)(2,1)S(1)}, u32[]{:S(2)}, u32[]{:S(2)}) %collective-permute-start.13) | collective-permute-done | bytes 32800 | tf_op jit(solution)/shard_map/ppermute | solution.py:261
  45.1 1.8 %collective-permute-start.14 = (bf16[256,1536]{1,0:T(8,128)(2,1)S(1)}, bf16[256,1536]{1,0:T(8,128)(2,1)S(1)}, u32[]{:S(2)}, u32[]{:S(2)}) collective-permute-start(bf16[256,1536]{1,0:T(8,128)(2,1)S(1)} %get-tuple-element.46), channel_id=1, source_target_pairs={{0,8},{4,20},{8,24},{12,4},{16,0},{20,28},{24,16},{28,12},{1,9},{5... | collective-permute-start | bytes 2359304 | tf_op jit(solution)/shard_map/ppermute | solution.py:261
  47.0 1.6 %convolution_bitcast_fusion.3 = f32[1,256,256]{2,1,0:T(8,128)S(1)} fusion(bf16[256,1536]{1,0:T(8,128)(2,1)S(1)} %copy-done.1, bf16[256,1536]{1,0:T(8,128)(2,1)} %collective-permute-done.2.refs_3_), kind=kOutput, calls=%fused_computation.3 | convolution fusion | flops 201326592 | bytes 1835008 | tf_op jit(solution)/shard_map/ap,bp->ab/dot_general | solution.py:118
  48.6 0.1 collective-permute-start.20
  48.7 0.4 convolution_bitcast_fusion.2
  49.1 1.5 %collective-permute-start.15 = (bf16[2,64,256]{2,1,0:T(8,128)(2,1)S(1)}, bf16[2,64,256]{2,1,0:T(8,128)(2,1)S(1)}, u32[]{:S(2)}, u32[]{:S(2)}) collective-permute-start(bf16[2,64,256]{2,1,0:T(8,128)(2,1)S(1)} %get-tuple-element.54), channel_id=1, source_target_pairs={{0,1},{1,2},{2,3},{3,0},{4,5},{5,6},{6,7},{7,4},{8,9},{9,10},{10,1... | collective-permute-start | bytes 196616 | tf_op jit(solution)/shard_map/ppermute | solution.py:258
  50.6 1.0 collective-permute-start.16
  51.6 1.7 %collective-permute-start.17 = (bf16[2,64,256]{2,1,0:T(8,128)(2,1)S(1)}, bf16[2,64,256]{2,1,0:T(8,128)(2,1)S(1)}, u32[]{:S(2)}, u32[]{:S(2)}) collective-permute-start(bf16[2,64,256]{2,1,0:T(8,128)(2,1)S(1)} %get-tuple-element.56), channel_id=1, source_target_pairs={{0,3},{1,0},{2,1},{3,2},{4,7},{5,4},{6,5},{7,6},{8,11},{9,8},{10,9... | collective-permute-start | bytes 196616 | tf_op jit(solution)/shard_map/ppermute | solution.py:258
  53.3 0.8 collective-permute-done.15
  54.1 1.4 %collective-permute-done.16 = bf16[2,64,256]{2,1,0:T(8,128)(2,1)S(1)} collective-permute-done((bf16[2,64,256]{2,1,0:T(8,128)(2,1)S(1)}, bf16[2,64,256]{2,1,0:T(8,128)(2,1)S(1)}, u32[]{:S(2)}, u32[]{:S(2)}) %collective-permute-start.16) | collective-permute-done | bytes 65568 | tf_op jit(solution)/shard_map/ppermute | solution.py:258
  55.6 1.0 collective-permute-start.19
  56.6 2.6 %collective-permute-start.18 = (bf16[4,64,256]{2,1,0:T(8,128)(2,1)S(1)}, bf16[4,64,256]{2,1,0:T(8,128)(2,1)S(1)}, u32[]{:S(2)}, u32[]{:S(2)}) collective-permute-start(bf16[4,64,256]{2,1,0:T(8,128)(2,1)S(1)} %pad_maximum_fusion.refs_12_), channel_id=1, source_target_pairs={{0,1},{1,2},{2,3},{3,0},{4,5},{5,6},{6,7},{7,4},{8,9},{9,10},{10,1... | collective-permute-start | bytes 393224 | tf_op jit(solution)/shard_map/ppermute | solution.py:258
  59.2 0.7 collective-permute-done.14.refs_5_
  59.9 4.0 %collective-permute-done.19.refs_14_ = bf16[4,64,256]{2,1,0:T(8,128)(2,1)S(1)} collective-permute-done((bf16[4,64,256]{2,1,0:T(8,128)(2,1)S(1)}, bf16[4,64,256]{2,1,0:T(8,128)(2,1)S(1)}, u32[]{:S(2)}, u32[]{:S(2)}) %collective-permute-start.19) | collective-permute-done | bytes 131104 | tf_op jit(solution)/shard_map/ppermute | solution.py:258
  63.9 3.6 %collective-permute-done.20.refs_6_ = bf16[256,1536]{1,0:T(8,128)(2,1)S(1)} collective-permute-done((bf16[256,1536]{1,0:T(8,128)(2,1)S(1)}, bf16[256,1536]{1,0:T(8,128)(2,1)S(1)}, u32[]{:S(2)}, u32[]{:S(2)}) %collective-permute-start.20) | collective-permute-done | bytes 786464 | tf_op jit(solution)/shard_map/ppermute | solution.py:261
  67.4 4.1 %collective-permute-start.21 = (bf16[256,1536]{1,0:T(8,128)(2,1)S(1)}, bf16[256,1536]{1,0:T(8,128)(2,1)S(1)}, u32[]{:S(2)}, u32[]{:S(2)}) collective-permute-start(bf16[256,1536]{1,0:T(8,128)(2,1)S(1)} %get-tuple-element.50), channel_id=1, source_target_pairs={{0,28},{4,24},{8,20},{12,16},{16,8},{20,12},{24,0},{28,4},{1,29},{... | collective-permute-start | bytes 2359304 | tf_op jit(solution)/shard_map/ppermute | solution.py:261
  71.6 0.4 convolution_bitcast_fusion.1
  72.0 0.4 convolution_bitcast_fusion
  72.5 0.1 collective-permute-start.23
  72.5 0.6 collective-permute-start.24
  73.1 2.7 %collective-permute-start.25 = (bf16[2,64,256]{2,1,0:T(8,128)(2,1)S(1)}, bf16[2,64,256]{2,1,0:T(8,128)(2,1)S(1)}, u32[]{:S(2)}, u32[]{:S(2)}) collective-permute-start(bf16[2,64,256]{2,1,0:T(8,128)(2,1)S(1)} %get-tuple-element.53), channel_id=1, source_target_pairs={{0,3},{1,0},{2,1},{3,2},{4,7},{5,4},{6,5},{7,6},{8,11},{9,8},{10,9... | collective-permute-start | bytes 196616 | tf_op jit(solution)/shard_map/ppermute | solution.py:258
  75.8 0.4 collective-permute-start.22
  76.1 2.0 %collective-permute-done.23 = bf16[2,64,256]{2,1,0:T(8,128)(2,1)S(1)} collective-permute-done((bf16[2,64,256]{2,1,0:T(8,128)(2,1)S(1)}, bf16[2,64,256]{2,1,0:T(8,128)(2,1)S(1)}, u32[]{:S(2)}, u32[]{:S(2)}) %collective-permute-start.23) | collective-permute-done | bytes 65568 | tf_op jit(solution)/shard_map/ppermute | solution.py:258
  78.1 1.4 %collective-permute-done.24 = bf16[2,64,256]{2,1,0:T(8,128)(2,1)S(1)} collective-permute-done((bf16[2,64,256]{2,1,0:T(8,128)(2,1)S(1)}, bf16[2,64,256]{2,1,0:T(8,128)(2,1)S(1)}, u32[]{:S(2)}, u32[]{:S(2)}) %collective-permute-start.24) | collective-permute-done | bytes 65568 | tf_op jit(solution)/shard_map/ppermute | solution.py:258
  79.5 0.1 collective-permute-done.25
  79.7 4.8 %collective-permute-start.28 = (bf16[2,64,256]{2,1,0:T(8,128)(2,1)S(1)}, bf16[2,64,256]{2,1,0:T(8,128)(2,1)S(1)}, u32[]{:S(2)}, u32[]{:S(2)}) collective-permute-start(bf16[2,64,256]{2,1,0:T(8,128)(2,1)S(1)} %fusion.35.refs_16_), channel_id=1, source_target_pairs={{0,3},{1,0},{2,1},{3,2},{4,7},{5,4},{6,5},{7,6},{8,11},{9,8},{10,9... | collective-permute-start | bytes 196616 | tf_op jit(solution)/shard_map/ppermute | solution.py:258
  84.5 0.4 collective-permute-start.26
  84.8 1.0 collective-permute-done.28.refs_19_
  85.8 2.7 %collective-permute-done.27.refs_18_ = bf16[2,64,256]{2,1,0:T(8,128)(2,1)S(1)} collective-permute-done((bf16[2,64,256]{2,1,0:T(8,128)(2,1)S(1)}, bf16[2,64,256]{2,1,0:T(8,128)(2,1)S(1)}, u32[]{:S(2)}, u32[]{:S(2)}) %collective-permute-start.27) | collective-permute-done | bytes 65568 | tf_op jit(solution)/shard_map/ppermute | solution.py:258
  88.5 0.9 collective-permute-done.26.refs_17_
  89.5 0.5 copy-done.21
  90.0 0.9 copy-done.7
  90.9 7.1 %accumulate.1 = bf16[4,256,1536]{2,1,0:T(8,128)(2,1)} custom-call(s32[26]{0:T(128)} %get-tuple-element.28.plan.refs_0_, bf16[4,256,1536]{2,1,0:T(8,128)(2,1)} %refs_0_.3, bf16[256,1536]{1,0:T(8,128)(2,1)} %copy-done.2, bf16[256,1536]{1,0:T(8,128)(2,1)} %collective-permute-done.1.refs_2_, bf16[256,1536]{1,0:T(8,128)(2,1)} %collective-permute-done.2.refs_3_, ...), custom_call_target="tpu_custom_call" | custom-call | flops 1 | bytes 1 | tf_op jit(solution)/shard_map/accumulate/pallas_call | solution.py:217
  (60 shorter events, 0.3 us)
Async XLA Ops:
  3.6 4.3 %collective-permute-start = (bf16[256,1536]{1,0:T(8,128)(2,1)S(1)}, bf16[256,1536]{1,0:T(8,128)(2,1)S(1)}, u32[]{:S(2)}, u32[]{:S(2)}) collective-permute-start(bf16[256,1536]{1,0:T(8,128)(2,1)S(1)} %get-tuple-element.29), channel_id=1, source_target_pairs={{0,4},{4,0},{8,12},{12,8},{16,20},{20,16},{24,28},{28,24},{1,5},{5... | collective-permute-start | bytes 2359304 | tf_op jit(solution)/shard_map/ppermute | solution.py:261
  3.8 21.9 %collective-permute-start.1 = (bf16[256,1536]{1,0:T(8,128)(2,1)}, bf16[256,1536]{1,0:T(8,128)(2,1)}, u32[]{:S(2)}, u32[]{:S(2)}) collective-permute-start(bf16[256,1536]{1,0:T(8,128)(2,1)} %get-tuple-element.30), channel_id=1, source_target_pairs={{0,24},{4,28},{8,16},{12,20},{16,12},{20,8},{24,4},{28,0},{1,25},{... | collective-permute-start | bytes 2359304 | tf_op jit(solution)/shard_map/ppermute | solution.py:261
  7.9 7.4 %copy-start.2 = (bf16[256,1536]{1,0:T(8,128)(2,1)}, bf16[256,1536]{1,0:T(8,128)(2,1)S(1)}, u32[]{:S(2)}) copy-start(bf16[256,1536]{1,0:T(8,128)(2,1)S(1)} %collective-permute-done.refs_1_) | copy-start | bytes 2359300
  8.3 7.0 %copy-start.6 = (f32[1,256,256]{2,1,0:T(8,128)}, f32[1,256,256]{2,1,0:T(8,128)S(1)}, u32[]{:S(2)}) copy-start(f32[1,256,256]{2,1,0:T(8,128)S(1)} %convolution_bitcast_fusion.4) | copy-start | bytes 786436
  9.1 16.6 %collective-permute-start.3 = (f32[2,64,256]{2,1,0:T(8,128)}, f32[2,64,256]{2,1,0:T(8,128)}, u32[]{:S(2)}, u32[]{:S(2)}) collective-permute-start(f32[2,64,256]{2,1,0:T(8,128)} %get-tuple-element.57), channel_id=1, source_target_pairs={{0,1},{1,2},{2,3},{3,0},{4,5},{5,6},{6,7},{7,4},{8,9},{9,10},{10,1... | collective-permute-start | bytes 393224 | tf_op jit(solution)/shard_map/ppermute | solution.py:258
  10.4 15.3 %collective-permute-start.4 = (f32[2,64,256]{2,1,0:T(8,128)}, f32[2,64,256]{2,1,0:T(8,128)}, u32[]{:S(2)}, u32[]{:S(2)}) collective-permute-start(f32[2,64,256]{2,1,0:T(8,128)} %get-tuple-element.58), channel_id=1, source_target_pairs={{0,2},{1,3},{2,0},{3,1},{4,6},{5,7},{6,4},{7,5},{8,10},{9,11},{10,... | collective-permute-start | bytes 393224 | tf_op jit(solution)/shard_map/ppermute | solution.py:258
  12.7 13.0 %collective-permute-start.5 = (f32[2,64,256]{2,1,0:T(8,128)S(1)}, f32[2,64,256]{2,1,0:T(8,128)}, u32[]{:S(2)}, u32[]{:S(2)}) collective-permute-start(f32[2,64,256]{2,1,0:T(8,128)S(1)} %get-tuple-element.59), channel_id=1, source_target_pairs={{0,3},{1,0},{2,1},{3,2},{4,7},{5,4},{6,5},{7,6},{8,11},{9,8},{10,9... | collective-permute-start | bytes 393224 | tf_op jit(solution)/shard_map/ppermute | solution.py:258
  13.8 26.7 %collective-permute-start.2 = (bf16[256,1536]{1,0:T(8,128)(2,1)S(1)}, bf16[256,1536]{1,0:T(8,128)(2,1)}, u32[]{:S(2)}, u32[]{:S(2)}) collective-permute-start(bf16[256,1536]{1,0:T(8,128)(2,1)S(1)} %get-tuple-element.31), channel_id=1, source_target_pairs={{0,12},{4,16},{8,4},{12,24},{16,28},{20,0},{24,20},{28,8},{1,13},{... | collective-permute-start | bytes 2359304 | tf_op jit(solution)/shard_map/ppermute | solution.py:261
  17.9 0.9 copy-start
  21.2 19.3 %copy-start.22 = (f32[1,64,256]{2,1,0:T(8,128)S(1)}, f32[1,64,256]{2,1,0:T(8,128)}, u32[]{:S(2)}) copy-start(f32[1,64,256]{2,1,0:T(8,128)} %get-tuple-element.35) | copy-start | bytes 196612
  21.2 25.8 %copy-start.1 = (bf16[256,1536]{1,0:T(8,128)(2,1)S(1)}, bf16[256,1536]{1,0:T(8,128)(2,1)}, u32[]{:S(2)}) copy-start(bf16[256,1536]{1,0:T(8,128)(2,1)} %copy-done) | copy-start | bytes 2359300
  26.9 22.3 %copy-start.9 = (bf16[2,64,256]{2,1,0:T(8,128)(2,1)}, bf16[2,64,256]{2,1,0:T(8,128)(2,1)S(1)}, u32[]{:S(2)}) copy-start(bf16[2,64,256]{2,1,0:T(8,128)(2,1)S(1)} %fusion.33.refs_8_) | copy-start | bytes 196612
  26.9 28.6 %copy-start.15 = (f32[2,64,256]{2,1,0:T(8,128)S(1)}, f32[2,64,256]{2,1,0:T(8,128)}, u32[]{:S(2)}) copy-start(f32[2,64,256]{2,1,0:T(8,128)} %get-tuple-element.36) | copy-start | bytes 393220
  26.9 21.7 %collective-permute-start.12 = (bf16[256,1536]{1,0:T(8,128)(2,1)}, bf16[256,1536]{1,0:T(8,128)(2,1)S(1)}, u32[]{:S(2)}, u32[]{:S(2)}) collective-permute-start(bf16[256,1536]{1,0:T(8,128)(2,1)} %copy-done), channel_id=1, source_target_pairs={{0,20},{4,8},{8,28},{12,0},{16,4},{20,24},{24,12},{28,16},{1,21},{... | collective-permute-start | bytes 2359304 | tf_op jit(solution)/shard_map/ppermute | solution.py:261
  29.8 4.4 %collective-permute-start.8 = (bf16[1,64,256]{2,1,0:T(8,128)(2,1)S(1)}, bf16[1,64,256]{2,1,0:T(8,128)(2,1)S(1)}, u32[]{:S(2)}, u32[]{:S(2)}) collective-permute-start(bf16[1,64,256]{2,1,0:T(8,128)(2,1)S(1)} %get-tuple-element.60), channel_id=1, source_target_pairs={{0,3},{1,0},{2,1},{3,2},{4,7},{5,4},{6,5},{7,6},{8,11},{9,8},{10,9... | collective-permute-start | bytes 98312 | tf_op jit(solution)/shard_map/ppermute | solution.py:258
  33.2 3.7 %collective-permute-start.7 = (bf16[1,64,256]{2,1,0:T(8,128)(2,1)S(1)}, bf16[1,64,256]{2,1,0:T(8,128)(2,1)S(1)}, u32[]{:S(2)}, u32[]{:S(2)}) collective-permute-start(bf16[1,64,256]{2,1,0:T(8,128)(2,1)S(1)} %get-tuple-element.61), channel_id=1, source_target_pairs={{0,2},{1,3},{2,0},{3,1},{4,6},{5,7},{6,4},{7,5},{8,10},{9,11},{10,... | collective-permute-start | bytes 98312 | tf_op jit(solution)/shard_map/ppermute | solution.py:258
  33.2 4.6 %collective-permute-start.6 = (bf16[1,64,256]{2,1,0:T(8,128)(2,1)S(1)}, bf16[1,64,256]{2,1,0:T(8,128)(2,1)S(1)}, u32[]{:S(2)}, u32[]{:S(2)}) collective-permute-start(bf16[1,64,256]{2,1,0:T(8,128)(2,1)S(1)} %get-tuple-element.62), channel_id=1, source_target_pairs={{0,1},{1,2},{2,3},{3,0},{4,5},{5,6},{6,7},{7,4},{8,9},{9,10},{10,1... | collective-permute-start | bytes 98312 | tf_op jit(solution)/shard_map/ppermute | solution.py:258
  37.8 9.2 %collective-permute-start.11 = (bf16[2,64,256]{2,1,0:T(8,128)(2,1)S(1)}, bf16[2,64,256]{2,1,0:T(8,128)(2,1)S(1)}, u32[]{:S(2)}, u32[]{:S(2)}) collective-permute-start(bf16[2,64,256]{2,1,0:T(8,128)(2,1)S(1)} %fusion.33.refs_8_), channel_id=1, source_target_pairs={{0,3},{1,0},{2,1},{3,2},{4,7},{5,4},{6,5},{7,6},{8,11},{9,8},{10,9... | collective-permute-start | bytes 196616 | tf_op jit(solution)/shard_map/ppermute | solution.py:258
  38.6 8.3 %collective-permute-start.10 = (bf16[2,64,256]{2,1,0:T(8,128)(2,1)S(1)}, bf16[2,64,256]{2,1,0:T(8,128)(2,1)S(1)}, u32[]{:S(2)}, u32[]{:S(2)}) collective-permute-start(bf16[2,64,256]{2,1,0:T(8,128)(2,1)S(1)} %fusion.33.refs_8_), channel_id=1, source_target_pairs={{0,2},{1,3},{2,0},{3,1},{4,6},{5,7},{6,4},{7,5},{8,10},{9,11},{10,... | collective-permute-start | bytes 196616 | tf_op jit(solution)/shard_map/ppermute | solution.py:258
  39.0 8.0 %collective-permute-start.9 = (bf16[2,64,256]{2,1,0:T(8,128)(2,1)S(1)}, bf16[2,64,256]{2,1,0:T(8,128)(2,1)S(1)}, u32[]{:S(2)}, u32[]{:S(2)}) collective-permute-start(bf16[2,64,256]{2,1,0:T(8,128)(2,1)S(1)} %fusion.33.refs_8_), channel_id=1, source_target_pairs={{0,1},{1,2},{2,3},{3,0},{4,5},{5,6},{6,7},{7,4},{8,9},{9,10},{10,1... | collective-permute-start | bytes 196616 | tf_op jit(solution)/shard_map/ppermute | solution.py:258
  40.5 4.6 %collective-permute-start.13 = (bf16[1,64,256]{2,1,0:T(8,128)(2,1)S(1)}, bf16[1,64,256]{2,1,0:T(8,128)(2,1)S(1)}, u32[]{:S(2)}, u32[]{:S(2)}) collective-permute-start(bf16[1,64,256]{2,1,0:T(8,128)(2,1)S(1)} %fusion.40), channel_id=1, source_target_pairs={{0,28},{4,24},{8,20},{12,16},{16,8},{20,12},{24,0},{28,4},{1,29},{... | collective-permute-start | bytes 98312 | tf_op jit(solution)/shard_map/ppermute | solution.py:261
  45.1 14.8 %collective-permute-start.14 = (bf16[256,1536]{1,0:T(8,128)(2,1)S(1)}, bf16[256,1536]{1,0:T(8,128)(2,1)S(1)}, u32[]{:S(2)}, u32[]{:S(2)}) collective-permute-start(bf16[256,1536]{1,0:T(8,128)(2,1)S(1)} %get-tuple-element.46), channel_id=1, source_target_pairs={{0,8},{4,20},{8,24},{12,4},{16,0},{20,28},{24,16},{28,12},{1,9},{5... | collective-permute-start | bytes 2359304 | tf_op jit(solution)/shard_map/ppermute | solution.py:261
  47.0 25.0 %copy-start.16 = (bf16[2,64,256]{2,1,0:T(8,128)(2,1)}, bf16[2,64,256]{2,1,0:T(8,128)(2,1)S(1)}, u32[]{:S(2)}) copy-start(bf16[2,64,256]{2,1,0:T(8,128)(2,1)S(1)} %collective-permute-done.11.refs_11_) | copy-start | bytes 196612
  47.0 25.0 %copy-start.17 = (bf16[2,64,256]{2,1,0:T(8,128)(2,1)}, bf16[2,64,256]{2,1,0:T(8,128)(2,1)S(1)}, u32[]{:S(2)}) copy-start(bf16[2,64,256]{2,1,0:T(8,128)(2,1)S(1)} %collective-permute-done.10.refs_10_) | copy-start | bytes 196612
  47.0 25.0 %copy-start.18 = (bf16[2,64,256]{2,1,0:T(8,128)(2,1)}, bf16[2,64,256]{2,1,0:T(8,128)(2,1)S(1)}, u32[]{:S(2)}) copy-start(bf16[2,64,256]{2,1,0:T(8,128)(2,1)S(1)} %collective-permute-done.9.refs_9_) | copy-start | bytes 196612
  48.6 23.8 %copy-start.3 = (bf16[256,1536]{1,0:T(8,128)(2,1)}, bf16[256,1536]{1,0:T(8,128)(2,1)S(1)}, u32[]{:S(2)}) copy-start(bf16[256,1536]{1,0:T(8,128)(2,1)S(1)} %collective-permute-done.12.refs_4_) | copy-start | bytes 2359300
  48.6 18.8 %collective-permute-start.20 = (bf16[256,1536]{1,0:T(8,128)(2,1)S(1)}, bf16[256,1536]{1,0:T(8,128)(2,1)S(1)}, u32[]{:S(2)}, u32[]{:S(2)}) collective-permute-start(bf16[256,1536]{1,0:T(8,128)(2,1)S(1)} %get-tuple-element.48), channel_id=1, source_target_pairs={{0,16},{4,12},{8,0},{12,28},{16,24},{20,4},{24,8},{28,20},{1,17},{... | collective-permute-start | bytes 2359304 | tf_op jit(solution)/shard_map/ppermute | solution.py:261
  49.1 30.5 %copy-start.14 = (f32[2,64,256]{2,1,0:T(8,128)S(1)}, f32[2,64,256]{2,1,0:T(8,128)}, u32[]{:S(2)}) copy-start(f32[2,64,256]{2,1,0:T(8,128)} %get-tuple-element.37) | copy-start | bytes 393220
  49.1 5.0 %collective-permute-start.15 = (bf16[2,64,256]{2,1,0:T(8,128)(2,1)S(1)}, bf16[2,64,256]{2,1,0:T(8,128)(2,1)S(1)}, u32[]{:S(2)}, u32[]{:S(2)}) collective-permute-start(bf16[2,64,256]{2,1,0:T(8,128)(2,1)S(1)} %get-tuple-element.54), channel_id=1, source_target_pairs={{0,1},{1,2},{2,3},{3,0},{4,5},{5,6},{6,7},{7,4},{8,9},{9,10},{10,1... | collective-permute-start | bytes 196616 | tf_op jit(solution)/shard_map/ppermute | solution.py:258
  50.6 4.9 %collective-permute-start.16 = (bf16[2,64,256]{2,1,0:T(8,128)(2,1)S(1)}, bf16[2,64,256]{2,1,0:T(8,128)(2,1)S(1)}, u32[]{:S(2)}, u32[]{:S(2)}) collective-permute-start(bf16[2,64,256]{2,1,0:T(8,128)(2,1)S(1)} %get-tuple-element.55), channel_id=1, source_target_pairs={{0,2},{1,3},{2,0},{3,1},{4,6},{5,7},{6,4},{7,5},{8,10},{9,11},{10,... | collective-permute-start | bytes 196616 | tf_op jit(solution)/shard_map/ppermute | solution.py:258
  51.6 3.9 %collective-permute-start.17 = (bf16[2,64,256]{2,1,0:T(8,128)(2,1)S(1)}, bf16[2,64,256]{2,1,0:T(8,128)(2,1)S(1)}, u32[]{:S(2)}, u32[]{:S(2)}) collective-permute-start(bf16[2,64,256]{2,1,0:T(8,128)(2,1)S(1)} %get-tuple-element.56), channel_id=1, source_target_pairs={{0,3},{1,0},{2,1},{3,2},{4,7},{5,4},{6,5},{7,6},{8,11},{9,8},{10,9... | collective-permute-start | bytes 196616 | tf_op jit(solution)/shard_map/ppermute | solution.py:258
  55.6 33.8 %copy-start.8 = (bf16[4,64,256]{2,1,0:T(8,128)(2,1)}, bf16[4,64,256]{2,1,0:T(8,128)(2,1)S(1)}, u32[]{:S(2)}) copy-start(bf16[4,64,256]{2,1,0:T(8,128)(2,1)S(1)} %pad_maximum_fusion.refs_12_) | copy-start | bytes 393220
  55.6 8.3 %collective-permute-start.19 = (bf16[4,64,256]{2,1,0:T(8,128)(2,1)S(1)}, bf16[4,64,256]{2,1,0:T(8,128)(2,1)S(1)}, u32[]{:S(2)}, u32[]{:S(2)}) collective-permute-start(bf16[4,64,256]{2,1,0:T(8,128)(2,1)S(1)} %pad_maximum_fusion.refs_12_), channel_id=1, source_target_pairs={{0,2},{1,3},{2,0},{3,1},{4,6},{5,7},{6,4},{7,5},{8,10},{9,11},{10,... | collective-permute-start | bytes 393224 | tf_op jit(solution)/shard_map/ppermute | solution.py:258
  56.6 7.3 %collective-permute-start.18 = (bf16[4,64,256]{2,1,0:T(8,128)(2,1)S(1)}, bf16[4,64,256]{2,1,0:T(8,128)(2,1)S(1)}, u32[]{:S(2)}, u32[]{:S(2)}) collective-permute-start(bf16[4,64,256]{2,1,0:T(8,128)(2,1)S(1)} %pad_maximum_fusion.refs_12_), channel_id=1, source_target_pairs={{0,1},{1,2},{2,3},{3,0},{4,5},{5,6},{6,7},{7,4},{8,9},{9,10},{10,1... | collective-permute-start | bytes 393224 | tf_op jit(solution)/shard_map/ppermute | solution.py:258
  59.9 29.5 %copy-start.4 = (bf16[256,1536]{1,0:T(8,128)(2,1)}, bf16[256,1536]{1,0:T(8,128)(2,1)S(1)}, u32[]{:S(2)}) copy-start(bf16[256,1536]{1,0:T(8,128)(2,1)S(1)} %collective-permute-done.14.refs_5_) | copy-start | bytes 2359300
  63.9 25.6 %copy-start.11 = (bf16[4,64,256]{2,1,0:T(8,128)(2,1)}, bf16[4,64,256]{2,1,0:T(8,128)(2,1)S(1)}, u32[]{:S(2)}) copy-start(bf16[4,64,256]{2,1,0:T(8,128)(2,1)S(1)} %collective-permute-done.19.refs_14_) | copy-start | bytes 393220
  63.9 25.6 %copy-start.12 = (bf16[4,64,256]{2,1,0:T(8,128)(2,1)}, bf16[4,64,256]{2,1,0:T(8,128)(2,1)S(1)}, u32[]{:S(2)}) copy-start(bf16[4,64,256]{2,1,0:T(8,128)(2,1)S(1)} %collective-permute-done.18.refs_13_) | copy-start | bytes 393220
  67.4 22.0 %copy-start.5 = (bf16[256,1536]{1,0:T(8,128)(2,1)}, bf16[256,1536]{1,0:T(8,128)(2,1)S(1)}, u32[]{:S(2)}) copy-start(bf16[256,1536]{1,0:T(8,128)(2,1)S(1)} %collective-permute-done.20.refs_6_) | copy-start | bytes 2359300
  67.4 22.0 %collective-permute-start.21 = (bf16[256,1536]{1,0:T(8,128)(2,1)S(1)}, bf16[256,1536]{1,0:T(8,128)(2,1)S(1)}, u32[]{:S(2)}, u32[]{:S(2)}) collective-permute-start(bf16[256,1536]{1,0:T(8,128)(2,1)S(1)} %get-tuple-element.50), channel_id=1, source_target_pairs={{0,28},{4,24},{8,20},{12,16},{16,8},{20,12},{24,0},{28,4},{1,29},{... | collective-permute-start | bytes 2359304 | tf_op jit(solution)/shard_map/ppermute | solution.py:261
  72.5 5.6 %collective-permute-start.23 = (bf16[2,64,256]{2,1,0:T(8,128)(2,1)S(1)}, bf16[2,64,256]{2,1,0:T(8,128)(2,1)S(1)}, u32[]{:S(2)}, u32[]{:S(2)}) collective-permute-start(bf16[2,64,256]{2,1,0:T(8,128)(2,1)S(1)} %get-tuple-element.51), channel_id=1, source_target_pairs={{0,1},{1,2},{2,3},{3,0},{4,5},{5,6},{6,7},{7,4},{8,9},{9,10},{10,1... | collective-permute-start | bytes 196616 | tf_op jit(solution)/shard_map/ppermute | solution.py:258
  72.5 7.0 %collective-permute-start.24 = (bf16[2,64,256]{2,1,0:T(8,128)(2,1)S(1)}, bf16[2,64,256]{2,1,0:T(8,128)(2,1)S(1)}, u32[]{:S(2)}, u32[]{:S(2)}) collective-permute-start(bf16[2,64,256]{2,1,0:T(8,128)(2,1)S(1)} %get-tuple-element.52), channel_id=1, source_target_pairs={{0,2},{1,3},{2,0},{3,1},{4,6},{5,7},{6,4},{7,5},{8,10},{9,11},{10,... | collective-permute-start | bytes 196616 | tf_op jit(solution)/shard_map/ppermute | solution.py:258
  73.1 6.5 %collective-permute-start.25 = (bf16[2,64,256]{2,1,0:T(8,128)(2,1)S(1)}, bf16[2,64,256]{2,1,0:T(8,128)(2,1)S(1)}, u32[]{:S(2)}, u32[]{:S(2)}) collective-permute-start(bf16[2,64,256]{2,1,0:T(8,128)(2,1)S(1)} %get-tuple-element.53), channel_id=1, source_target_pairs={{0,3},{1,0},{2,1},{3,2},{4,7},{5,4},{6,5},{7,6},{8,11},{9,8},{10,9... | collective-permute-start | bytes 196616 | tf_op jit(solution)/shard_map/ppermute | solution.py:258
  75.8 9.1 %collective-permute-start.22 = (bf16[4,64,256]{2,1,0:T(8,128)(2,1)S(1)}, bf16[4,64,256]{2,1,0:T(8,128)(2,1)S(1)}, u32[]{:S(2)}, u32[]{:S(2)}) collective-permute-start(bf16[4,64,256]{2,1,0:T(8,128)(2,1)S(1)} %pad_maximum_fusion.refs_12_), channel_id=1, source_target_pairs={{0,3},{1,0},{2,1},{3,2},{4,7},{5,4},{6,5},{7,6},{8,11},{9,8},{10,9... | collective-permute-start | bytes 393224 | tf_op jit(solution)/shard_map/ppermute | solution.py:258
  79.7 9.8 %copy-start.10 = (bf16[2,64,256]{2,1,0:T(8,128)(2,1)}, bf16[2,64,256]{2,1,0:T(8,128)(2,1)S(1)}, u32[]{:S(2)}) copy-start(bf16[2,64,256]{2,1,0:T(8,128)(2,1)S(1)} %fusion.35.refs_16_) | copy-start | bytes 196612
  79.7 6.1 %collective-permute-start.28 = (bf16[2,64,256]{2,1,0:T(8,128)(2,1)S(1)}, bf16[2,64,256]{2,1,0:T(8,128)(2,1)S(1)}, u32[]{:S(2)}, u32[]{:S(2)}) collective-permute-start(bf16[2,64,256]{2,1,0:T(8,128)(2,1)S(1)} %fusion.35.refs_16_), channel_id=1, source_target_pairs={{0,3},{1,0},{2,1},{3,2},{4,7},{5,4},{6,5},{7,6},{8,11},{9,8},{10,9... | collective-permute-start | bytes 196616 | tf_op jit(solution)/shard_map/ppermute | solution.py:258
  84.5 4.0 %collective-permute-start.27 = (bf16[2,64,256]{2,1,0:T(8,128)(2,1)S(1)}, bf16[2,64,256]{2,1,0:T(8,128)(2,1)S(1)}, u32[]{:S(2)}, u32[]{:S(2)}) collective-permute-start(bf16[2,64,256]{2,1,0:T(8,128)(2,1)S(1)} %fusion.35.refs_16_), channel_id=1, source_target_pairs={{0,2},{1,3},{2,0},{3,1},{4,6},{5,7},{6,4},{7,5},{8,10},{9,11},{10,... | collective-permute-start | bytes 196616 | tf_op jit(solution)/shard_map/ppermute | solution.py:258
  84.5 4.9 %collective-permute-start.26 = (bf16[2,64,256]{2,1,0:T(8,128)(2,1)S(1)}, bf16[2,64,256]{2,1,0:T(8,128)(2,1)S(1)}, u32[]{:S(2)}, u32[]{:S(2)}) collective-permute-start(bf16[2,64,256]{2,1,0:T(8,128)(2,1)S(1)} %fusion.35.refs_16_), channel_id=1, source_target_pairs={{0,1},{1,2},{2,3},{3,0},{4,5},{5,6},{6,7},{7,4},{8,9},{9,10},{10,1... | collective-permute-start | bytes 196616 | tf_op jit(solution)/shard_map/ppermute | solution.py:258
  84.8 4.6 %copy-start.13 = (bf16[4,64,256]{2,1,0:T(8,128)(2,1)}, bf16[4,64,256]{2,1,0:T(8,128)(2,1)S(1)}, u32[]{:S(2)}) copy-start(bf16[4,64,256]{2,1,0:T(8,128)(2,1)S(1)} %collective-permute-done.22.refs_15_) | copy-start | bytes 393220
  85.8 3.7 %copy-start.19 = (bf16[2,64,256]{2,1,0:T(8,128)(2,1)}, bf16[2,64,256]{2,1,0:T(8,128)(2,1)S(1)}, u32[]{:S(2)}) copy-start(bf16[2,64,256]{2,1,0:T(8,128)(2,1)S(1)} %collective-permute-done.28.refs_19_) | copy-start | bytes 196612
  88.5 1.0 %copy-start.20 = (bf16[2,64,256]{2,1,0:T(8,128)(2,1)}, bf16[2,64,256]{2,1,0:T(8,128)(2,1)S(1)}, u32[]{:S(2)}) copy-start(bf16[2,64,256]{2,1,0:T(8,128)(2,1)S(1)} %collective-permute-done.27.refs_18_) | copy-start | bytes 196612
  89.4 0.6 copy-start.21
  90.0 0.9 copy-start.7

commit v4 on v3

--- a/solution.py
+++ b/solution.py
@@ -299,7 +299,7 @@
     parts, held = reduced([far], [from_step[0]], jnp.bfloat16)
     mine = amplitudes(held, energies[1])
     theirs = send(mine, backward[0])
-    groups = [spread(after(local, *held[1:]))]
+    groups = [spread(after(local, mine))]
     move(theirs)
     waiting = [mine, theirs]
     items = [

time: 99.9 us -> 97.7 us (0.978); the launches traced: 98 us -> 97.3 us
    ppermute x8, waiting for transfers between devices: 9.86 us -> 5.83 us  [send(): return lax.ppermute(array, 'orb', list(enumerate(step)))]
    ppermute x21, waiting for transfers between devices: 18.4 us -> 22.1 us  [around(): lax.ppermute(array, 'aux', [(i, (i + shift) % shards) for i in range(shar...]
    ppermute x8, starting transfers between devices: 16.4 us -> 14.7 us  [send(): return lax.ppermute(array, 'orb', list(enumerate(step)))]
    ppermute x21, starting transfers between devices: 27.7 us -> 29 us  [around(): lax.ppermute(array, 'aux', [(i, (i + shift) % shards) for i in range(shar...]
where the time goes in v4:
time: 97.7 us; the launch traced here: 97.3 us
  starting transfers between devices  43.7 us (45%)
  waiting for transfers between devices  27.9 us (29%)
  Pallas kernels  15.7 us (16%)
  matrix products  5.09 us (5%)
  local copies, waits for them, and re-layouts  2.41 us (2%)
  other arithmetic  2.15 us (2%)
    ppermute x21, starting transfers between devices, around(): lax.ppermute(array, 'aux', [(i, (i + shift) % shards) for i in range(shar...  29 us
    ppermute x21, waiting for transfers between devices, around(): lax.ppermute(array, 'aux', [(i, (i + shift) % shards) for i in range(shar...  22.1 us
    ppermute x8, starting transfers between devices, send(): return lax.ppermute(array, 'orb', list(enumerate(step)))  14.7 us
    pallas_call x1, Pallas kernels, accumulate(): pl.pallas_call(body, grid_spec=pltpu.PrefetchScalarGridSpec(num_scalar_pr...  7.11 us
    pallas_call x2, Pallas kernels, pick(): pl.pallas_call(body, grid_spec=pltpu.PrefetchScalarGridSpec(num_scalar_pr...  6.22 us
    ppermute x8, waiting for transfers between devices, send(): return lax.ppermute(array, 'orb', list(enumerate(step)))  5.83 us
    dot_general x7, matrix products, kernel_parts(): jnp.einsum('ap,bp->ab', mine, other, preferred_element_type=jnp.float32)  5.09 us
    pallas_call x1, Pallas kernels, denominators(): pl.pallas_call(body, grid_spec=pltpu.PrefetchScalarGridSpec(num_scalar_pr...  2.39 us
  transfers between devices with their start and end apart: 29, of which 16 were waited for; matrix products, arithmetic and copies ran while one was open for 7% of the time, Pallas kernels for 5%

profile of v4, /device:TPU:1, one launch (start us, length us, event | category | flops | bytes accessed | tf_op | source)
XLA Modules:
  0.0 97.3 jit_solution(17503146526350724269)
XLA Ops:
  0.0 3.7 %pick.2 = (bf16[256,1536]{1,0:T(8,128)(2,1)S(1)}, bf16[256,1536]{1,0:T(8,128)(2,1)}, bf16[256,1536]{1,0:T(8,128)(2,1)S(1)}, bf16[256,1536]{1,0:T(8,128)(2,1)S(1)}, s32[26]{0:T(128)}) custom-call(s32[8,8]{1,0:T(8,128)} %refs_0_.2, s32[8,8]{1,0:T(8,128)} %refs_1_.2, bf16[4,256,1536]{2,1,0:T(8,128)(2,1)} %refs_0_.3), custom_call_target="tpu_custom_call" | custom-call | flops 1 | bytes 1 | tf_op jit(solution)/shard_map/pick/pallas_call | solution.py:96
  3.7 0.1 collective-permute-start
  3.8 3.6 %collective-permute-start.1 = (bf16[256,1536]{1,0:T(8,128)(2,1)}, bf16[256,1536]{1,0:T(8,128)(2,1)}, u32[]{:S(2)}, u32[]{:S(2)}) collective-permute-start(bf16[256,1536]{1,0:T(8,128)(2,1)} %get-tuple-element.30), channel_id=1, source_target_pairs={{0,24},{4,28},{8,16},{12,20},{16,12},{20,8},{24,4},{28,0},{1,25},{... | collective-permute-start | bytes 2359304 | tf_op jit(solution)/shard_map/ppermute | solution.py:261
  7.3 0.4 convolution_bitcast_fusion.5
  7.7 0.0 collective-permute-done.refs_1_
  7.8 0.4 convolution_bitcast_fusion.4
  8.2 0.8 fusion.31
  9.0 1.3 %collective-permute-start.3 = (f32[2,64,256]{2,1,0:T(8,128)}, f32[2,64,256]{2,1,0:T(8,128)}, u32[]{:S(2)}, u32[]{:S(2)}) collective-permute-start(f32[2,64,256]{2,1,0:T(8,128)} %get-tuple-element.57), channel_id=1, source_target_pairs={{0,1},{1,2},{2,3},{3,0},{4,5},{5,6},{6,7},{7,4},{8,9},{9,10},{10,1... | collective-permute-start | bytes 393224 | tf_op jit(solution)/shard_map/ppermute | solution.py:258
  10.3 2.3 %collective-permute-start.4 = (f32[2,64,256]{2,1,0:T(8,128)}, f32[2,64,256]{2,1,0:T(8,128)}, u32[]{:S(2)}, u32[]{:S(2)}) collective-permute-start(f32[2,64,256]{2,1,0:T(8,128)} %get-tuple-element.58), channel_id=1, source_target_pairs={{0,2},{1,3},{2,0},{3,1},{4,6},{5,7},{6,4},{7,5},{8,10},{9,11},{10,... | collective-permute-start | bytes 393224 | tf_op jit(solution)/shard_map/ppermute | solution.py:258
  12.6 1.1 %collective-permute-start.5 = (f32[2,64,256]{2,1,0:T(8,128)S(1)}, f32[2,64,256]{2,1,0:T(8,128)}, u32[]{:S(2)}, u32[]{:S(2)}) collective-permute-start(f32[2,64,256]{2,1,0:T(8,128)S(1)} %get-tuple-element.59), channel_id=1, source_target_pairs={{0,3},{1,0},{2,1},{3,2},{4,7},{5,4},{6,5},{7,6},{8,11},{9,8},{10,9... | collective-permute-start | bytes 393224 | tf_op jit(solution)/shard_map/ppermute | solution.py:258
  13.7 1.7 %collective-permute-start.2 = (bf16[256,1536]{1,0:T(8,128)(2,1)S(1)}, bf16[256,1536]{1,0:T(8,128)(2,1)}, u32[]{:S(2)}, u32[]{:S(2)}) collective-permute-start(bf16[256,1536]{1,0:T(8,128)(2,1)S(1)} %get-tuple-element.31), channel_id=1, source_target_pairs={{0,12},{4,16},{8,4},{12,24},{16,28},{20,0},{24,20},{28,8},{1,13},{... | collective-permute-start | bytes 2359304 | tf_op jit(solution)/shard_map/ppermute | solution.py:261
  15.3 2.6 %pick.3 = (bf16[256,1536]{1,0:T(8,128)(2,1)S(1)}, bf16[256,1536]{1,0:T(8,128)(2,1)S(1)}, bf16[256,1536]{1,0:T(8,128)(2,1)S(1)}, bf16[256,1536]{1,0:T(8,128)(2,1)S(1)}) custom-call(s32[26]{0:T(128)} %get-tuple-element.28.plan.refs_0_, bf16[4,256,1536]{2,1,0:T(8,128)(2,1)} %refs_0_.3), custom_call_target="tpu_custom_call" | custom-call | flops 1 | bytes 1 | tf_op jit(solution)/shard_map/pick/pallas_call | solution.py:96
  17.9 0.9 copy-done
  18.8 2.4 %denominators.1 = (f32[2,64,256]{2,1,0:T(8,128)}, f32[1,64,256]{2,1,0:T(8,128)}, f32[2,64,256]{2,1,0:T(8,128)}, f32[2,64,256]{2,1,0:T(8,128)}) custom-call(s32[26]{0:T(128)} %get-tuple-element.28.plan.refs_0_, f32[32,256]{1,0:T(8,128)} %energies.1), custom_call_target="tpu_custom_call" | custom-call | flops 1 | bytes 1 | tf_op jit(solution)/shard_map/denominators/pallas_call | solution.py:147
  21.2 1.0 %collective-permute-done.4 = f32[2,64,256]{2,1,0:T(8,128)} collective-permute-done((f32[2,64,256]{2,1,0:T(8,128)}, f32[2,64,256]{2,1,0:T(8,128)}, u32[]{:S(2)}, u32[]{:S(2)}) %collective-permute-start.4) | collective-permute-done | bytes 131104 | tf_op jit(solution)/shard_map/ppermute | solution.py:258
  22.2 1.1 %fusion.33.refs_8_ = bf16[2,64,256]{2,1,0:T(8,128)(2,1)S(1)} fusion(f32[2,64,256]{2,1,0:T(8,128)} %get-tuple-element.33, f32[2,64,256]{2,1,0:T(8,128)} %collective-permute-done.5, f32[2,64,256]{2,1,0:T(8,128)} %collective-permute-done.4, f32[2,64,256]{2,1,0:T(8,128)} %collective-permute-done.3, s32[]{:T(128)S(6)} %select_n.8, f32[1,256,256]{2,1,0:T(8,128)} %copy-done.6, ...), kind=kLoop, calls=%fused_computation.64 | loop fusion | flops 229376 | bytes 1114116 | tf_op jit(solution)/shard_map/convert_element_type | solution.py:166
  23.3 2.2 %collective-permute-done.1.refs_2_ = bf16[256,1536]{1,0:T(8,128)(2,1)} collective-permute-done((bf16[256,1536]{1,0:T(8,128)(2,1)}, bf16[256,1536]{1,0:T(8,128)(2,1)}, u32[]{:S(2)}, u32[]{:S(2)}) %collective-permute-start.1) | collective-permute-done | bytes 786464 | tf_op jit(solution)/shard_map/ppermute | solution.py:261
  25.6 1.5 %collective-permute-start.12 = (bf16[256,1536]{1,0:T(8,128)(2,1)}, bf16[256,1536]{1,0:T(8,128)(2,1)S(1)}, u32[]{:S(2)}, u32[]{:S(2)}) collective-permute-start(bf16[256,1536]{1,0:T(8,128)(2,1)} %copy-done), channel_id=1, source_target_pairs={{0,20},{4,8},{8,28},{12,0},{16,4},{20,24},{24,12},{28,16},{1,21},{... | collective-permute-start | bytes 2359304 | tf_op jit(solution)/shard_map/ppermute | solution.py:261
  27.0 1.5 %fusion.44 = f32[256,256]{1,0:T(8,128)S(1)} fusion(bf16[256,1536]{1,0:T(8,128)(2,1)S(1)} %get-tuple-element.50, bf16[256,1536]{1,0:T(8,128)(2,1)} %collective-permute-done.1.refs_2_), kind=kOutput, calls=%fused_computation.79 | convolution fusion | flops 201326592 | bytes 1835008 | tf_op jit(solution)/shard_map/ap,bp->ab/dot_general | solution.py:118
  28.6 1.3 %collective-permute-start.6 = (bf16[1,64,256]{2,1,0:T(8,128)(2,1)S(1)}, bf16[1,64,256]{2,1,0:T(8,128)(2,1)S(1)}, u32[]{:S(2)}, u32[]{:S(2)}) collective-permute-start(bf16[1,64,256]{2,1,0:T(8,128)(2,1)S(1)} %get-tuple-element.60), channel_id=1, source_target_pairs={{0,1},{1,2},{2,3},{3,0},{4,5},{5,6},{6,7},{7,4},{8,9},{9,10},{10,1... | collective-permute-start | bytes 98312 | tf_op jit(solution)/shard_map/ppermute | solution.py:258
  30.0 2.1 %collective-permute-start.8 = (bf16[1,64,256]{2,1,0:T(8,128)(2,1)S(1)}, bf16[1,64,256]{2,1,0:T(8,128)(2,1)S(1)}, u32[]{:S(2)}, u32[]{:S(2)}) collective-permute-start(bf16[1,64,256]{2,1,0:T(8,128)(2,1)S(1)} %get-tuple-element.61), channel_id=1, source_target_pairs={{0,3},{1,0},{2,1},{3,2},{4,7},{5,4},{6,5},{7,6},{8,11},{9,8},{10,9... | collective-permute-start | bytes 98312 | tf_op jit(solution)/shard_map/ppermute | solution.py:258
  32.0 0.4 collective-permute-start.7
  32.4 0.8 collective-permute-done.6
  33.3 0.0 collective-permute-done.8
  33.3 2.4 %collective-permute-done.7 = bf16[1,64,256]{2,1,0:T(8,128)(2,1)S(1)} collective-permute-done((bf16[1,64,256]{2,1,0:T(8,128)(2,1)S(1)}, bf16[1,64,256]{2,1,0:T(8,128)(2,1)S(1)}, u32[]{:S(2)}, u32[]{:S(2)}) %collective-permute-start.7) | collective-permute-done | bytes 32800 | tf_op jit(solution)/shard_map/ppermute | solution.py:258
  35.7 2.0 %collective-permute-start.11 = (bf16[2,64,256]{2,1,0:T(8,128)(2,1)S(1)}, bf16[2,64,256]{2,1,0:T(8,128)(2,1)S(1)}, u32[]{:S(2)}, u32[]{:S(2)}) collective-permute-start(bf16[2,64,256]{2,1,0:T(8,128)(2,1)S(1)} %fusion.33.refs_8_), channel_id=1, source_target_pairs={{0,3},{1,0},{2,1},{3,2},{4,7},{5,4},{6,5},{7,6},{8,11},{9,8},{10,9... | collective-permute-start | bytes 196616 | tf_op jit(solution)/shard_map/ppermute | solution.py:258
  37.8 0.0 collective-permute-start.10
  37.8 0.4 collective-permute-start.9
  38.1 1.7 %collective-permute-done.2.refs_3_ = bf16[256,1536]{1,0:T(8,128)(2,1)} collective-permute-done((bf16[256,1536]{1,0:T(8,128)(2,1)S(1)}, bf16[256,1536]{1,0:T(8,128)(2,1)}, u32[]{:S(2)}, u32[]{:S(2)}) %collective-permute-start.2) | collective-permute-done | bytes 786464 | tf_op jit(solution)/shard_map/ppermute | solution.py:261
  39.9 2.1 %collective-permute-start.13 = (bf16[1,64,256]{2,1,0:T(8,128)(2,1)S(1)}, bf16[1,64,256]{2,1,0:T(8,128)(2,1)S(1)}, u32[]{:S(2)}, u32[]{:S(2)}) collective-permute-start(bf16[1,64,256]{2,1,0:T(8,128)(2,1)S(1)} %fusion.40), channel_id=1, source_target_pairs={{0,28},{4,24},{8,20},{12,16},{16,8},{20,12},{24,0},{28,4},{1,29},{... | collective-permute-start | bytes 98312 | tf_op jit(solution)/shard_map/ppermute | solution.py:261
  42.0 1.9 %collective-permute-done.13 = bf16[1,64,256]{2,1,0:T(8,128)(2,1)S(1)} collective-permute-done((bf16[1,64,256]{2,1,0:T(8,128)(2,1)S(1)}, bf16[1,64,256]{2,1,0:T(8,128)(2,1)S(1)}, u32[]{:S(2)}, u32[]{:S(2)}) %collective-permute-start.13) | collective-permute-done | bytes 32800 | tf_op jit(solution)/shard_map/ppermute | solution.py:261
  43.8 1.3 %collective-permute-start.14 = (bf16[256,1536]{1,0:T(8,128)(2,1)S(1)}, bf16[256,1536]{1,0:T(8,128)(2,1)S(1)}, u32[]{:S(2)}, u32[]{:S(2)}) collective-permute-start(bf16[256,1536]{1,0:T(8,128)(2,1)S(1)} %get-tuple-element.46), channel_id=1, source_target_pairs={{0,8},{4,20},{8,24},{12,4},{16,0},{20,28},{24,16},{28,12},{1,9},{5... | collective-permute-start | bytes 2359304 | tf_op jit(solution)/shard_map/ppermute | solution.py:261
  45.1 0.0 collective-permute-done.9.refs_9_
  45.2 1.6 %convolution_bitcast_fusion.3 = f32[1,256,256]{2,1,0:T(8,128)S(1)} fusion(bf16[256,1536]{1,0:T(8,128)(2,1)S(1)} %copy-done.1, bf16[256,1536]{1,0:T(8,128)(2,1)} %collective-permute-done.2.refs_3_), kind=kOutput, calls=%fused_computation.3 | convolution fusion | flops 201326592 | bytes 1835008 | tf_op jit(solution)/shard_map/ap,bp->ab/dot_general | solution.py:118
  46.8 0.2 collective-permute-start.20
  47.0 0.4 convolution_bitcast_fusion.2
  47.5 1.8 %collective-permute-start.15 = (bf16[2,64,256]{2,1,0:T(8,128)(2,1)S(1)}, bf16[2,64,256]{2,1,0:T(8,128)(2,1)S(1)}, u32[]{:S(2)}, u32[]{:S(2)}) collective-permute-start(bf16[2,64,256]{2,1,0:T(8,128)(2,1)S(1)} %get-tuple-element.54), channel_id=1, source_target_pairs={{0,1},{1,2},{2,3},{3,0},{4,5},{5,6},{6,7},{7,4},{8,9},{9,10},{10,1... | collective-permute-start | bytes 196616 | tf_op jit(solution)/shard_map/ppermute | solution.py:258
  49.3 2.2 %collective-permute-start.16 = (bf16[2,64,256]{2,1,0:T(8,128)(2,1)S(1)}, bf16[2,64,256]{2,1,0:T(8,128)(2,1)S(1)}, u32[]{:S(2)}, u32[]{:S(2)}) collective-permute-start(bf16[2,64,256]{2,1,0:T(8,128)(2,1)S(1)} %get-tuple-element.55), channel_id=1, source_target_pairs={{0,2},{1,3},{2,0},{3,1},{4,6},{5,7},{6,4},{7,5},{8,10},{9,11},{10,... | collective-permute-start | bytes 196616 | tf_op jit(solution)/shard_map/ppermute | solution.py:258
  51.5 0.9 collective-permute-start.17
  52.4 0.4 collective-permute-done.15
  52.8 1.5 %collective-permute-done.16 = bf16[2,64,256]{2,1,0:T(8,128)(2,1)S(1)} collective-permute-done((bf16[2,64,256]{2,1,0:T(8,128)(2,1)S(1)}, bf16[2,64,256]{2,1,0:T(8,128)(2,1)S(1)}, u32[]{:S(2)}, u32[]{:S(2)}) %collective-permute-start.16) | collective-permute-done | bytes 65568 | tf_op jit(solution)/shard_map/ppermute | solution.py:258
  54.3 0.6 collective-permute-done.17
  55.0 0.7 collective-permute-start.19
  55.7 2.7 %collective-permute-start.18 = (bf16[4,64,256]{2,1,0:T(8,128)(2,1)S(1)}, bf16[4,64,256]{2,1,0:T(8,128)(2,1)S(1)}, u32[]{:S(2)}, u32[]{:S(2)}) collective-permute-start(bf16[4,64,256]{2,1,0:T(8,128)(2,1)S(1)} %pad_maximum_fusion.refs_12_), channel_id=1, source_target_pairs={{0,1},{1,2},{2,3},{3,0},{4,5},{5,6},{6,7},{7,4},{8,9},{9,10},{10,1... | collective-permute-start | bytes 393224 | tf_op jit(solution)/shard_map/ppermute | solution.py:258
  58.5 0.0 collective-permute-done.14.refs_5_
  58.5 7.8 %collective-permute-done.19.refs_14_ = bf16[4,64,256]{2,1,0:T(8,128)(2,1)S(1)} collective-permute-done((bf16[4,64,256]{2,1,0:T(8,128)(2,1)S(1)}, bf16[4,64,256]{2,1,0:T(8,128)(2,1)S(1)}, u32[]{:S(2)}, u32[]{:S(2)}) %collective-permute-start.19) | collective-permute-done | bytes 131104 | tf_op jit(solution)/shard_map/ppermute | solution.py:258
  66.2 4.3 %collective-permute-start.21 = (bf16[256,1536]{1,0:T(8,128)(2,1)S(1)}, bf16[256,1536]{1,0:T(8,128)(2,1)S(1)}, u32[]{:S(2)}, u32[]{:S(2)}) collective-permute-start(bf16[256,1536]{1,0:T(8,128)(2,1)S(1)} %get-tuple-element.50), channel_id=1, source_target_pairs={{0,28},{4,24},{8,20},{12,16},{16,8},{20,12},{24,0},{28,4},{1,29},{... | collective-permute-start | bytes 2359304 | tf_op jit(solution)/shard_map/ppermute | solution.py:261
  70.5 0.4 convolution_bitcast_fusion.1
  71.0 0.4 convolution_bitcast_fusion
  71.4 0.1 collective-permute-start.23
  71.5 0.7 collective-permute-start.24
  72.2 2.5 %collective-permute-start.25 = (bf16[2,64,256]{2,1,0:T(8,128)(2,1)S(1)}, bf16[2,64,256]{2,1,0:T(8,128)(2,1)S(1)}, u32[]{:S(2)}, u32[]{:S(2)}) collective-permute-start(bf16[2,64,256]{2,1,0:T(8,128)(2,1)S(1)} %get-tuple-element.53), channel_id=1, source_target_pairs={{0,3},{1,0},{2,1},{3,2},{4,7},{5,4},{6,5},{7,6},{8,11},{9,8},{10,9... | collective-permute-start | bytes 196616 | tf_op jit(solution)/shard_map/ppermute | solution.py:258
  74.7 0.4 collective-permute-start.22
  75.1 2.0 %collective-permute-done.23 = bf16[2,64,256]{2,1,0:T(8,128)(2,1)S(1)} collective-permute-done((bf16[2,64,256]{2,1,0:T(8,128)(2,1)S(1)}, bf16[2,64,256]{2,1,0:T(8,128)(2,1)S(1)}, u32[]{:S(2)}, u32[]{:S(2)}) %collective-permute-start.23) | collective-permute-done | bytes 65568 | tf_op jit(solution)/shard_map/ppermute | solution.py:258
  77.1 0.9 collective-permute-done.24
  78.0 0.1 collective-permute-done.25
  78.1 5.7 %collective-permute-start.28 = (bf16[2,64,256]{2,1,0:T(8,128)(2,1)S(1)}, bf16[2,64,256]{2,1,0:T(8,128)(2,1)S(1)}, u32[]{:S(2)}, u32[]{:S(2)}) collective-permute-start(bf16[2,64,256]{2,1,0:T(8,128)(2,1)S(1)} %fusion.35.refs_16_), channel_id=1, source_target_pairs={{0,3},{1,0},{2,1},{3,2},{4,7},{5,4},{6,5},{7,6},{8,11},{9,8},{10,9... | collective-permute-start | bytes 196616 | tf_op jit(solution)/shard_map/ppermute | solution.py:258
  83.8 0.4 collective-permute-start.26
  84.1 1.0 collective-permute-done.28.refs_19_
  85.1 2.7 %collective-permute-done.27.refs_18_ = bf16[2,64,256]{2,1,0:T(8,128)(2,1)S(1)} collective-permute-done((bf16[2,64,256]{2,1,0:T(8,128)(2,1)S(1)}, bf16[2,64,256]{2,1,0:T(8,128)(2,1)S(1)}, u32[]{:S(2)}, u32[]{:S(2)}) %collective-permute-start.27) | collective-permute-done | bytes 65568 | tf_op jit(solution)/shard_map/ppermute | solution.py:258
  87.8 0.9 collective-permute-done.26.refs_17_
  88.8 0.5 copy-done.21
  89.3 0.9 copy-done.7
  90.2 7.1 %accumulate.1 = bf16[4,256,1536]{2,1,0:T(8,128)(2,1)} custom-call(s32[26]{0:T(128)} %get-tuple-element.28.plan.refs_0_, bf16[4,256,1536]{2,1,0:T(8,128)(2,1)} %refs_0_.3, bf16[256,1536]{1,0:T(8,128)(2,1)} %copy-done.2, bf16[256,1536]{1,0:T(8,128)(2,1)} %collective-permute-done.1.refs_2_, bf16[256,1536]{1,0:T(8,128)(2,1)} %collective-permute-done.2.refs_3_, ...), custom_call_target="tpu_custom_call" | custom-call | flops 1 | bytes 1 | tf_op jit(solution)/shard_map/accumulate/pallas_call | solution.py:217
  (60 shorter events, 0.3 us)
Async XLA Ops:
  3.7 4.1 %collective-permute-start = (bf16[256,1536]{1,0:T(8,128)(2,1)S(1)}, bf16[256,1536]{1,0:T(8,128)(2,1)S(1)}, u32[]{:S(2)}, u32[]{:S(2)}) collective-permute-start(bf16[256,1536]{1,0:T(8,128)(2,1)S(1)} %get-tuple-element.29), channel_id=1, source_target_pairs={{0,4},{4,0},{8,12},{12,8},{16,20},{20,16},{24,28},{28,24},{1,5},{5... | collective-permute-start | bytes 2359304 | tf_op jit(solution)/shard_map/ppermute | solution.py:261
  3.8 21.8 %collective-permute-start.1 = (bf16[256,1536]{1,0:T(8,128)(2,1)}, bf16[256,1536]{1,0:T(8,128)(2,1)}, u32[]{:S(2)}, u32[]{:S(2)}) collective-permute-start(bf16[256,1536]{1,0:T(8,128)(2,1)} %get-tuple-element.30), channel_id=1, source_target_pairs={{0,24},{4,28},{8,16},{12,20},{16,12},{20,8},{24,4},{28,0},{1,25},{... | collective-permute-start | bytes 2359304 | tf_op jit(solution)/shard_map/ppermute | solution.py:261
  7.8 7.6 %copy-start.2 = (bf16[256,1536]{1,0:T(8,128)(2,1)}, bf16[256,1536]{1,0:T(8,128)(2,1)S(1)}, u32[]{:S(2)}) copy-start(bf16[256,1536]{1,0:T(8,128)(2,1)S(1)} %collective-permute-done.refs_1_) | copy-start | bytes 2359300
  8.2 7.2 %copy-start.6 = (f32[1,256,256]{2,1,0:T(8,128)}, f32[1,256,256]{2,1,0:T(8,128)S(1)}, u32[]{:S(2)}) copy-start(f32[1,256,256]{2,1,0:T(8,128)S(1)} %convolution_bitcast_fusion.4) | copy-start | bytes 786436
  9.0 12.2 %collective-permute-start.3 = (f32[2,64,256]{2,1,0:T(8,128)}, f32[2,64,256]{2,1,0:T(8,128)}, u32[]{:S(2)}, u32[]{:S(2)}) collective-permute-start(f32[2,64,256]{2,1,0:T(8,128)} %get-tuple-element.57), channel_id=1, source_target_pairs={{0,1},{1,2},{2,3},{3,0},{4,5},{5,6},{6,7},{7,4},{8,9},{9,10},{10,1... | collective-permute-start | bytes 393224 | tf_op jit(solution)/shard_map/ppermute | solution.py:258
  10.3 11.9 %collective-permute-start.4 = (f32[2,64,256]{2,1,0:T(8,128)}, f32[2,64,256]{2,1,0:T(8,128)}, u32[]{:S(2)}, u32[]{:S(2)}) collective-permute-start(f32[2,64,256]{2,1,0:T(8,128)} %get-tuple-element.58), channel_id=1, source_target_pairs={{0,2},{1,3},{2,0},{3,1},{4,6},{5,7},{6,4},{7,5},{8,10},{9,11},{10,... | collective-permute-start | bytes 393224 | tf_op jit(solution)/shard_map/ppermute | solution.py:258
  12.6 9.6 %collective-permute-start.5 = (f32[2,64,256]{2,1,0:T(8,128)S(1)}, f32[2,64,256]{2,1,0:T(8,128)}, u32[]{:S(2)}, u32[]{:S(2)}) collective-permute-start(f32[2,64,256]{2,1,0:T(8,128)S(1)} %get-tuple-element.59), channel_id=1, source_target_pairs={{0,3},{1,0},{2,1},{3,2},{4,7},{5,4},{6,5},{7,6},{8,11},{9,8},{10,9... | collective-permute-start | bytes 393224 | tf_op jit(solution)/shard_map/ppermute | solution.py:258
  13.7 26.2 %collective-permute-start.2 = (bf16[256,1536]{1,0:T(8,128)(2,1)S(1)}, bf16[256,1536]{1,0:T(8,128)(2,1)}, u32[]{:S(2)}, u32[]{:S(2)}) collective-permute-start(bf16[256,1536]{1,0:T(8,128)(2,1)S(1)} %get-tuple-element.31), channel_id=1, source_target_pairs={{0,12},{4,16},{8,4},{12,24},{16,28},{20,0},{24,20},{28,8},{1,13},{... | collective-permute-start | bytes 2359304 | tf_op jit(solution)/shard_map/ppermute | solution.py:261
  17.9 0.9 copy-start
  21.2 14.5 %copy-start.22 = (f32[1,64,256]{2,1,0:T(8,128)S(1)}, f32[1,64,256]{2,1,0:T(8,128)}, u32[]{:S(2)}) copy-start(f32[1,64,256]{2,1,0:T(8,128)} %get-tuple-element.35) | copy-start | bytes 196612
  21.2 24.0 %copy-start.1 = (bf16[256,1536]{1,0:T(8,128)(2,1)S(1)}, bf16[256,1536]{1,0:T(8,128)(2,1)}, u32[]{:S(2)}) copy-start(bf16[256,1536]{1,0:T(8,128)(2,1)} %copy-done) | copy-start | bytes 2359300
  23.3 24.1 %copy-start.9 = (bf16[2,64,256]{2,1,0:T(8,128)(2,1)}, bf16[2,64,256]{2,1,0:T(8,128)(2,1)S(1)}, u32[]{:S(2)}) copy-start(bf16[2,64,256]{2,1,0:T(8,128)(2,1)S(1)} %fusion.33.refs_8_) | copy-start | bytes 196612
  25.6 29.4 %copy-start.15 = (f32[2,64,256]{2,1,0:T(8,128)S(1)}, f32[2,64,256]{2,1,0:T(8,128)}, u32[]{:S(2)}) copy-start(f32[2,64,256]{2,1,0:T(8,128)} %get-tuple-element.36) | copy-start | bytes 393220
  25.6 21.2 %collective-permute-start.12 = (bf16[256,1536]{1,0:T(8,128)(2,1)}, bf16[256,1536]{1,0:T(8,128)(2,1)S(1)}, u32[]{:S(2)}, u32[]{:S(2)}) collective-permute-start(bf16[256,1536]{1,0:T(8,128)(2,1)} %copy-done), channel_id=1, source_target_pairs={{0,20},{4,8},{8,28},{12,0},{16,4},{20,24},{24,12},{28,16},{1,21},{... | collective-permute-start | bytes 2359304 | tf_op jit(solution)/shard_map/ppermute | solution.py:261
  28.6 4.7 %collective-permute-start.6 = (bf16[1,64,256]{2,1,0:T(8,128)(2,1)S(1)}, bf16[1,64,256]{2,1,0:T(8,128)(2,1)S(1)}, u32[]{:S(2)}, u32[]{:S(2)}) collective-permute-start(bf16[1,64,256]{2,1,0:T(8,128)(2,1)S(1)} %get-tuple-element.60), channel_id=1, source_target_pairs={{0,1},{1,2},{2,3},{3,0},{4,5},{5,6},{6,7},{7,4},{8,9},{9,10},{10,1... | collective-permute-start | bytes 98312 | tf_op jit(solution)/shard_map/ppermute | solution.py:258
  30.0 3.3 %collective-permute-start.8 = (bf16[1,64,256]{2,1,0:T(8,128)(2,1)S(1)}, bf16[1,64,256]{2,1,0:T(8,128)(2,1)S(1)}, u32[]{:S(2)}, u32[]{:S(2)}) collective-permute-start(bf16[1,64,256]{2,1,0:T(8,128)(2,1)S(1)} %get-tuple-element.61), channel_id=1, source_target_pairs={{0,3},{1,0},{2,1},{3,2},{4,7},{5,4},{6,5},{7,6},{8,11},{9,8},{10,9... | collective-permute-start | bytes 98312 | tf_op jit(solution)/shard_map/ppermute | solution.py:258
  32.0 3.7 %collective-permute-start.7 = (bf16[1,64,256]{2,1,0:T(8,128)(2,1)S(1)}, bf16[1,64,256]{2,1,0:T(8,128)(2,1)S(1)}, u32[]{:S(2)}, u32[]{:S(2)}) collective-permute-start(bf16[1,64,256]{2,1,0:T(8,128)(2,1)S(1)} %get-tuple-element.62), channel_id=1, source_target_pairs={{0,2},{1,3},{2,0},{3,1},{4,6},{5,7},{6,4},{7,5},{8,10},{9,11},{10,... | collective-permute-start | bytes 98312 | tf_op jit(solution)/shard_map/ppermute | solution.py:258
  35.7 9.4 %collective-permute-start.11 = (bf16[2,64,256]{2,1,0:T(8,128)(2,1)S(1)}, bf16[2,64,256]{2,1,0:T(8,128)(2,1)S(1)}, u32[]{:S(2)}, u32[]{:S(2)}) collective-permute-start(bf16[2,64,256]{2,1,0:T(8,128)(2,1)S(1)} %fusion.33.refs_8_), channel_id=1, source_target_pairs={{0,3},{1,0},{2,1},{3,2},{4,7},{5,4},{6,5},{7,6},{8,11},{9,8},{10,9... | collective-permute-start | bytes 196616 | tf_op jit(solution)/shard_map/ppermute | solution.py:258
  37.8 7.4 %collective-permute-start.10 = (bf16[2,64,256]{2,1,0:T(8,128)(2,1)S(1)}, bf16[2,64,256]{2,1,0:T(8,128)(2,1)S(1)}, u32[]{:S(2)}, u32[]{:S(2)}) collective-permute-start(bf16[2,64,256]{2,1,0:T(8,128)(2,1)S(1)} %fusion.33.refs_8_), channel_id=1, source_target_pairs={{0,2},{1,3},{2,0},{3,1},{4,6},{5,7},{6,4},{7,5},{8,10},{9,11},{10,... | collective-permute-start | bytes 196616 | tf_op jit(solution)/shard_map/ppermute | solution.py:258
  37.8 7.4 %collective-permute-start.9 = (bf16[2,64,256]{2,1,0:T(8,128)(2,1)S(1)}, bf16[2,64,256]{2,1,0:T(8,128)(2,1)S(1)}, u32[]{:S(2)}, u32[]{:S(2)}) collective-permute-start(bf16[2,64,256]{2,1,0:T(8,128)(2,1)S(1)} %fusion.33.refs_8_), channel_id=1, source_target_pairs={{0,1},{1,2},{2,3},{3,0},{4,5},{5,6},{6,7},{7,4},{8,9},{9,10},{10,1... | collective-permute-start | bytes 196616 | tf_op jit(solution)/shard_map/ppermute | solution.py:258
  39.9 4.0 %collective-permute-start.13 = (bf16[1,64,256]{2,1,0:T(8,128)(2,1)S(1)}, bf16[1,64,256]{2,1,0:T(8,128)(2,1)S(1)}, u32[]{:S(2)}, u32[]{:S(2)}) collective-permute-start(bf16[1,64,256]{2,1,0:T(8,128)(2,1)S(1)} %fusion.40), channel_id=1, source_target_pairs={{0,28},{4,24},{8,20},{12,16},{16,8},{20,12},{24,0},{28,4},{1,29},{... | collective-permute-start | bytes 98312 | tf_op jit(solution)/shard_map/ppermute | solution.py:261
  43.8 14.6 %collective-permute-start.14 = (bf16[256,1536]{1,0:T(8,128)(2,1)S(1)}, bf16[256,1536]{1,0:T(8,128)(2,1)S(1)}, u32[]{:S(2)}, u32[]{:S(2)}) collective-permute-start(bf16[256,1536]{1,0:T(8,128)(2,1)S(1)} %get-tuple-element.46), channel_id=1, source_target_pairs={{0,8},{4,20},{8,24},{12,4},{16,0},{20,28},{24,16},{28,12},{1,9},{5... | collective-permute-start | bytes 2359304 | tf_op jit(solution)/shard_map/ppermute | solution.py:261
  45.1 25.8 %copy-start.16 = (bf16[2,64,256]{2,1,0:T(8,128)(2,1)}, bf16[2,64,256]{2,1,0:T(8,128)(2,1)S(1)}, u32[]{:S(2)}) copy-start(bf16[2,64,256]{2,1,0:T(8,128)(2,1)S(1)} %collective-permute-done.11.refs_11_) | copy-start | bytes 196612
  45.1 25.8 %copy-start.17 = (bf16[2,64,256]{2,1,0:T(8,128)(2,1)}, bf16[2,64,256]{2,1,0:T(8,128)(2,1)S(1)}, u32[]{:S(2)}) copy-start(bf16[2,64,256]{2,1,0:T(8,128)(2,1)S(1)} %collective-permute-done.10.refs_10_) | copy-start | bytes 196612
  45.2 25.8 %copy-start.18 = (bf16[2,64,256]{2,1,0:T(8,128)(2,1)}, bf16[2,64,256]{2,1,0:T(8,128)(2,1)S(1)}, u32[]{:S(2)}) copy-start(bf16[2,64,256]{2,1,0:T(8,128)(2,1)S(1)} %collective-permute-done.9.refs_9_) | copy-start | bytes 196612
  46.8 24.6 %copy-start.3 = (bf16[256,1536]{1,0:T(8,128)(2,1)}, bf16[256,1536]{1,0:T(8,128)(2,1)S(1)}, u32[]{:S(2)}) copy-start(bf16[256,1536]{1,0:T(8,128)(2,1)S(1)} %collective-permute-done.12.refs_4_) | copy-start | bytes 2359300
  46.8 19.5 %collective-permute-start.20 = (bf16[256,1536]{1,0:T(8,128)(2,1)S(1)}, bf16[256,1536]{1,0:T(8,128)(2,1)S(1)}, u32[]{:S(2)}, u32[]{:S(2)}) collective-permute-start(bf16[256,1536]{1,0:T(8,128)(2,1)S(1)} %get-tuple-element.48), channel_id=1, source_target_pairs={{0,16},{4,12},{8,0},{12,28},{16,24},{20,4},{24,8},{28,20},{1,17},{... | collective-permute-start | bytes 2359304 | tf_op jit(solution)/shard_map/ppermute | solution.py:261
  47.4 30.6 %copy-start.14 = (f32[2,64,256]{2,1,0:T(8,128)S(1)}, f32[2,64,256]{2,1,0:T(8,128)}, u32[]{:S(2)}) copy-start(f32[2,64,256]{2,1,0:T(8,128)} %get-tuple-element.37) | copy-start | bytes 393220
  47.5 5.4 %collective-permute-start.15 = (bf16[2,64,256]{2,1,0:T(8,128)(2,1)S(1)}, bf16[2,64,256]{2,1,0:T(8,128)(2,1)S(1)}, u32[]{:S(2)}, u32[]{:S(2)}) collective-permute-start(bf16[2,64,256]{2,1,0:T(8,128)(2,1)S(1)} %get-tuple-element.54), channel_id=1, source_target_pairs={{0,1},{1,2},{2,3},{3,0},{4,5},{5,6},{6,7},{7,4},{8,9},{9,10},{10,1... | collective-permute-start | bytes 196616 | tf_op jit(solution)/shard_map/ppermute | solution.py:258
  49.3 5.1 %collective-permute-start.16 = (bf16[2,64,256]{2,1,0:T(8,128)(2,1)S(1)}, bf16[2,64,256]{2,1,0:T(8,128)(2,1)S(1)}, u32[]{:S(2)}, u32[]{:S(2)}) collective-permute-start(bf16[2,64,256]{2,1,0:T(8,128)(2,1)S(1)} %get-tuple-element.55), channel_id=1, source_target_pairs={{0,2},{1,3},{2,0},{3,1},{4,6},{5,7},{6,4},{7,5},{8,10},{9,11},{10,... | collective-permute-start | bytes 196616 | tf_op jit(solution)/shard_map/ppermute | solution.py:258
  51.5 3.5 %collective-permute-start.17 = (bf16[2,64,256]{2,1,0:T(8,128)(2,1)S(1)}, bf16[2,64,256]{2,1,0:T(8,128)(2,1)S(1)}, u32[]{:S(2)}, u32[]{:S(2)}) collective-permute-start(bf16[2,64,256]{2,1,0:T(8,128)(2,1)S(1)} %get-tuple-element.56), channel_id=1, source_target_pairs={{0,3},{1,0},{2,1},{3,2},{4,7},{5,4},{6,5},{7,6},{8,11},{9,8},{10,9... | collective-permute-start | bytes 196616 | tf_op jit(solution)/shard_map/ppermute | solution.py:258
  55.0 33.7 %copy-start.8 = (bf16[4,64,256]{2,1,0:T(8,128)(2,1)}, bf16[4,64,256]{2,1,0:T(8,128)(2,1)S(1)}, u32[]{:S(2)}) copy-start(bf16[4,64,256]{2,1,0:T(8,128)(2,1)S(1)} %pad_maximum_fusion.refs_12_) | copy-start | bytes 393220
  55.0 11.2 %collective-permute-start.19 = (bf16[4,64,256]{2,1,0:T(8,128)(2,1)S(1)}, bf16[4,64,256]{2,1,0:T(8,128)(2,1)S(1)}, u32[]{:S(2)}, u32[]{:S(2)}) collective-permute-start(bf16[4,64,256]{2,1,0:T(8,128)(2,1)S(1)} %pad_maximum_fusion.refs_12_), channel_id=1, source_target_pairs={{0,2},{1,3},{2,0},{3,1},{4,6},{5,7},{6,4},{7,5},{8,10},{9,11},{10,... | collective-permute-start | bytes 393224 | tf_op jit(solution)/shard_map/ppermute | solution.py:258
  55.7 10.5 %collective-permute-start.18 = (bf16[4,64,256]{2,1,0:T(8,128)(2,1)S(1)}, bf16[4,64,256]{2,1,0:T(8,128)(2,1)S(1)}, u32[]{:S(2)}, u32[]{:S(2)}) collective-permute-start(bf16[4,64,256]{2,1,0:T(8,128)(2,1)S(1)} %pad_maximum_fusion.refs_12_), channel_id=1, source_target_pairs={{0,1},{1,2},{2,3},{3,0},{4,5},{5,6},{6,7},{7,4},{8,9},{9,10},{10,1... | collective-permute-start | bytes 393224 | tf_op jit(solution)/shard_map/ppermute | solution.py:258
  58.5 30.2 %copy-start.4 = (bf16[256,1536]{1,0:T(8,128)(2,1)}, bf16[256,1536]{1,0:T(8,128)(2,1)S(1)}, u32[]{:S(2)}) copy-start(bf16[256,1536]{1,0:T(8,128)(2,1)S(1)} %collective-permute-done.14.refs_5_) | copy-start | bytes 2359300
  66.2 22.5 %copy-start.11 = (bf16[4,64,256]{2,1,0:T(8,128)(2,1)}, bf16[4,64,256]{2,1,0:T(8,128)(2,1)S(1)}, u32[]{:S(2)}) copy-start(bf16[4,64,256]{2,1,0:T(8,128)(2,1)S(1)} %collective-permute-done.19.refs_14_) | copy-start | bytes 393220
  66.2 22.5 %copy-start.12 = (bf16[4,64,256]{2,1,0:T(8,128)(2,1)}, bf16[4,64,256]{2,1,0:T(8,128)(2,1)S(1)}, u32[]{:S(2)}) copy-start(bf16[4,64,256]{2,1,0:T(8,128)(2,1)S(1)} %collective-permute-done.18.refs_13_) | copy-start | bytes 393220
  66.2 22.5 %copy-start.5 = (bf16[256,1536]{1,0:T(8,128)(2,1)}, bf16[256,1536]{1,0:T(8,128)(2,1)S(1)}, u32[]{:S(2)}) copy-start(bf16[256,1536]{1,0:T(8,128)(2,1)S(1)} %collective-permute-done.20.refs_6_) | copy-start | bytes 2359300
  66.2 22.5 %collective-permute-start.21 = (bf16[256,1536]{1,0:T(8,128)(2,1)S(1)}, bf16[256,1536]{1,0:T(8,128)(2,1)S(1)}, u32[]{:S(2)}, u32[]{:S(2)}) collective-permute-start(bf16[256,1536]{1,0:T(8,128)(2,1)S(1)} %get-tuple-element.50), channel_id=1, source_target_pairs={{0,28},{4,24},{8,20},{12,16},{16,8},{20,12},{24,0},{28,4},{1,29},{... | collective-permute-start | bytes 2359304 | tf_op jit(solution)/shard_map/ppermute | solution.py:261
  71.4 5.6 %collective-permute-start.23 = (bf16[2,64,256]{2,1,0:T(8,128)(2,1)S(1)}, bf16[2,64,256]{2,1,0:T(8,128)(2,1)S(1)}, u32[]{:S(2)}, u32[]{:S(2)}) collective-permute-start(bf16[2,64,256]{2,1,0:T(8,128)(2,1)S(1)} %get-tuple-element.51), channel_id=1, source_target_pairs={{0,1},{1,2},{2,3},{3,0},{4,5},{5,6},{6,7},{7,4},{8,9},{9,10},{10,1... | collective-permute-start | bytes 196616 | tf_op jit(solution)/shard_map/ppermute | solution.py:258
  71.5 6.5 %collective-permute-start.24 = (bf16[2,64,256]{2,1,0:T(8,128)(2,1)S(1)}, bf16[2,64,256]{2,1,0:T(8,128)(2,1)S(1)}, u32[]{:S(2)}, u32[]{:S(2)}) collective-permute-start(bf16[2,64,256]{2,1,0:T(8,128)(2,1)S(1)} %get-tuple-element.52), channel_id=1, source_target_pairs={{0,2},{1,3},{2,0},{3,1},{4,6},{5,7},{6,4},{7,5},{8,10},{9,11},{10,... | collective-permute-start | bytes 196616 | tf_op jit(solution)/shard_map/ppermute | solution.py:258
  72.2 5.8 %collective-permute-start.25 = (bf16[2,64,256]{2,1,0:T(8,128)(2,1)S(1)}, bf16[2,64,256]{2,1,0:T(8,128)(2,1)S(1)}, u32[]{:S(2)}, u32[]{:S(2)}) collective-permute-start(bf16[2,64,256]{2,1,0:T(8,128)(2,1)S(1)} %get-tuple-element.53), channel_id=1, source_target_pairs={{0,3},{1,0},{2,1},{3,2},{4,7},{5,4},{6,5},{7,6},{8,11},{9,8},{10,9... | collective-permute-start | bytes 196616 | tf_op jit(solution)/shard_map/ppermute | solution.py:258
  74.7 9.4 %collective-permute-start.22 = (bf16[4,64,256]{2,1,0:T(8,128)(2,1)S(1)}, bf16[4,64,256]{2,1,0:T(8,128)(2,1)S(1)}, u32[]{:S(2)}, u32[]{:S(2)}) collective-permute-start(bf16[4,64,256]{2,1,0:T(8,128)(2,1)S(1)} %pad_maximum_fusion.refs_12_), channel_id=1, source_target_pairs={{0,3},{1,0},{2,1},{3,2},{4,7},{5,4},{6,5},{7,6},{8,11},{9,8},{10,9... | collective-permute-start | bytes 393224 | tf_op jit(solution)/shard_map/ppermute | solution.py:258
  78.1 10.7 %copy-start.10 = (bf16[2,64,256]{2,1,0:T(8,128)(2,1)}, bf16[2,64,256]{2,1,0:T(8,128)(2,1)S(1)}, u32[]{:S(2)}) copy-start(bf16[2,64,256]{2,1,0:T(8,128)(2,1)S(1)} %fusion.35.refs_16_) | copy-start | bytes 196612
  78.1 7.0 %collective-permute-start.28 = (bf16[2,64,256]{2,1,0:T(8,128)(2,1)S(1)}, bf16[2,64,256]{2,1,0:T(8,128)(2,1)S(1)}, u32[]{:S(2)}, u32[]{:S(2)}) collective-permute-start(bf16[2,64,256]{2,1,0:T(8,128)(2,1)S(1)} %fusion.35.refs_16_), channel_id=1, source_target_pairs={{0,3},{1,0},{2,1},{3,2},{4,7},{5,4},{6,5},{7,6},{8,11},{9,8},{10,9... | collective-permute-start | bytes 196616 | tf_op jit(solution)/shard_map/ppermute | solution.py:258
  83.8 4.0 %collective-permute-start.27 = (bf16[2,64,256]{2,1,0:T(8,128)(2,1)S(1)}, bf16[2,64,256]{2,1,0:T(8,128)(2,1)S(1)}, u32[]{:S(2)}, u32[]{:S(2)}) collective-permute-start(bf16[2,64,256]{2,1,0:T(8,128)(2,1)S(1)} %fusion.35.refs_16_), channel_id=1, source_target_pairs={{0,2},{1,3},{2,0},{3,1},{4,6},{5,7},{6,4},{7,5},{8,10},{9,11},{10,... | collective-permute-start | bytes 196616 | tf_op jit(solution)/shard_map/ppermute | solution.py:258
  83.8 4.9 %collective-permute-start.26 = (bf16[2,64,256]{2,1,0:T(8,128)(2,1)S(1)}, bf16[2,64,256]{2,1,0:T(8,128)(2,1)S(1)}, u32[]{:S(2)}, u32[]{:S(2)}) collective-permute-start(bf16[2,64,256]{2,1,0:T(8,128)(2,1)S(1)} %fusion.35.refs_16_), channel_id=1, source_target_pairs={{0,1},{1,2},{2,3},{3,0},{4,5},{5,6},{6,7},{7,4},{8,9},{9,10},{10,1... | collective-permute-start | bytes 196616 | tf_op jit(solution)/shard_map/ppermute | solution.py:258
  84.1 4.6 %copy-start.13 = (bf16[4,64,256]{2,1,0:T(8,128)(2,1)}, bf16[4,64,256]{2,1,0:T(8,128)(2,1)S(1)}, u32[]{:S(2)}) copy-start(bf16[4,64,256]{2,1,0:T(8,128)(2,1)S(1)} %collective-permute-done.22.refs_15_) | copy-start | bytes 393220
  85.1 3.7 %copy-start.19 = (bf16[2,64,256]{2,1,0:T(8,128)(2,1)}, bf16[2,64,256]{2,1,0:T(8,128)(2,1)S(1)}, u32[]{:S(2)}) copy-start(bf16[2,64,256]{2,1,0:T(8,128)(2,1)S(1)} %collective-permute-done.28.refs_19_) | copy-start | bytes 196612
  87.8 1.0 %copy-start.20 = (bf16[2,64,256]{2,1,0:T(8,128)(2,1)}, bf16[2,64,256]{2,1,0:T(8,128)(2,1)S(1)}, u32[]{:S(2)}) copy-start(bf16[2,64,256]{2,1,0:T(8,128)(2,1)S(1)} %collective-permute-done.27.refs_18_) | copy-start | bytes 196612
  88.7 0.6 copy-start.21
  89.3 0.9 copy-start.7
